TPU v7x, 32 devices: a whole 2x2x4 slice. The times are simulated.
32 devices in a mesh: seq: 2 (over y), fsdp: 16 (over z, x, core).
Axes of the slice: x: 2, y: 2, z: 4, core: 2. Of those that a mesh axis runs over, the one named last changes fastest.
Arguments:
- inputs: bfloat16 [16, 512, 1536], P('fsdp', 'seq'), may hold values from -6 to 6
- segment_ids: int32 [16, 512], P('fsdp'), may hold values from 0 to 3, never falling along the last dimension, each value on 1 to 256 neighbouring positions
- attn_gain: bfloat16 [1536], P(('seq', 'fsdp')), may hold values from 0.5 to 1.5
- q_weight: bfloat16 [1536, 1536], P(('seq', 'fsdp')), may hold values from -0.15625 to 0.15625
- k_weight: bfloat16 [1536, 256], P(('seq', 'fsdp')), may hold values from -0.15625 to 0.15625
- v_weight: bfloat16 [1536, 256], P(('seq', 'fsdp')), may hold values from -0.15625 to 0.15625
- qkv_bias: bfloat16 [2048], P(('seq', 'fsdp')), may hold values from -3 to 3
- o_weight: bfloat16 [1536, 1536], P(('seq', 'fsdp')), may hold values from -1.5 to 1.5
- mlp_gain: bfloat16 [1536], P(('seq', 'fsdp')), may hold values from 0.5 to 1.5
- gate_weight: bfloat16 [1536, 8960], P(('seq', 'fsdp')), may hold values from -0.15625 to 0.15625
- up_weight: bfloat16 [1536, 8960], P(('seq', 'fsdp')), may hold values from -0.15625 to 0.15625
- down_weight: bfloat16 [8960, 1536], P(('seq', 'fsdp')), may hold values from -0.0625 to 0.0625
- cotangent: bfloat16 [16, 512, 1536], P('fsdp', 'seq'), may hold values from -6 to 6
Outputs:
- output: bfloat16 [16, 512, 1536], P('fsdp', 'seq')
- input_grad: bfloat16 [16, 512, 1536], P('fsdp', 'seq')
- attn_gain_grad: float32 [1536], P(('seq', 'fsdp'))
- q_weight_grad: float32 [1536, 1536], P(('seq', 'fsdp'))
- k_weight_grad: float32 [1536, 256], P(('seq', 'fsdp'))
- v_weight_grad: float32 [1536, 256], P(('seq', 'fsdp'))
- qkv_bias_grad: float32 [2048], P(('seq', 'fsdp'))
- o_weight_grad: float32 [1536, 1536], P(('seq', 'fsdp'))
- mlp_gain_grad: float32 [1536], P(('seq', 'fsdp'))
- gate_weight_grad: float32 [1536, 8960], P(('seq', 'fsdp'))
- up_weight_grad: float32 [1536, 8960], P(('seq', 'fsdp'))
- down_weight_grad: float32 [8960, 1536], P(('seq', 'fsdp'))
Inputs may be any that keep to these rules, and one draw needn't show every extreme that they name: `segment_ids`: document numbers never fall along a sequence; each document has 1 to 256 positions and one has exactly 256.
All inputs are finite; a program needn't handle non-finite values.
Results may differ from a plain program's by a relative error of at most 0.013.
Values may be sent and summed in bfloat16 or wider, within the bound.
A program may use at most 512 MiB of HBM per device.

v0:
```python
import jax
import jax.numpy as jnp
from jax import lax
from jax.sharding import PartitionSpec as P

HD = 128


EPS = 1e-06
ROPE_BASE = 1000000.0
MASKED = -1e30


def tables(positions):
    freq = ROPE_BASE ** (-jnp.arange(0, HD, 2).astype(jnp.float32) / HD)
    angle = positions.astype(jnp.float32)[:, None] * freq[None, :]
    return (jnp.cos(angle), jnp.sin(angle))


def rotate(values, cosine, sine):
    count = values.shape[0]
    split = values.reshape(count, -1, HD)
    half = HD // 2
    first = split[..., :half]
    second = split[..., half:]
    cos_b = cosine[:, None, :]
    sin_b = sine[:, None, :]
    turned = jnp.concatenate(
        [first * cos_b - second * sin_b, second * cos_b + first * sin_b], axis=-1
    )
    return turned.reshape(count, -1)


def unrotate(values, cosine, sine):
    count = values.shape[0]
    split = values.reshape(count, -1, HD)
    half = HD // 2
    first = split[..., :half]
    second = split[..., half:]
    cos_b = cosine[:, None, :]
    sin_b = sine[:, None, :]
    turned = jnp.concatenate(
        [first * cos_b + second * sin_b, second * cos_b - first * sin_b], axis=-1
    )
    return turned.reshape(count, -1)


def norm_back(grad_normed, normed, rescale, gain_vec):
    grad_gain = jnp.sum(grad_normed * normed, axis=0)
    scaled = grad_normed * gain_vec
    grad_x = rescale * (scaled - normed * jnp.mean(scaled * normed, axis=-1, keepdims=True))
    return (grad_gain, grad_x)


def gather_attention(shards):
    return (
        lax.all_gather(shards[0], ("seq", "fsdp"), axis=0, tiled=True),
        lax.all_gather(shards[1], ("seq", "fsdp"), axis=0, tiled=True),
        lax.all_gather(shards[2], ("seq", "fsdp"), axis=0, tiled=True),
        lax.all_gather(shards[3], ("seq", "fsdp"), axis=0, tiled=True),
        lax.all_gather(shards[4], ("seq", "fsdp"), axis=0, tiled=True),
        lax.all_gather(shards[5], ("seq", "fsdp"), axis=0, tiled=True),
    )


def gather_mlp(shards):
    return (
        lax.all_gather(shards[0], ("seq", "fsdp"), axis=0, tiled=True),
        lax.all_gather(shards[1], ("seq", "fsdp"), axis=0, tiled=True),
        lax.all_gather(shards[2], ("seq", "fsdp"), axis=0, tiled=True),
        lax.all_gather(shards[3], ("seq", "fsdp"), axis=0, tiled=True),
    )


def outer_term(left, right):
    return jnp.einsum("tc,th->ch", left, right, preferred_element_type=jnp.float32)


def body(
    inputs,
    segment_ids,
    attn_gain,
    q_weight,
    k_weight,
    v_weight,
    qkv_bias,
    o_weight,
    mlp_gain,
    gate_weight,
    up_weight,
    down_weight,
    cotangent,
):
    tok_rows = inputs.shape[1]
    hidden_in = inputs[0].astype(jnp.float32)
    grad_out = cotangent[0]
    seg_all = segment_ids[0]
    length = seg_all.shape[0]
    seq_place = lax.axis_index("seq")
    tok_pos = seq_place * tok_rows + jnp.arange(tok_rows)
    cos_tok, sin_tok = tables(tok_pos)
    all_pos = jnp.arange(length)
    cos_all, sin_all = tables(all_pos)
    attn_shards = (attn_gain, q_weight, k_weight, v_weight, qkv_bias, o_weight)
    mlp_shards = (mlp_gain, gate_weight, up_weight, down_weight)
    gain_one, full_query, full_key, full_value, full_bias, full_out = gather_attention(attn_shards)
    query_width = full_query.shape[1]
    key_width = full_key.shape[1]
    bias_float = full_bias.astype(jnp.float32)
    query_bias = bias_float[:query_width]
    key_bias = bias_float[query_width : query_width + key_width]
    value_bias = bias_float[query_width + key_width :]
    rescale_one = lax.rsqrt(jnp.mean(hidden_in * hidden_in, axis=-1, keepdims=True) + EPS)
    normed_one = hidden_in * rescale_one
    input_one = (normed_one * gain_one.astype(jnp.float32)).astype(jnp.bfloat16)
    query_pre = jnp.dot(input_one, full_query, preferred_element_type=jnp.float32) + query_bias
    key_pre = jnp.dot(input_one, full_key, preferred_element_type=jnp.float32) + key_bias
    value_pre = jnp.dot(input_one, full_value, preferred_element_type=jnp.float32) + value_bias
    query_tok = rotate(query_pre, cos_tok, sin_tok).astype(jnp.bfloat16)
    key_tok = rotate(key_pre, cos_tok, sin_tok).astype(jnp.bfloat16)
    value_tok = value_pre.astype(jnp.bfloat16)
    query_recv, key_recv, value_recv = (
        lax.all_to_all(query_tok, "seq", split_axis=1, concat_axis=0, tiled=True),
        lax.all_to_all(key_tok, "seq", split_axis=1, concat_axis=0, tiled=True),
        lax.all_to_all(value_tok, "seq", split_axis=1, concat_axis=0, tiled=True),
    )
    kv_local = key_recv.shape[1] // HD
    q_local = query_recv.shape[1] // HD
    group_size = q_local // kv_local
    block_count = length // length
    query_blocks = query_recv.reshape(block_count, length, kv_local, group_size, HD)
    key_heads = key_recv.reshape(length, kv_local, HD)
    value_heads = value_recv.reshape(length, kv_local, HD)
    block_starts = jnp.arange(block_count) * length
    score_scale = HD ** (-0.5)

    def scores_of(query_block, start):
        raw_scores = (
            jnp.einsum("qkgd,pkd->kgqp", query_block, key_heads, preferred_element_type=jnp.float32)
            * score_scale
        )
        query_pos = start + jnp.arange(length)
        allowed = (query_pos[:, None] >= all_pos[None, :]) & (seg_all[:, None] == seg_all[None, :])
        return jnp.where(allowed[None, None], raw_scores, MASKED)

    def forward_block(item):
        query_block, start = item
        masked = scores_of(query_block, start)
        row_max = jnp.max(masked, axis=-1, keepdims=True)
        exponent = jnp.exp(masked - row_max)
        row_total = jnp.sum(exponent, axis=-1, keepdims=True)
        attn_probs = (exponent / row_total).astype(jnp.bfloat16)
        mixture = jnp.einsum(
            "kgqp,pkd->qkgd", attn_probs, value_heads, preferred_element_type=jnp.float32
        )
        return (mixture.astype(jnp.bfloat16), (row_max + jnp.log(row_total))[..., 0])

    attn_blocks, lse_blocks = lax.map(forward_block, (query_blocks, block_starts))
    attn_head = attn_blocks.reshape(length, q_local * HD)
    attn_tok = lax.all_to_all(attn_head, "seq", split_axis=0, concat_axis=1, tiled=True)
    middle = hidden_in + jnp.dot(attn_tok, full_out, preferred_element_type=jnp.float32)
    gain_two, full_gate, full_up, full_down = gather_mlp(mlp_shards)
    rescale_two = lax.rsqrt(jnp.mean(middle * middle, axis=-1, keepdims=True) + EPS)
    normed_two = middle * rescale_two
    input_two = (normed_two * gain_two.astype(jnp.float32)).astype(jnp.bfloat16)
    gate_pre = jnp.dot(input_two, full_gate, preferred_element_type=jnp.float32)
    up_pre = jnp.dot(input_two, full_up, preferred_element_type=jnp.float32)
    gate_sig = jax.nn.sigmoid(gate_pre)
    gate_act = gate_pre * gate_sig
    inner = (gate_act * up_pre).astype(jnp.bfloat16)
    result = middle + jnp.dot(inner, full_down, preferred_element_type=jnp.float32)
    output = result.astype(jnp.bfloat16)[None]
    gain_two, full_gate, full_up, full_down = gather_mlp(mlp_shards)
    hidden_units = full_gate.shape[1]
    grad_inner = jnp.einsum("td,fd->tf", grad_out, full_down, preferred_element_type=jnp.float32)
    grad_gate = grad_inner * up_pre * gate_sig * (1.0 + gate_pre * (1.0 - gate_sig))
    grad_up = grad_inner * gate_act
    grad_both = jnp.concatenate([grad_gate, grad_up], axis=1).astype(jnp.bfloat16)
    grad_input_two = jnp.einsum(
        "tf,cf->tc", grad_both[:, :hidden_units], full_gate, preferred_element_type=jnp.float32
    ) + jnp.einsum(
        "tf,cf->tc", grad_both[:, hidden_units:], full_up, preferred_element_type=jnp.float32
    )
    grad_gain_two, grad_mid = norm_back(
        grad_input_two, normed_two, rescale_two, gain_two.astype(jnp.float32)
    )
    grad_mid = grad_mid + grad_out.astype(jnp.float32)
    both_rows = lax.psum_scatter(
        outer_term(input_two, grad_both), ("seq", "fsdp"), scatter_dimension=0, tiled=True
    )
    grad_down_w = lax.psum_scatter(
        outer_term(inner, grad_out), ("seq", "fsdp"), scatter_dimension=0, tiled=True
    )
    grad_gate_w = both_rows[:, :hidden_units]
    grad_up_w = both_rows[:, hidden_units:]
    gain_one, full_query, full_key, full_value, full_bias, full_out = gather_attention(attn_shards)
    grad_branch = grad_mid.astype(jnp.bfloat16)
    grad_out_w = lax.psum_scatter(
        outer_term(attn_tok, grad_branch), ("seq", "fsdp"), scatter_dimension=0, tiled=True
    )
    grad_attn_tok = jnp.einsum(
        "td,hd->th", grad_branch, full_out, preferred_element_type=jnp.float32
    ).astype(jnp.bfloat16)
    grad_attn_head = lax.all_to_all(grad_attn_tok, "seq", split_axis=1, concat_axis=0, tiled=True)
    grad_blocks = grad_attn_head.reshape(block_count, length, kv_local, group_size, HD)

    def backward_block(carry, item):
        key_accum, value_accum = carry
        query_block, grad_block, lse_block, start = item
        masked = scores_of(query_block, start)
        attn_probs = jnp.exp(masked - lse_block[..., None])
        probs_low = attn_probs.astype(jnp.bfloat16)
        grad_probs = jnp.einsum(
            "qkgd,pkd->kgqp", grad_block, value_heads, preferred_element_type=jnp.float32
        )
        inner_sum = jnp.sum(attn_probs * grad_probs, axis=-1, keepdims=True)
        grad_scores = (attn_probs * (grad_probs - inner_sum)).astype(jnp.bfloat16)
        grad_query = (
            jnp.einsum("kgqp,pkd->qkgd", grad_scores, key_heads, preferred_element_type=jnp.float32)
            * score_scale
        )
        key_accum = (
            key_accum
            + jnp.einsum(
                "kgqp,qkgd->pkd", grad_scores, query_block, preferred_element_type=jnp.float32
            )
            * score_scale
        )
        value_accum = value_accum + jnp.einsum(
            "kgqp,qkgd->pkd", probs_low, grad_block, preferred_element_type=jnp.float32
        )
        return ((key_accum, value_accum), grad_query)

    empty_heads = jnp.zeros((length, kv_local, HD), jnp.float32)
    (grad_key_head, grad_value_head), grad_query_blocks = lax.scan(
        backward_block,
        (empty_heads, empty_heads),
        (query_blocks, grad_blocks, lse_blocks, block_starts),
    )
    grad_query_pre = unrotate(
        grad_query_blocks.reshape(length, q_local * HD), cos_all, sin_all
    ).astype(jnp.bfloat16)
    grad_key_pre = unrotate(grad_key_head.reshape(length, kv_local * HD), cos_all, sin_all).astype(
        jnp.bfloat16
    )
    grad_value_pre = grad_value_head.reshape(length, kv_local * HD).astype(jnp.bfloat16)
    grad_query_tok, grad_key_tok, grad_value_tok = (
        lax.all_to_all(grad_query_pre, "seq", split_axis=0, concat_axis=1, tiled=True),
        lax.all_to_all(grad_key_pre, "seq", split_axis=0, concat_axis=1, tiled=True),
        lax.all_to_all(grad_value_pre, "seq", split_axis=0, concat_axis=1, tiled=True),
    )
    query_cols = grad_query_tok.shape[1]
    key_cols = grad_key_tok.shape[1]
    grad_qkv_tok = jnp.concatenate([grad_query_tok, grad_key_tok, grad_value_tok], axis=1)
    qkv_rows = lax.psum_scatter(
        outer_term(input_one, grad_qkv_tok), ("seq", "fsdp"), scatter_dimension=0, tiled=True
    )
    grad_query_w = qkv_rows[:, :query_cols]
    grad_key_w = qkv_rows[:, query_cols : query_cols + key_cols]
    grad_value_w = qkv_rows[:, query_cols + key_cols :]
    grad_qkv_sum = jnp.sum(grad_qkv_tok.astype(jnp.float32), axis=0)
    grad_input_one = (
        jnp.einsum("th,ch->tc", grad_query_tok, full_query, preferred_element_type=jnp.float32)
        + jnp.einsum("th,ch->tc", grad_key_tok, full_key, preferred_element_type=jnp.float32)
        + jnp.einsum("th,ch->tc", grad_value_tok, full_value, preferred_element_type=jnp.float32)
    )
    grad_gain_one, grad_first = norm_back(
        grad_input_one, normed_one, rescale_one, gain_one.astype(jnp.float32)
    )
    grad_total = grad_mid + grad_first
    small_sums = (
        lax.psum_scatter(grad_gain_one, ("seq", "fsdp"), scatter_dimension=0, tiled=True),
        lax.psum_scatter(grad_qkv_sum, ("seq", "fsdp"), scatter_dimension=0, tiled=True),
        lax.psum_scatter(grad_gain_two, ("seq", "fsdp"), scatter_dimension=0, tiled=True),
    )
    return (
        output,
        grad_total.astype(jnp.bfloat16)[None],
        small_sums[0],
        grad_query_w,
        grad_key_w,
        grad_value_w,
        small_sums[1],
        grad_out_w,
        small_sums[2],
        grad_gate_w,
        grad_up_w,
        grad_down_w,
    )


def solution(mesh):
    placed = (
        P("fsdp", "seq", None),
        P("fsdp", None),
        P(("seq", "fsdp")),
        P(("seq", "fsdp"), None),
        P(("seq", "fsdp"), None),
        P(("seq", "fsdp"), None),
        P(("seq", "fsdp")),
        P(("seq", "fsdp"), None),
        P(("seq", "fsdp")),
        P(("seq", "fsdp"), None),
        P(("seq", "fsdp"), None),
        P(("seq", "fsdp"), None),
        P("fsdp", "seq", None),
    )
    return jax.shard_map(
        body,
        mesh=mesh,
        in_specs=placed,
        out_specs=(
            P("fsdp", "seq", None),
            P("fsdp", "seq", None),
            P(("seq", "fsdp")),
            P(("seq", "fsdp"), None),
            P(("seq", "fsdp"), None),
            P(("seq", "fsdp"), None),
            P(("seq", "fsdp")),
            P(("seq", "fsdp"), None),
            P(("seq", "fsdp")),
            P(("seq", "fsdp"), None),
            P(("seq", "fsdp"), None),
            P(("seq", "fsdp"), None),
        ),
        check_vma=False,
    )
```

profile of v0, /device:TPU:0, one launch (start us, length us, event | category | flops | bytes accessed | tf_op | source)
XLA Modules:
  0.0 2437.9 jit_solution(7162234540868021717)
XLA Ops:
  13.2 42.3 %all-reduce.8 = (bf16[2048]{0:T(1024)(128)(2,1)S(1)}, bf16[1536]{0:T(1024)(128)(2,1)S(1)}, bf16[1536]{0:T(1024)(128)(2,1)S(1)}) all-reduce(bf16[2048]{0:T(1024)(128)(2,1)S(1)} %dynamic-update-slice.1, bf16[1536]{0:T(1024)(128)(2,1)S(1)} %dynamic-update-slice, ...), channel_id=1, replica_groups=mesh['seq'=2,'fsdp'=16] {'seq','fsdp'}, use_global_device_ids=true, to_apply=%add.1 | all-reduce | flops 5120 | bytes 20480
  55.7 44.4 %all_gather.40 = bf16[1536,256]{1,0:T(8,128)(2,1)S(1)} all-gather(bf16[48,256]{1,0:T(8,128)(2,1)S(1)} %copy-done.24), channel_id=1, replica_groups=mesh['seq'=2,'fsdp'=16] {'seq','fsdp'}, dimensions={0}, use_global_device_ids=true | all-gather | bytes 811008 | tf_op jit(solution)/shard_map/all_gather | solution.py:60
  106.0 40.2 %all_gather.42 = bf16[1536,256]{1,0:T(8,128)(2,1)S(1)} all-gather(bf16[48,256]{1,0:T(8,128)(2,1)S(1)} %copy-done.25), channel_id=1, replica_groups=mesh['seq'=2,'fsdp'=16] {'seq','fsdp'}, dimensions={0}, use_global_device_ids=true | all-gather | bytes 811008 | tf_op jit(solution)/shard_map/all_gather | solution.py:59
  167.7 10.2 all-to-all-done.2
  189.4 19.7 all-to-all-done.3
  213.5 104.5 %all-gather.10.cloned.1.call-done = bf16[1536,8960]{1,0:T(8,128)(2,1)} async-done(((bf16[48,8960]{1,0:T(8,128)(2,1)}), bf16[1536,8960]{1,0:T(8,128)(2,1)}) %all-gather.10.cloned.1.call-update) | async-done | bytes 27525136 | tf_op jit(solution)/shard_map/all_gather | solution.py:69
  318.0 15.3 fusion.77
  333.3 151.5 %all-gather.12.cloned.1.call-done = bf16[1536,8960]{1,0:T(8,128)(2,1)} async-done(((bf16[48,8960]{1,0:T(8,128)(2,1)}), bf16[1536,8960]{1,0:T(8,128)(2,1)}) %all-gather.12.cloned.1.call-update) | async-done | bytes 27525136 | tf_op jit(solution)/shard_map/all_gather | solution.py:70
  484.9 15.2 fusion.78
  500.0 151.7 %all-gather.14.cloned.1.call-done = bf16[8960,1536]{1,0:T(8,128)(2,1)} async-done(((bf16[280,1536]{1,0:T(8,128)(2,1)}), bf16[8960,1536]{1,0:T(8,128)(2,1)}) %all-gather.14.cloned.1.call-update) | async-done | bytes 27525136 | tf_op jit(solution)/shard_map/all_gather | solution.py:71
  651.7 21.4 multiply_convert_fusion
  673.1 14.8 fusion.79
  687.9 15.4 multiply_reduce_fusion
  713.4 9.4 all-to-all-done.4
  754.6 11.3 all_to_all.125
  766.8 6.4 fusion.55
  774.3 47.0 %fusion = f32[1536,17920]{1,0:T(8,128)} fusion(bf16[256,1536]{1,0:T(8,128)(2,1)S(1)} %copy-done.12, bf16[256,8960]{1,0:T(8,128)(2,1)} %get-tuple-element.79, bf16[256,8960]{1,0:T(8,128)(2,1)} %get-tuple-element.80), kind=kOutput, calls=%fused_computation | convolution fusion | flops 14111211520 | bytes 120061952 | tf_op jit(solution)/shard_map/tc,th->ch/dot_general | solution.py:76
  829.2 22.7 fusion.51
  851.9 15.6 fusion.18
  874.8 40.4 %all-reduce.7 = (f32[1536]{0:T(1024)S(1)}, f32[2048]{0:T(1024)S(1)}, f32[1536]{0:T(1024)S(1)}) all-reduce(f32[1536]{0:T(1024)S(1)} %get-tuple-element.60, f32[2048]{0:T(1024)S(1)} %convert_reduce_fusion, f32[1536]{0:T(1024)S(1)} %copy-done.29), channel_id=2, replica_groups=mesh['seq'=2,'fsdp'=16] {'seq','fsdp'}, use_global_device_ids=true, to_apply=%region_8.9.clone | all-reduce | flops 5120 | bytes 40960
  919.8 7.8 reduce-scatter.7.cloned.1.call-done
  930.7 889.7 %reduce-scatter.11.cloned.1.call-done = f32[48,17920]{1,0:T(8,128)} async-done(((f32[1536,17920]{1,0:T(8,128)}), f32[48,17920]{1,0:T(8,128)}) %reduce-scatter.11.cloned.1.call-update) | async-done | bytes 3440656 | tf_op jit(solution)/shard_map/reduce_scatter | solution.py:188
  1824.4 137.3 %reduce-scatter.9.cloned.1.call-done = f32[48,1536]{1,0:T(8,128)} async-done(((f32[1536,1536]{1,0:T(8,128)}), f32[48,1536]{1,0:T(8,128)}) %reduce-scatter.9.cloned.1.call-update) | async-done | bytes 294928 | tf_op jit(solution)/shard_map/reduce_scatter | solution.py:198
  1961.7 469.4 %reduce-scatter.13.cloned.1.call-done = f32[280,1536]{1,0:T(8,128)} async-done(((f32[8960,1536]{1,0:T(8,128)}), f32[280,1536]{1,0:T(8,128)}) %reduce-scatter.13.cloned.1.call-update) | async-done | bytes 1720336
  (180 shorter events, 119.5 us)
Async XLA Ops:
  7.2 141.2 %all-gather.6.cloned.1.call-start = ((), (), s32[]{:S(2)}) async-start(), calls=%async_computation.12 | async-start | bytes 4866048 | tf_op jit(solution)/shard_map/all_gather | solution.py:58
  7.9 181.5 %all-gather.8.cloned.1.call-start = ((), (), s32[]{:S(2)}) async-start(), calls=%async_computation.13 | async-start | bytes 4866048 | tf_op jit(solution)/shard_map/all_gather | solution.py:62
  8.7 309.3 %all-gather.10.cloned.1.call-start = ((), (), s32[]{:S(2)}) async-start(), calls=%async_computation.14 | async-start | bytes 28385280 | tf_op jit(solution)/shard_map/all_gather | solution.py:69
  9.4 96.5 %copy-start.25 = (bf16[48,256]{1,0:T(8,128)(2,1)S(1)}, bf16[48,256]{1,0:T(8,128)(2,1)}, u32[]{:S(2)}) copy-start(bf16[48,256]{1,0:T(8,128)(2,1)} %param.17) | copy-start | bytes 73732
  9.4 475.4 %all-gather.12.cloned.1.call-start = ((), (), s32[]{:S(2)}) async-start(), calls=%async_computation.15 | async-start | bytes 28385280 | tf_op jit(solution)/shard_map/all_gather | solution.py:70
  10.0 641.7 %all-gather.14.cloned.1.call-start = ((), (), s32[]{:S(2)}) async-start(), calls=%async_computation.16 | async-start | bytes 28385280 | tf_op jit(solution)/shard_map/all_gather | solution.py:71
  55.4 92.9 %copy-start.18 = (f32[1536]{0:T(1024)}, f32[1536]{0:T(1024)S(1)}, u32[]{:S(2)}) copy-start(f32[1536]{0:T(1024)S(1)} %convert_element_type.154) | copy-start | bytes 18436
  55.7 92.7 %copy-start.22 = (f32[256]{0:T(256)}, f32[256]{0:T(256)S(1)}, u32[]{:S(2)}) copy-start(f32[256]{0:T(256)S(1)} %add_rsqrt_fusion.1) | copy-start | bytes 3076
  102.2 53.2 %all-to-all-start = ((bf16[256,2,128]{0,2,1:T(8,128)(2,1)}), bf16[256,2,128]{0,2,1:T(8,128)(2,1)S(1)}, u32[]{:S(2)}, u32[]{:S(2)}) async-start(bf16[256,2,128]{0,2,1:T(8,128)(2,1)} %bitcast.2), calls=%async_computation | async-start | bytes 262144 | tf_op jit(solution)/shard_map/all_to_all | solution.py:125
  105.6 605.7 %copy-start.30 = (f32[64]{0:T(128)}, f32[64]{0:T(128)S(1)}, u32[]{:S(2)}) copy-start(f32[64]{0:T(128)S(1)} %multiply_power_fusion) | copy-start | bytes 772
  155.4 8.2 all-to-all-start.1
  163.6 14.4 all-to-all-start.2
  185.7 23.4 all-to-all-start.3
  189.4 521.9 %copy-start.26 = (f32[512]{0:T(512)}, f32[512]{0:T(512)S(1)}, u32[]{:S(2)}) copy-start(f32[512]{0:T(512)S(1)} %iota_convert_fusion) | copy-start | bytes 6148
  213.2 474.7 %copy-start.2 = (f32[256,1536]{1,0:T(8,128)}, f32[256,1536]{1,0:T(8,128)S(1)}, u32[]{:S(2)}) copy-start(f32[256,1536]{1,0:T(8,128)S(1)} %get-tuple-element.103) | copy-start | bytes 4718596
  213.4 104.6 %copy-start.11 = (bf16[256,1536]{1,0:T(8,128)(2,1)}, bf16[256,1536]{1,0:T(8,128)(2,1)S(1)}, u32[]{:S(2)}) copy-start(bf16[256,1536]{1,0:T(8,128)(2,1)S(1)} %multiply_convert_fusion.3) | copy-start | bytes 2359300
  333.3 318.4 %copy-start.9 = (bf16[1,256,1536]{2,1,0:T(8,128)(2,1)S(1)}, bf16[1,256,1536]{2,1,0:T(8,128)(2,1)}, u32[]{:S(2)}) copy-start(bf16[1,256,1536]{2,1,0:T(8,128)(2,1)} %param.25) | copy-start | bytes 2359300
  707.7 15.0 all-to-all-start.4
  738.9 7.8 all-to-all-start.6
  746.7 7.8 all-to-all-start.7
  750.1 177.4 %reduce-scatter.7.cloned.1.call-start = ((), (), s32[]{:S(2)}) async-start(), calls=%async_computation.17 | async-start | bytes 12976128 | tf_op jit(solution)/shard_map/reduce_scatter | solution.py:255
  773.2 1047.2 %reduce-scatter.11.cloned.1.call-start = ((), (), s32[]{:S(2)}) async-start(), calls=%async_computation.19 | async-start | bytes 113541120 | tf_op jit(solution)/shard_map/reduce_scatter | solution.py:188
  821.4 1140.3 %reduce-scatter.9.cloned.1.call-start = ((), (), s32[]{:S(2)}) async-start(), calls=%async_computation.18 | async-start | bytes 9732096 | tf_op jit(solution)/shard_map/reduce_scatter | solution.py:198
  827.9 1603.1 %reduce-scatter.13.cloned.1.call-start = ((), (), s32[]{:S(2)}) async-start(), calls=%async_computation.20 | async-start | bytes 56770560
  (28 other events, 236.4 us)
Sparse Core Ops, SparseCore 0:
  10.9 70.6 all-gather.5
  84.4 64.1 all-gather.7
  151.5 166.4 all-gather.9
  320.8 164.0 all-gather.11
  487.6 164.0 all-gather.13
  773.4 154.1 reduce-scatter.6
  935.1 885.2 reduce-scatter.10
  1826.9 134.7 reduce-scatter.8
  1969.8 461.1 reduce-scatter.12
where the time goes:
time: 2450 us; the launch traced here: 2440 us
  waiting for transfers between devices  1960 us (80%)
  matrix products  208 us (8%)
  blocking collectives  179 us (7%)
  local copies, waits for them, and re-layouts  34.3 us (1%)
  starting transfers between devices  24.6 us (1%)
    reduce_scatter x1, waiting for transfers between devices, body(): lax.psum_scatter(outer_term(input_two, grad_both), ('seq', 'fsdp'), scatt...  890 us
    unnamed x10, waiting for transfers between devices  473 us
    all_gather x1, waiting for transfers between devices, gather_mlp(): lax.all_gather(shards[3], ('seq', 'fsdp'), axis=0, tiled=True)  152 us
    all_gather x1, waiting for transfers between devices, gather_mlp(): lax.all_gather(shards[2], ('seq', 'fsdp'), axis=0, tiled=True)  152 us
    reduce_scatter x1, waiting for transfers between devices, body(): lax.psum_scatter(outer_term(attn_tok, grad_branch), ('seq', 'fsdp'), scat...  137 us
    all_gather x1, waiting for transfers between devices, gather_mlp(): lax.all_gather(shards[1], ('seq', 'fsdp'), axis=0, tiled=True)  105 us
    unnamed x2, blocking collectives  82.7 us
    dot_general x4, matrix products, outer_term(): jnp.einsum('tc,th->ch', left, right, preferred_element_type=jnp.float32)  81.6 us
  transfers between devices with their start and end apart: 16, of which 13 were waited for; matrix products, arithmetic and copies ran while one was open for 7% of the time, Pallas kernels for 0%

commit v1 on v0

v1 whole, which is shorter than its diff:
```python
import jax
import jax.numpy as jnp
from jax import lax
from jax.sharding import Mesh, PartitionSpec as P

HD = 128
EPS = 1e-06
ROPE_BASE = 1000000.0
MASKED = -1e30
NZ = 4
NC = 2
ALL = ("y", "z", "x", "c")
TP = ("z", "c")
DP = ("y", "x")
F32 = jnp.float32
BF16 = jnp.bfloat16


def tables(positions):
    freq = ROPE_BASE ** (-jnp.arange(0, HD, 2).astype(F32) / HD)
    angle = positions.astype(F32)[:, None] * freq[None, :]
    return (jnp.cos(angle), jnp.sin(angle))


def rotate(values, cosine, sine):
    count = values.shape[0]
    split = values.reshape(count, -1, HD)
    half = HD // 2
    first = split[..., :half]
    second = split[..., half:]
    cos_b = cosine[:, None, :]
    sin_b = sine[:, None, :]
    turned = jnp.concatenate(
        [first * cos_b - second * sin_b, second * cos_b + first * sin_b], axis=-1
    )
    return turned.reshape(count, -1)


def dot(a, b):
    return jnp.dot(a, b, preferred_element_type=F32)


def dot_nt(a, b):
    return lax.dot_general(a, b, (((1,), (1,)), ((), ())), preferred_element_type=F32)


def dot_tn(a, b):
    return lax.dot_general(a, b, (((0,), (0,)), ((), ())), preferred_element_type=F32)


def norm_back(grad_normed, normed, rescale, gain_vec):
    grad_gain = jnp.sum(grad_normed * normed, axis=0)
    scaled = grad_normed * gain_vec
    grad_x = rescale * (scaled - normed * jnp.mean(scaled * normed, axis=-1, keepdims=True))
    return (grad_gain, grad_x)


def make_body(ny, nx):
    def spread_columns(shard):
        rows, cols = shard.shape
        fs = cols // (ny * NZ * nx * NC)
        view = shard.reshape(rows, ny, NZ, nx, NC, fs)
        return view.transpose(2, 4, 0, 1, 3, 5).reshape(NZ * NC, rows, ny * nx * fs)

    def unspread_columns(blocks):
        _, rows, width = blocks.shape
        fs = width // (ny * nx)
        view = blocks.reshape(NZ, NC, rows, ny, nx, fs)
        return view.transpose(2, 3, 0, 4, 1, 5).reshape(rows, -1)

    def gather_columns(shard):
        blocks = spread_columns(shard)
        rows, width = blocks.shape[1:]
        mine = lax.all_to_all(blocks, TP, split_axis=0, concat_axis=0, tiled=True)
        full = lax.all_gather(mine, DP, axis=0, tiled=False)
        view = full.reshape(ny, nx, NZ, NC, rows, width).transpose(0, 2, 1, 3, 4, 5)
        return view.reshape(-1, width)

    def scatter_columns(grad):
        width = grad.shape[1]
        rows = grad.shape[0] // (ny * NZ * nx * NC)
        view = grad.reshape(ny, NZ, nx, NC, rows, width).transpose(0, 2, 1, 3, 4, 5)
        view = view.reshape(ny * nx * NZ * NC, rows, width)
        part = lax.psum_scatter(view, DP, scatter_dimension=0, tiled=True)
        back = lax.all_to_all(part, TP, split_axis=0, concat_axis=0, tiled=True)
        return unspread_columns(back).astype(F32)

    def body(
        inputs,
        segment_ids,
        attn_gain,
        q_weight,
        k_weight,
        v_weight,
        qkv_bias,
        o_weight,
        mlp_gain,
        gate_weight,
        up_weight,
        down_weight,
        cotangent,
    ):
        tok_rows = inputs.shape[1]
        hidden_in = inputs[0].astype(F32)
        grad_out = cotangent[0]
        seg_all = segment_ids[0]
        length = seg_all.shape[0]
        seq_place = lax.axis_index("y")
        tok_pos = seq_place * tok_rows + jnp.arange(tok_rows)
        cos_tok, sin_tok = tables(tok_pos)
        query_width = q_weight.shape[1]
        key_width = k_weight.shape[1]
        kv_heads = key_width // HD
        q_heads = query_width // HD
        group = q_heads // kv_heads

        packed = jnp.concatenate([q_weight, k_weight, v_weight, o_weight], axis=1)
        full = lax.all_gather(packed, ALL, axis=0, tiled=True)
        qkv_width = query_width + 2 * key_width
        full_qkv = full[:, :qkv_width]
        full_out = full[:, qkv_width:]
        small = jnp.concatenate([attn_gain, qkv_bias, mlp_gain])[None]
        small_all = lax.all_gather(small, ALL, axis=0, tiled=True).astype(F32)
        g_rows = attn_gain.shape[0]
        b_rows = qkv_bias.shape[0]
        gain_one = small_all[:, :g_rows].reshape(-1)
        bias = small_all[:, g_rows : g_rows + b_rows].reshape(-1)
        gain_two = small_all[:, g_rows + b_rows :].reshape(-1)

        grad_out_all = lax.all_gather(grad_out, TP, axis=0, tiled=True)
        full_gate = gather_columns(gate_weight)
        full_up = gather_columns(up_weight)
        full_down = lax.all_gather(down_weight, DP, axis=0, tiled=True)

        rescale_one = lax.rsqrt(jnp.mean(hidden_in * hidden_in, axis=-1, keepdims=True) + EPS)
        normed_one = hidden_in * rescale_one
        input_one = (normed_one * gain_one).astype(BF16)
        qkv_pre = dot(input_one, full_qkv) + bias
        query = rotate(qkv_pre[:, :query_width], cos_tok, sin_tok).astype(BF16)
        key = rotate(qkv_pre[:, query_width : query_width + key_width], cos_tok, sin_tok)
        kv = jnp.concatenate([key, qkv_pre[:, query_width + key_width :]], axis=1).astype(BF16)
        kv_all = lax.all_gather(kv, "y", axis=0, tiled=True)
        key_heads = kv_all[:, :key_width].reshape(length, kv_heads, HD)
        value_heads = kv_all[:, key_width:].reshape(length, kv_heads, HD)
        query_heads = query.reshape(tok_rows, kv_heads, group, HD)
        score_scale = HD ** (-0.5)
        all_pos = jnp.arange(length)
        seg_tok = lax.dynamic_slice(seg_all, (seq_place * tok_rows,), (tok_rows,))
        allowed = (tok_pos[:, None] >= all_pos[None, :]) & (seg_tok[:, None] == seg_all[None, :])
        scores = (
            jnp.einsum("qkgd,pkd->kgqp", query_heads, key_heads, preferred_element_type=F32)
            * score_scale
        )
        masked = jnp.where(allowed[None, None], scores, MASKED)
        row_max = jnp.max(masked, axis=-1, keepdims=True)
        exponent = jnp.exp(masked - row_max)
        row_total = jnp.sum(exponent, axis=-1, keepdims=True)
        probs = exponent / row_total
        probs_low = probs.astype(BF16)
        mixture = jnp.einsum("kgqp,pkd->qkgd", probs_low, value_heads, preferred_element_type=F32)
        attn_tok = mixture.astype(BF16).reshape(tok_rows, query_width)
        middle = hidden_in + dot(attn_tok, full_out)

        rescale_two = lax.rsqrt(jnp.mean(middle * middle, axis=-1, keepdims=True) + EPS)
        normed_two = middle * rescale_two
        input_two = (normed_two * gain_two).astype(BF16)
        input_all = lax.all_gather(input_two, TP, axis=0, tiled=True)
        gate_pre = dot(input_all, full_gate)
        up_pre = dot(input_all, full_up)
        gate_sig = jax.nn.sigmoid(gate_pre)
        gate_act = gate_pre * gate_sig
        inner = (gate_act * up_pre).astype(BF16)
        grad_inner = dot_nt(grad_out_all, full_down)
        grad_gate = (
            grad_inner * up_pre * gate_sig * (1.0 + gate_pre * (1.0 - gate_sig))
        ).astype(BF16)
        grad_up = (grad_inner * gate_act).astype(BF16)
        grad_in_part = (dot_nt(grad_gate, full_gate) + dot_nt(grad_up, full_up)).astype(BF16)
        grad_input_two = lax.psum_scatter(
            grad_in_part, TP, scatter_dimension=0, tiled=True
        ).astype(F32)
        out_part = dot(inner, full_down).astype(BF16)
        out_sum = lax.psum_scatter(out_part, TP, scatter_dimension=0, tiled=True)
        output = (middle + out_sum.astype(F32)).astype(BF16)[None]

        grad_gate_w = scatter_columns(dot_tn(input_all, grad_gate).astype(BF16))
        grad_up_w = scatter_columns(dot_tn(input_all, grad_up).astype(BF16))
        grad_down_w = lax.psum_scatter(
            dot_tn(inner, grad_out_all).astype(BF16), DP, scatter_dimension=0, tiled=True
        ).astype(F32)

        grad_gain_two, grad_mid = norm_back(grad_input_two, normed_two, rescale_two, gain_two)
        grad_mid = grad_mid + grad_out.astype(F32)
        grad_branch = grad_mid.astype(BF16)
        grad_attn = dot_nt(grad_branch, full_out).astype(BF16)
        grad_heads = grad_attn.reshape(tok_rows, kv_heads, group, HD)
        grad_probs = jnp.einsum(
            "qkgd,pkd->kgqp", grad_heads, value_heads, preferred_element_type=F32
        )
        inner_sum = jnp.sum(probs * grad_probs, axis=-1, keepdims=True)
        grad_scores = (probs * (grad_probs - inner_sum)).astype(BF16)
        grad_query = (
            jnp.einsum("kgqp,pkd->qkgd", grad_scores, key_heads, preferred_element_type=F32)
            * score_scale
        ).reshape(tok_rows, query_width)
        grad_key = (
            jnp.einsum("kgqp,qkgd->pkd", grad_scores, query_heads, preferred_element_type=F32)
            * score_scale
        ).reshape(length, key_width)
        grad_value = jnp.einsum(
            "kgqp,qkgd->pkd", probs_low, grad_heads, preferred_element_type=F32
        ).reshape(length, key_width)
        grad_kv = jnp.concatenate([grad_key, grad_value], axis=1).astype(BF16)
        other = lax.dynamic_slice(
            grad_kv, ((1 - seq_place) * tok_rows, 0), (tok_rows, 2 * key_width)
        )
        own = lax.dynamic_slice(grad_kv, (seq_place * tok_rows, 0), (tok_rows, 2 * key_width))
        swapped = lax.ppermute(other, "y", [(0, 1), (1, 0)])
        grad_kv_tok = own.astype(F32) + swapped.astype(F32)
        grad_query_pre = rotate(grad_query, cos_tok, -sin_tok).astype(BF16)
        grad_key_pre = rotate(grad_kv_tok[:, :key_width], cos_tok, -sin_tok).astype(BF16)
        grad_value_pre = grad_kv_tok[:, key_width:].astype(BF16)
        grad_qkv = jnp.concatenate([grad_query_pre, grad_key_pre, grad_value_pre], axis=1)
        grad_attn_w = lax.psum_scatter(
            jnp.concatenate(
                [dot_tn(input_one, grad_qkv), dot_tn(attn_tok, grad_branch)], axis=1
            ).astype(BF16),
            ALL,
            scatter_dimension=0,
            tiled=True,
        ).astype(F32)
        grad_qkv_sum = jnp.sum(grad_qkv.astype(F32), axis=0)
        grad_input_one = dot_nt(grad_qkv, full_qkv)
        grad_gain_one, grad_first = norm_back(grad_input_one, normed_one, rescale_one, gain_one)
        grad_total = grad_mid + grad_first
        shards = small_all.shape[0]
        small_grads = jnp.concatenate(
            [
                grad_gain_one.reshape(shards, -1),
                grad_qkv_sum.reshape(shards, -1),
                grad_gain_two.reshape(shards, -1),
            ],
            axis=1,
        )
        small_sums = lax.psum_scatter(small_grads, ALL, scatter_dimension=0, tiled=True)[0]
        return (
            output,
            grad_total.astype(BF16)[None],
            small_sums[:g_rows],
            grad_attn_w[:, :query_width],
            grad_attn_w[:, query_width : query_width + key_width],
            grad_attn_w[:, query_width + key_width : qkv_width],
            small_sums[g_rows : g_rows + b_rows],
            grad_attn_w[:, qkv_width:],
            small_sums[g_rows + b_rows :],
            grad_gate_w,
            grad_up_w,
            grad_down_w,
        )

    return body


def solution(mesh):
    ny = mesh.shape["seq"]
    nx = mesh.shape["fsdp"] // (NZ * NC)
    grid = Mesh(mesh.devices.reshape(ny, NZ, nx, NC), ALL)
    tokens = P(("z", "x", "c"), "y", None)
    rows = P(ALL, None)
    vec = P(ALL)
    return jax.shard_map(
        make_body(ny, nx),
        mesh=grid,
        in_specs=(
            tokens,
            P(("z", "x", "c"), None),
            vec,
            rows,
            rows,
            rows,
            vec,
            rows,
            vec,
            rows,
            rows,
            rows,
            tokens,
        ),
        out_specs=(tokens, tokens, vec, rows, rows, rows, vec, rows, vec, rows, rows, rows),
        check_vma=False,
    )
```

time: 2450 us -> 914 us (0.37)
  waiting for transfers between devices: 1960 us -> 461 us
  matrix products: 208 us -> 161 us
  local copies, waits for them, and re-layouts: 34.3 us -> 72.2 us
  blocking collectives: 179 us -> 153 us
    reduce_scatter x3 -> x5, waiting for transfers between devices: 1030 us -> 199 us  [the longest x1 68.7 us: body(): out_sum = lax.psum_scatter(out_part, TP, scatter_dimension=0, tiled=True)]
    unnamed x10 -> x13, waiting for transfers between devices: 473 us -> 46.1 us
    all_gather x5 -> x6, waiting for transfers between devices: 408 us -> 209 us  [the longest x1 66.3 us: body(): grad_out_all = lax.all_gather(grad_out, TP, axis=0, tiled=True)]
    all_gather x2 -> x1, blocking collectives: 84.6 us -> 15.1 us  [body(): kv_all = lax.all_gather(kv, 'y', axis=0, tiled=True)]
    dot_general x24 -> x20, matrix products: 208 us -> 156 us  [the longest x5 58.2 us: dot_nt(): lax.dot_general(a, b, (((1,), (1,)), ((), ())), preferred_element_type=F32)]
    all_to_all x7 -> x3, waiting for transfers between devices: 45.2 us -> 0.01 us  [the longest x1 0.01 us: gather_columns(): mine = lax.all_to_all(blocks, TP, split_axis=0, concat_axis=0, tiled=True)]
    convert_element_type x6 -> x10, local copies, waits for them, and re-layouts: 3.71 us -> 36.6 us  [the longest x6 27.6 us: scatter_columns(): return unspread_columns(back).astype(F32)]
    all_to_all x1, blocking collectives: 11.3 us -> 36.7 us  [gather_columns(): mine = lax.all_to_all(blocks, TP, split_axis=0, concat_axis=0, tiled=True)]
  transfers between devices with their start and end apart: 16 -> 16, of which waited for: 13 -> 12; matrix products, arithmetic and copies ran while one was open for 7% -> 22% of each run, Pallas kernels for 0% -> 0%
where the time goes in v1:
time: 914 us; the launch traced here: 905 us
  waiting for transfers between devices  461 us (50%)
  matrix products  161 us (18%)
  blocking collectives  153 us (17%)
  local copies, waits for them, and re-layouts  72.2 us (8%)
  other arithmetic  27.5 us (3%)
  starting transfers between devices  15.6 us (2%)
  between operations  15.5 us (2%)
    unnamed x2, blocking collectives  101 us
    reduce_scatter x1, waiting for transfers between devices, body(): out_sum = lax.psum_scatter(out_part, TP, scatter_dimension=0, tiled=True)  68.7 us
    reduce_scatter x1, waiting for transfers between devices, body(): lax.psum_scatter(jnp.concatenate([dot_tn(input_one, grad_qkv), dot_tn(att...  66.7 us
    all_gather x1, waiting for transfers between devices, body(): grad_out_all = lax.all_gather(grad_out, TP, axis=0, tiled=True)  66.3 us
    all_gather x1, waiting for transfers between devices, body(): input_all = lax.all_gather(input_two, TP, axis=0, tiled=True)  62.7 us
    reduce_scatter x2, waiting for transfers between devices, scatter_columns(): part = lax.psum_scatter(view, DP, scatter_dimension=0, tiled=True)  60.2 us
    dot_general x5, matrix products, dot_nt(): lax.dot_general(a, b, (((1,), (1,)), ((), ())), preferred_element_type=F32)  58.2 us
    all_gather x2, waiting for transfers between devices, gather_columns(): full = lax.all_gather(mine, DP, axis=0, tiled=False)  55.6 us
  transfers between devices with their start and end apart: 16, of which 12 were waited for; matrix products, arithmetic and copies ran while one was open for 22% of the time, Pallas kernels for 0%

profile of v1, /device:TPU:0, one launch (start us, length us, event | category | flops | bytes accessed | tf_op | source)
XLA Modules:
  0.0 905.1 jit_solution(3185320676612491110)
XLA Ops:
  15.1 36.7 %all_to_all.20 = bf16[8,48,1120]{2,1,0:T(8,128)(2,1)} all-to-all(bf16[8,48,1120]{2,1,0:T(8,128)(2,1)S(1)} %reshape.301), channel_id=1, replica_groups=mesh['y'=2,'z'=4,'x'=2,'c'=2] {'z','c'}, dimensions={0} | all-to-all | bytes 1720320 | tf_op jit(solution)/shard_map/all_to_all | solution.py:74
  60.7 60.0 %all-reduce = bf16[5120]{0:T(1024)(128)(2,1)S(1)} all-reduce(bf16[5120]{0:T(1024)(128)(2,1)S(1)} %dynamic-update-slice), channel_id=2, replica_groups=mesh['y'=2,'z'=4,'x'=2,'c'=2] {'y','z','x','c'}, use_global_device_ids=true, to_apply=%add | all-reduce | flops 5120 | bytes 20480
  130.9 15.1 %all_gather.32 = bf16[512,512]{1,0:T(8,128)(2,1)S(1)} all-gather(bf16[256,512]{1,0:T(8,128)(2,1)S(1)} %pad_maximum_fusion.5), channel_id=1, replica_groups=mesh['y'=2,'z'=4,'x'=2,'c'=2] {'y'}, dimensions={0}, use_global_device_ids=true | all-gather | bytes 786432 | tf_op jit(solution)/shard_map/all_gather | solution.py:142
  165.8 8.3 all-gather.17.cloned.1.call-done
  176.4 47.4 %all-gather.19.cloned.1.call-done = bf16[32,48,1120]{2,1,0:T(8,128)(2,1)} async-done(((bf16[8,48,1120]{2,1,0:T(8,128)(2,1)}), bf16[32,48,1120]{2,1,0:T(8,128)(2,1)}) %all-gather.19.cloned.1.call-update) | async-done | bytes 3440656 | tf_op jit(solution)/shard_map/all_gather | solution.py:75
  227.9 62.7 %all-gather.13.cloned.1.call-done = bf16[2048,1536]{1,0:T(8,128)(2,1)} async-done(((bf16[256,1536]{1,0:T(8,128)(2,1)}), bf16[2048,1536]{1,0:T(8,128)(2,1)}) %all-gather.13.cloned.1.call-update) | async-done | bytes 6291472 | tf_op jit(solution)/shard_map/all_gather | solution.py:167
  290.6 11.9 %fusion.86 = f32[2048,1120]{0,1:T(8,128)} fusion(bf16[2048,1536]{1,0:T(8,128)(2,1)} %all-gather.13.cloned.1.call-done, bf16[1536,1120]{1,0:T(8,128)(2,1)S(1)} %bitcast.164), kind=kOutput, calls=%fused_computation.138 | convolution fusion | flops 7046430720 | bytes 18907136 | tf_op jit(solution)/shard_map/dot_general | solution.py:40
  302.6 10.0 %fusion.87 = f32[2048,1120]{0,1:T(8,128)} fusion(bf16[2048,1536]{1,0:T(8,128)(2,1)S(1)} %copy-done.37, bf16[1536,1120]{1,0:T(8,128)(2,1)S(1)} %bitcast.166), kind=kOutput, calls=%fused_computation.139 | convolution fusion | flops 7046430720 | bytes 18907136 | tf_op jit(solution)/shard_map/dot_general | solution.py:40
  312.6 24.8 %all-gather.15.cloned.1.call-done = bf16[1120,1536]{1,0:T(8,128)(2,1)} async-done(((bf16[280,1536]{1,0:T(8,128)(2,1)}), bf16[1120,1536]{1,0:T(8,128)(2,1)}) %all-gather.15.cloned.1.call-update) | async-done | bytes 3440656 | tf_op jit(solution)/shard_map/all_gather | solution.py:133
  337.4 66.3 %all-gather.21.cloned.1.call-done = bf16[1,2048,1536]{2,1,0:T(8,128)(2,1)} async-done(((bf16[1,256,1536]{2,1,0:T(8,128)(2,1)}), bf16[1,2048,1536]{2,1,0:T(8,128)(2,1)}) %all-gather.21.cloned.1.call-update) | async-done | bytes 6291472 | tf_op jit(solution)/shard_map/all_gather | solution.py:130
  403.7 19.9 %multiply_convert_fusion = (bf16[2048,1120]{0,1:T(8,128)(2,1)S(1)}, bf16[2048,1120]{0,1:T(8,128)(2,1)}, bf16[2048,1120]{0,1:T(8,128)(2,1)}) fusion(f32[2048,1120]{0,1:T(8,128)} %fusion.86, f32[2048,1120]{0,1:T(8,128)} %fusion.87, bf16[1120,1536]{1,0:T(8,128)(2,1)} %all-gather.15.cloned.1.call-done, bf16[1,2048,1536]{2,1,0:T(8,128)(2,1)} %all-gather.21.cloned.1.call-done), kind=kOutput, calls=%fused_computation.3 | convolution fusion | flops 7080837120 | bytes 41844736 | tf_op jit(solution)/shard_map/dot_general | solution.py:44
  423.6 14.9 %fusion.88 = f32[2048,1536]{1,0:T(8,128)} fusion(bf16[2048,1120]{0,1:T(8,128)(2,1)} %get-tuple-element.17, bf16[1536,1120]{1,0:T(8,128)(2,1)S(1)} %bitcast.165), kind=kOutput, calls=%fused_computation.140 | convolution fusion | flops 7046430720 | bytes 20611072 | tf_op jit(solution)/shard_map/dot_general | solution.py:44
  438.5 12.9 %add_convert_fusion = bf16[2048,1536]{1,0:T(8,128)(2,1)} fusion(f32[2048,1536]{1,0:T(8,128)} %fusion.88, bf16[2048,1120]{0,1:T(8,128)(2,1)S(1)} %get-tuple-element.16, bf16[1536,1120]{1,0:T(8,128)(2,1)S(1)} %bitcast.167), kind=kOutput, calls=%fused_computation.1 | convolution fusion | flops 7052722176 | bytes 26902528 | tf_op jit(solution)/shard_map/dot_general | solution.py:44
  453.4 12.5 %convolution_convert_fusion = bf16[2048,1536]{1,0:T(8,128)(2,1)} fusion(bf16[2048,1120]{0,1:T(8,128)(2,1)} %get-tuple-element.18, bf16[1120,1536]{1,0:T(8,128)(2,1)S(1)} %copy-done.38), kind=kOutput, calls=%fused_computation.8 | convolution fusion | flops 7049576448 | bytes 14319616 | tf_op jit(solution)/shard_map/dot_general | solution.py:40
  466.0 12.6 %convolution_convert_fusion.3 = bf16[1536,1120]{0,1:T(8,128)(2,1)} fusion(bf16[2048,1120]{0,1:T(8,128)(2,1)} %get-tuple-element.17, bf16[2048,1536]{1,0:T(8,128)(2,1)} %all-gather.13.cloned.1.call-done), kind=kOutput, calls=%fused_computation.11 | convolution fusion | flops 7048151040 | bytes 14319616 | tf_op jit(solution)/shard_map/dot_general | solution.py:48
  485.2 12.2 %convolution_convert_fusion.2 = bf16[1536,1120]{0,1:T(8,128)(2,1)} fusion(bf16[2048,1120]{0,1:T(8,128)(2,1)} %copy-done.39, bf16[2048,1536]{1,0:T(8,128)(2,1)} %all-gather.13.cloned.1.call-done), kind=kOutput, calls=%fused_computation.10 | convolution fusion | flops 7048151040 | bytes 14319616 | tf_op jit(solution)/shard_map/dot_general | solution.py:48
  504.7 12.1 %convolution_convert_fusion.4 = bf16[1120,1536]{1,0:T(8,128)(2,1)} fusion(bf16[2048,1120]{0,1:T(8,128)(2,1)} %get-tuple-element.18, bf16[1,2048,1536]{2,1,0:T(8,128)(2,1)} %all-gather.21.cloned.1.call-done), kind=kOutput, calls=%fused_computation.12 | convolution fusion | flops 7048151040 | bytes 14319616 | tf_op jit(solution)/shard_map/dot_general | solution.py:48
  521.8 68.7 %reduce-scatter.9.cloned.1.call-done = bf16[256,1536]{1,0:T(8,128)(2,1)} async-done(((bf16[2048,1536]{1,0:T(8,128)(2,1)}), bf16[256,1536]{1,0:T(8,128)(2,1)}) %reduce-scatter.9.cloned.1.call-update) | async-done | bytes 786448 | tf_op jit(solution)/shard_map/reduce_scatter | solution.py:183
  630.2 14.6 %reduce-scatter.15.cloned.1.call-done = bf16[8,48,1120]{2,1,0:T(8,128)(2,1)} async-done(((bf16[32,48,1120]{2,1,0:T(8,128)(2,1)}), bf16[8,48,1120]{2,1,0:T(8,128)(2,1)}) %reduce-scatter.15.cloned.1.call-update) | async-done | bytes 860176 | tf_op jit(solution)/shard_map/reduce_scatter | solution.py:84
  649.4 45.6 %reduce-scatter.17.cloned.1.call-done = bf16[8,48,1120]{2,1,0:T(8,128)(2,1)} async-done(((bf16[32,48,1120]{2,1,0:T(8,128)(2,1)}), bf16[8,48,1120]{2,1,0:T(8,128)(2,1)}) %reduce-scatter.17.cloned.1.call-update) | async-done | bytes 860176 | tf_op jit(solution)/shard_map/reduce_scatter | solution.py:84
  699.6 44.9 %reduce-scatter.19.cloned.1.call-done = bf16[280,1536]{1,0:T(8,128)(2,1)} async-done(((bf16[1120,1536]{1,0:T(8,128)(2,1)}), bf16[280,1536]{1,0:T(8,128)(2,1)}) %reduce-scatter.19.cloned.1.call-update) | async-done | bytes 860176
  776.3 6.7 fusion.45
  783.1 40.9 %all-reduce.1 = f32[32,160]{1,0:T(8,128)S(1)} all-reduce(f32[32,160]{1,0:T(8,128)S(1)} %pad_maximum_fusion.8), channel_id=8, replica_groups=mesh['y'=2,'z'=4,'x'=2,'c'=2] {'y','z','x','c'}, use_global_device_ids=true, to_apply=%region_12.13.clone | all-reduce | flops 5120 | bytes 40960
  827.9 66.7 %reduce-scatter.13.cloned.1.call-done = bf16[48,3584]{1,0:T(8,128)(2,1)} async-done(((bf16[1536,3584]{1,0:T(8,128)(2,1)}), bf16[48,3584]{1,0:T(8,128)(2,1)}) %reduce-scatter.13.cloned.1.call-update) | async-done | bytes 344080 | tf_op jit(solution)/shard_map/reduce_scatter | solution.py:224
  (220 shorter events, 161.3 us)
Async XLA Ops:
  7.2 117.7 %all-gather.11.cloned.1.call-start = ((), (), s32[]{:S(2)}) async-start(), calls=%async_computation.10 | async-start | bytes 11354112 | tf_op jit(solution)/shard_map/all_gather | solution.py:118
  9.0 165.0 %all-gather.17.cloned.1.call-start = ((), (), s32[]{:S(2)}) async-start(), calls=%async_computation.18 | async-start | bytes 4423680 | tf_op jit(solution)/shard_map/all_gather | solution.py:75
  13.4 38.4 %copy-start.17 = (bf16[48,8960]{1,0:T(8,128)(2,1)S(1)}, bf16[48,8960]{1,0:T(8,128)(2,1)}, u32[]{:S(2)}) copy-start(bf16[48,8960]{1,0:T(8,128)(2,1)} %param.23) | copy-start | bytes 2580484
  54.2 69.6 %copy-start.33 = (s32[1,512]{1,0:T(1,128)S(1)}, s32[1,512]{1,0:T(1,128)}, u32[]{:S(2)}) copy-start(s32[1,512]{1,0:T(1,128)} %param.14) | copy-start | bytes 6148
  54.2 69.6 %copy-start.2 = (bf16[1,256,1536]{2,1,0:T(8,128)(2,1)S(1)}, bf16[1,256,1536]{2,1,0:T(8,128)(2,1)}, u32[]{:S(2)}) copy-start(bf16[1,256,1536]{2,1,0:T(8,128)(2,1)} %param.13) | copy-start | bytes 2359300
  56.8 65.5 %all-to-all-start.1 = ((bf16[8,48,1120]{2,1,0:T(8,128)(2,1)}), bf16[8,48,1120]{2,1,0:T(8,128)(2,1)S(1)}, u32[]{:S(2)}, u32[]{:S(2)}) async-start(bf16[8,48,1120]{2,1,0:T(8,128)(2,1)} %reshape.305), calls=%async_computation.1 | async-start | bytes 1769472 | tf_op jit(solution)/shard_map/all_to_all | solution.py:74
  60.4 163.4 %all-gather.19.cloned.1.call-start = ((), (), s32[]{:S(2)}) async-start(), calls=%async_computation.19 | async-start | bytes 4423680 | tf_op jit(solution)/shard_map/all_gather | solution.py:75
  122.1 26.0 %copy-start.13 = (f32[256,64]{0,1:T(8,128)}, f32[256,64]{0,1:T(8,128)S(1)}, u32[]{:S(2)}) copy-start(f32[256,64]{0,1:T(8,128)S(1)} %get-tuple-element.43) | copy-start | bytes 196612
  122.3 40.0 %copy-start.22 = (f32[1536]{0:T(1024)}, f32[1536]{0:T(1024)S(1)}, u32[]{:S(2)}) copy-start(f32[1536]{0:T(1024)S(1)} %mul.327) | copy-start | bytes 18436
  123.3 167.3 %all-gather.13.cloned.1.call-start = ((), (), s32[]{:S(2)}) async-start(), calls=%async_computation.11 | async-start | bytes 7077888 | tf_op jit(solution)/shard_map/all_gather | solution.py:167
  164.6 172.9 %all-gather.15.cloned.1.call-start = ((), (), s32[]{:S(2)}) async-start(), calls=%async_computation.12 | async-start | bytes 4300800 | tf_op jit(solution)/shard_map/all_gather | solution.py:133
  165.1 238.6 %all-gather.21.cloned.1.call-start = ((), (), s32[]{:S(2)}) async-start(), calls=%async_computation.20 | async-start | bytes 7077888 | tf_op jit(solution)/shard_map/all_gather | solution.py:130
  165.7 354.4 %reduce-scatter.11.cloned.1.call-start = ((), (), s32[]{:S(2)}) async-start(), calls=%async_computation.14 | async-start | bytes 7077888 | tf_op jit(solution)/shard_map/reduce_scatter | solution.py:179
  423.6 15.0 %copy-start.5 = (bf16[2,2,4,2,48,1120]{5,4,3,1,2,0:T(8,128)(2,1)S(1)}, bf16[2,2,4,2,48,1120]{5,4,3,1,2,0:T(8,128)(2,1)}, u32[]{:S(2)}) copy-start(bf16[2,2,4,2,48,1120]{5,4,3,1,2,0:T(8,128)(2,1)} %copy.110) | copy-start | bytes 10321924
  451.5 139.1 %reduce-scatter.9.cloned.1.call-start = ((), (), s32[]{:S(2)}) async-start(), calls=%async_computation.13 | async-start | bytes 7077888 | tf_op jit(solution)/shard_map/reduce_scatter | solution.py:183
  465.9 178.9 %reduce-scatter.15.cloned.1.call-start = ((), (), s32[]{:S(2)}) async-start(), calls=%async_computation.16 | async-start | bytes 4423680 | tf_op jit(solution)/shard_map/reduce_scatter | solution.py:84
  485.1 209.9 %reduce-scatter.17.cloned.1.call-start = ((), (), s32[]{:S(2)}) async-start(), calls=%async_computation.17 | async-start | bytes 4423680 | tf_op jit(solution)/shard_map/reduce_scatter | solution.py:84
  503.8 240.7 %reduce-scatter.19.cloned.1.call-start = ((), (), s32[]{:S(2)}) async-start(), calls=%async_computation.21 | async-start | bytes 4300800
  504.7 15.4 %copy-start.23 = (f32[1536]{0:T(1024)S(1)}, f32[1536]{0:T(1024)}, u32[]{:S(2)}) copy-start(f32[1536]{0:T(1024)} %copy-done.22) | copy-start | bytes 18436
  504.7 15.4 %copy-start.30 = (f32[256]{0:T(256)S(1)}, f32[256]{0:T(256)}, u32[]{:S(2)}) copy-start(f32[256]{0:T(256)} %copy-done.29) | copy-start | bytes 3076
  516.8 377.8 %reduce-scatter.13.cloned.1.call-start = ((), (), s32[]{:S(2)}) async-start(), calls=%async_computation.15 | async-start | bytes 11354112 | tf_op jit(solution)/shard_map/reduce_scatter | solution.py:224
  606.8 13.8 %collective-permute-start = (bf16[256,512]{0,1:T(8,128)(2,1)S(1)}, bf16[256,512]{0,1:T(8,128)(2,1)S(1)}, u32[]{:S(2)}, u32[]{:S(2)}) collective-permute-start(bf16[256,512]{0,1:T(8,128)(2,1)S(1)} %fusion.69), channel_id=1, source_target_pairs={{0,16},{16,0},{1,17},{17,1},{2,18},{18,2},{3,19},{19,3},{4,20},{20... | collective-permute-start | bytes 786440 | tf_op jit(solution)/shard_map/ppermute | solution.py:218
  644.8 50.2 %all-to-all-start.2 = ((bf16[8,48,1120]{2,1,0:T(8,128)(2,1)}), bf16[8,48,1120]{2,1,0:T(8,128)(2,1)}, u32[]{:S(2)}, u32[]{:S(2)}) async-start(bf16[8,48,1120]{2,1,0:T(8,128)(2,1)} %reduce-scatter.15.cloned.1.call-done), calls=%async_computation.6 | async-start | bytes 1769472 | tf_op jit(solution)/shard_map/all_to_all | solution.py:85
  695.0 65.6 %all-to-all-start.3 = ((bf16[8,48,1120]{2,1,0:T(8,128)(2,1)}), bf16[8,48,1120]{2,1,0:T(8,128)(2,1)}, u32[]{:S(2)}, u32[]{:S(2)}) async-start(bf16[8,48,1120]{2,1,0:T(8,128)(2,1)} %reduce-scatter.17.cloned.1.call-done), calls=%async_computation.8 | async-start | bytes 1769472 | tf_op jit(solution)/shard_map/all_to_all | solution.py:85
  (36 other events, 174.8 us)
Sparse Core Ops, SparseCore 0:
  11.5 109.6 all-gather.10
  123.0 50.9 all-gather.16
  176.5 47.2 all-gather.18
  225.8 64.7 all-gather.12
  292.3 45.0 all-gather.14
  338.9 64.7 all-gather.20
  451.6 68.4 reduce-scatter.10
  522.4 68.1 reduce-scatter.8
  593.7 51.1 reduce-scatter.14
  647.8 47.2 reduce-scatter.16
  698.1 46.3 reduce-scatter.18
  750.3 144.2 reduce-scatter.12

commit v2 on v1

--- a/solution.py
+++ b/solution.py
@@ -1,6 +1,8 @@
 import jax
 import jax.numpy as jnp
 from jax import lax
+from jax.experimental import pallas as pl
+from jax.experimental.pallas import tpu as pltpu
 from jax.sharding import Mesh, PartitionSpec as P
 
 HD = 128
@@ -55,6 +57,277 @@
     return (grad_gain, grad_x)
 
 
+class Wires:
+    def __init__(self, sems):
+        self.sems = sems
+        self.used = 0
+        self.started = []
+
+    def send(self, src, dst, recv_sem, device, cond=None):
+        copy = pltpu.make_async_remote_copy(
+            src_ref=src,
+            dst_ref=dst,
+            send_sem=self.sems.at[self.used],
+            recv_sem=recv_sem,
+            device_id=device,
+            device_id_type=pl.DeviceIdType.MESH,
+        )
+        self.used += 1
+        if cond is None:
+            copy.start()
+        else:
+            pl.when(cond)(copy.start)
+        self.started.append((copy, cond))
+
+    def arrived(self, dst, recv_sem, device):
+        pltpu.make_async_remote_copy(
+            src_ref=dst,
+            dst_ref=dst,
+            send_sem=self.sems.at[0],
+            recv_sem=recv_sem,
+            device_id=device,
+            device_id_type=pl.DeviceIdType.MESH,
+        ).wait_recv()
+
+    def finish(self):
+        for copy, cond in self.started:
+            if cond is None:
+                copy.wait_send()
+            else:
+                pl.when(cond)(copy.wait_send)
+
+
+def line_order(z, k):
+    if k == 0:
+        return z + 1 - 2 * (z % 2)
+    if k == 1:
+        return 2 - z // 2
+    return 3 - 3 * (z // 2)
+
+
+def greet(peers):
+    barrier = pltpu.get_barrier_semaphore()
+    for peer in peers:
+        pl.semaphore_signal(
+            barrier, inc=1, device_id=peer, device_id_type=pl.DeviceIdType.MESH
+        )
+    pl.semaphore_wait(barrier, len(peers))
+
+
+def place():
+    return tuple(lax.axis_index(name) for name in ALL)
+
+
+def line_peers(z, c):
+    peers = [{"c": 1 - c}]
+    for k in range(NZ - 1):
+        peers.append({"z": (z + k + 1) % NZ})
+    return peers
+
+
+class LineGather:
+    def __init__(self, wires, own, out, recv, z, c):
+        self.wires, self.own, self.out, self.recv, self.z, self.c = wires, own, out, recv, z, c
+
+    def begin(self):
+        w, z, c = self.wires, self.z, self.c
+        dst, sem = self.out.at[z, c], self.recv.at[z, c]
+        w.send(self.own, dst, sem, {"z": jnp.minimum(z + 1, NZ - 1)}, z < NZ - 1)
+        w.send(self.own, dst, sem, {"z": jnp.maximum(z - 1, 0)}, z > 0)
+        w.send(self.own, dst, sem, {"c": 1 - c})
+
+    def event(self, k):
+        w, z, c = self.wires, self.z, self.c
+        zq = line_order(z, k)
+        slot, sem = self.out.at[zq, c], self.recv.at[zq, c]
+        w.arrived(slot, sem, {"c": 1 - c})
+        onward = jnp.where(zq < z, jnp.minimum(z + 1, NZ - 1), jnp.maximum(z - 1, 0))
+        w.send(slot, slot, sem, {"z": onward}, (z > 0) & (z < NZ - 1))
+        w.send(slot, slot, sem, {"c": 1 - c})
+
+    def sibling(self, zq):
+        w, c = self.wires, self.c
+        w.arrived(self.out.at[zq, 1 - c], self.recv.at[zq, 1 - c], {"c": 1 - c})
+
+
+def token_gather_kernel(own, out, send_sems, local_sem, recv):
+    y, z, x, c = place()
+    greet(line_peers(z, c))
+    keep = pltpu.make_async_copy(own, out.at[z, c], local_sem)
+    keep.start()
+    wires = Wires(send_sems)
+    line = LineGather(wires, own, out, recv, z, c)
+    line.begin()
+    for k in range(NZ - 1):
+        line.event(k)
+    for zq in range(NZ):
+        line.sibling(zq)
+    wires.finish()
+    keep.wait()
+
+
+def token_gather(own, collective_id):
+    shape = (NZ, NC) + own.shape
+    out = pl.pallas_call(
+        token_gather_kernel,
+        name="token_gather",
+        out_shape=jax.ShapeDtypeStruct(shape, own.dtype),
+        in_specs=[pl.BlockSpec(memory_space=pl.ANY)],
+        out_specs=pl.BlockSpec(memory_space=pl.ANY),
+        scratch_shapes=[
+            pltpu.SemaphoreType.DMA((9,)),
+            pltpu.SemaphoreType.DMA,
+            pltpu.SemaphoreType.DMA((NZ, NC)),
+        ],
+        compiler_params=pltpu.CompilerParams(
+            collective_id=collective_id, has_side_effects=True
+        ),
+    )(own)
+    return out.reshape(-1, own.shape[1])
+
+
+def weight_gather_kernel(
+    nx, a, gu, d, tok, ao, guo, do, co, send_sems, local_sems, ra, rt, rw, rd, rc
+):
+    y, z, x, c = place()
+    sib = {"c": 1 - c}
+    ypeer = {"y": 1 - y}
+    xpeers = [(x + i + 1) % nx for i in range(nx - 1)]
+    planes = [{"x": xp} for xp in xpeers] + [ypeer]
+    cross = [{"z": (z + k + 1) % NZ, "c": 1 - c} for k in range(NZ - 1)]
+    greet(line_peers(z, c) + cross + planes)
+    locals_ = [
+        pltpu.make_async_copy(a, ao.at[y, z, x, c], local_sems.at[0]),
+        pltpu.make_async_copy(gu.at[z, c], guo.at[:, y, z, x, c], local_sems.at[1]),
+        pltpu.make_async_copy(d, do.at[y, x], local_sems.at[2]),
+        pltpu.make_async_copy(tok, co.at[z, c], local_sems.at[3]),
+    ]
+    for copy in locals_:
+        copy.start()
+    wires = Wires(send_sems)
+
+    def both_ways(src, dst, sem):
+        for peer in planes:
+            wires.send(src, dst, sem, peer)
+
+    own_slot, own_sem = ao.at[y, z, x, c], ra.at[y, z, x, c]
+    wires.send(a, own_slot, own_sem, {"z": jnp.minimum(z + 1, NZ - 1)}, z < NZ - 1)
+    wires.send(a, own_slot, own_sem, {"z": jnp.maximum(z - 1, 0)}, z > 0)
+    both_ways(a, own_slot, own_sem)
+    wires.send(a, own_slot, own_sem, sib)
+    for k in range(NZ - 1):
+        zq = line_order(z, k)
+        slot, sem = ao.at[y, zq, x, c], ra.at[y, zq, x, c]
+        wires.arrived(slot, sem, sib)
+        onward = jnp.where(zq < z, jnp.minimum(z + 1, NZ - 1), jnp.maximum(z - 1, 0))
+        wires.send(slot, slot, sem, {"z": onward}, (z > 0) & (z < NZ - 1))
+        both_ways(slot, slot, sem)
+        wires.send(slot, slot, sem, sib)
+
+    for k in range(NZ * NC - 1):
+        step = k + 1
+        zp, cp = (z + step // NC) % NZ, (c + step) % NC
+        wires.send(
+            gu.at[zp, cp], guo.at[:, y, z, x, c], rt.at[z, c], {"z": zp, "c": cp}
+        )
+    line = LineGather(wires, tok, co, rc, z, c)
+    line.begin()
+    half = d.shape[1] // 2
+    parts = [pl.ds(0, half), pl.ds(half, half)]
+    for h in range(2):
+        both_ways(d.at[:, parts[h]], do.at[y, x, :, parts[h]], rd.at[h, y, x])
+
+    def relay_attn(yq, xq, zq, peers):
+        slot, sem = ao.at[yq, zq, xq, c], ra.at[yq, zq, xq, c]
+        wires.arrived(slot, sem, sib)
+        for peer in peers:
+            wires.send(slot, slot, sem, peer)
+        wires.send(slot, slot, sem, sib)
+
+    for zq in range(NZ):
+        for xp in xpeers:
+            relay_attn(y, xp, zq, [ypeer] if zq < NZ // 2 else [])
+        relay_attn(1 - y, x, zq, planes[:-1] if zq >= NZ // 2 else [])
+
+    for k in range(NZ * NC - 1):
+        step = k + 1
+        zp, cp = (z + step // NC) % NZ, (c + step) % NC
+        wires.arrived(guo.at[:, y, zp, x, cp], rt.at[zp, cp], sib)
+    locals_[1].wait()
+    for m in range(2):
+        plane = guo.at[m, y, :, x]
+        both_ways(plane, plane, rw.at[m, y, x])
+    line.event(0)
+
+    def relay(ref, sem, peers):
+        wires.arrived(ref, sem, sib)
+        for peer in peers:
+            wires.send(ref, ref, sem, peer)
+
+    for xp in xpeers:
+        relay(do.at[y, xp, :, parts[0]], rd.at[0, y, xp], [ypeer])
+        relay(do.at[y, xp, :, parts[1]], rd.at[1, y, xp], [])
+    relay(do.at[1 - y, x, :, parts[1]], rd.at[1, 1 - y, x], planes[:-1])
+    relay(do.at[1 - y, x, :, parts[0]], rd.at[0, 1 - y, x], [])
+    for xp in xpeers:
+        for zq in range(NZ):
+            relay_attn(1 - y, xp, zq, [])
+    line.event(1)
+    for xp in xpeers:
+        relay(guo.at[0, y, :, xp], rw.at[0, y, xp], [ypeer])
+    relay(guo.at[1, 1 - y, :, x], rw.at[1, 1 - y, x], planes[:-1])
+    line.event(2)
+    for xp in xpeers:
+        relay(guo.at[1, y, :, xp], rw.at[1, y, xp], [])
+    relay(guo.at[0, 1 - y, :, x], rw.at[0, 1 - y, x], [])
+    for xp in xpeers:
+        for h in range(2):
+            relay(do.at[1 - y, xp, :, parts[h]], rd.at[h, 1 - y, xp], [])
+            relay(guo.at[h, 1 - y, :, xp], rw.at[h, 1 - y, xp], [])
+    for zq in range(NZ):
+        line.sibling(zq)
+    for yq in range(2):
+        for zq in range(NZ):
+            for xq in range(nx):
+                wires.arrived(ao.at[yq, zq, xq, 1 - c], ra.at[yq, zq, xq, 1 - c], sib)
+    wires.finish()
+    for i in (0, 2, 3):
+        locals_[i].wait()
+
+
+def weight_gather(ny, nx, a, gu, d, tok, collective_id):
+    sends = 3 + (nx + 1) + 3 * (nx + 2)
+    sends += 7 + 9 + 2 * nx
+    sends += 4 * nx + 2 * (nx - 1) + 2 * (nx - 1)
+    sends += 2 * nx + 2 * (nx - 1) + 4 * (nx - 1) + 2 * (nx - 1)
+    hbm = pl.BlockSpec(memory_space=pl.ANY)
+    grid = (ny, NZ, nx, NC)
+    return pl.pallas_call(
+        lambda *refs: weight_gather_kernel(nx, *refs),
+        name="weight_gather",
+        out_shape=(
+            jax.ShapeDtypeStruct(grid + a.shape, BF16),
+            jax.ShapeDtypeStruct((2,) + grid + gu.shape[3:], BF16),
+            jax.ShapeDtypeStruct((ny, nx) + d.shape, BF16),
+            jax.ShapeDtypeStruct((NZ, NC) + tok.shape, BF16),
+        ),
+        in_specs=[hbm] * 4,
+        out_specs=(hbm,) * 4,
+        scratch_shapes=[
+            pltpu.SemaphoreType.DMA((sends + 16,)),
+            pltpu.SemaphoreType.DMA((4,)),
+            pltpu.SemaphoreType.DMA(grid),
+            pltpu.SemaphoreType.DMA((NZ, NC)),
+            pltpu.SemaphoreType.DMA((2, ny, nx)),
+            pltpu.SemaphoreType.DMA((2, ny, nx)),
+            pltpu.SemaphoreType.DMA((NZ, NC)),
+        ],
+        compiler_params=pltpu.CompilerParams(
+            collective_id=collective_id, has_side_effects=True
+        ),
+    )(a, gu, d, tok)
+
+
 def make_body(ny, nx):
     def spread_columns(shard):
         rows, cols = shard.shape
@@ -67,14 +340,6 @@
         fs = width // (ny * nx)
         view = blocks.reshape(NZ, NC, rows, ny, nx, fs)
         return view.transpose(2, 3, 0, 4, 1, 5).reshape(rows, -1)
-
-    def gather_columns(shard):
-        blocks = spread_columns(shard)
-        rows, width = blocks.shape[1:]
-        mine = lax.all_to_all(blocks, TP, split_axis=0, concat_axis=0, tiled=True)
-        full = lax.all_gather(mine, DP, axis=0, tiled=False)
-        view = full.reshape(ny, nx, NZ, NC, rows, width).transpose(0, 2, 1, 3, 4, 5)
-        return view.reshape(-1, width)
 
     def scatter_columns(grad):
         width = grad.shape[1]
@@ -114,23 +379,41 @@
         q_heads = query_width // HD
         group = q_heads // kv_heads
 
-        packed = jnp.concatenate([q_weight, k_weight, v_weight, o_weight], axis=1)
-        full = lax.all_gather(packed, ALL, axis=0, tiled=True)
-        qkv_width = query_width + 2 * key_width
-        full_qkv = full[:, :qkv_width]
-        full_out = full[:, qkv_width:]
-        small = jnp.concatenate([attn_gain, qkv_bias, mlp_gain])[None]
-        small_all = lax.all_gather(small, ALL, axis=0, tiled=True).astype(F32)
         g_rows = attn_gain.shape[0]
         b_rows = qkv_bias.shape[0]
-        gain_one = small_all[:, :g_rows].reshape(-1)
-        bias = small_all[:, g_rows : g_rows + b_rows].reshape(-1)
-        gain_two = small_all[:, g_rows + b_rows :].reshape(-1)
-
-        grad_out_all = lax.all_gather(grad_out, TP, axis=0, tiled=True)
-        full_gate = gather_columns(gate_weight)
-        full_up = gather_columns(up_weight)
-        full_down = lax.all_gather(down_weight, DP, axis=0, tiled=True)
+        qkv_width = query_width + 2 * key_width
+        extra = jnp.concatenate(
+            [
+                attn_gain[:, None],
+                mlp_gain[:, None],
+                jnp.broadcast_to(qkv_bias[None], (g_rows, b_rows)),
+                jnp.zeros((g_rows, HD - 2 - b_rows), BF16),
+            ],
+            axis=1,
+        )
+        packed = jnp.concatenate([q_weight, k_weight, v_weight, o_weight, extra], axis=1)
+        columns = jnp.stack([spread_columns(gate_weight), spread_columns(up_weight)], axis=1)
+        attn_all, columns_all, down_all, grad_out_all = weight_gather(
+            ny,
+            nx,
+            packed,
+            columns.reshape((NZ, NC) + columns.shape[1:]),
+            down_weight,
+            grad_out,
+            0,
+        )
+        full = attn_all.reshape(-1, packed.shape[1])
+        full_qkv = full[:, :qkv_width]
+        full_out = full[:, qkv_width : qkv_width + query_width]
+        tail = attn_all[..., qkv_width + query_width :].astype(F32)
+        gain_one = tail[..., 0].reshape(-1)
+        gain_two = tail[..., 1].reshape(-1)
+        bias = tail[..., 0, 2 : 2 + b_rows].reshape(-1)
+        width = columns.shape[-1]
+        full_gate = columns_all[0].reshape(-1, width)
+        full_up = columns_all[1].reshape(-1, width)
+        full_down = down_all.reshape(width, -1)
+        grad_out_all = grad_out_all.reshape(-1, grad_out.shape[1])
 
         rescale_one = lax.rsqrt(jnp.mean(hidden_in * hidden_in, axis=-1, keepdims=True) + EPS)
         normed_one = hidden_in * rescale_one
@@ -164,7 +447,7 @@
         rescale_two = lax.rsqrt(jnp.mean(middle * middle, axis=-1, keepdims=True) + EPS)
         normed_two = middle * rescale_two
         input_two = (normed_two * gain_two).astype(BF16)
-        input_all = lax.all_gather(input_two, TP, axis=0, tiled=True)
+        input_all = token_gather(input_two, 1)
         gate_pre = dot(input_all, full_gate)
         up_pre = dot(input_all, full_up)
         gate_sig = jax.nn.sigmoid(gate_pre)
@@ -233,7 +516,7 @@
         grad_input_one = dot_nt(grad_qkv, full_qkv)
         grad_gain_one, grad_first = norm_back(grad_input_one, normed_one, rescale_one, gain_one)
         grad_total = grad_mid + grad_first
-        shards = small_all.shape[0]
+        shards = ny * NZ * nx * NC
         small_grads = jnp.concatenate(
             [
                 grad_gain_one.reshape(shards, -1),

time: 914 us -> 804 us (0.88)
  Pallas kernels: 0 us -> 212 us
  waiting for transfers between devices: 461 us -> 253 us
  blocking collectives: 153 us -> 48.5 us
    pallas_call x0 -> x2, Pallas kernels: none -> 212 us  [the longest x1 155 us: weight_gather(): pl.pallas_call(lambda *refs: weight_gather_kernel(nx, *refs), name='weigh...]
    all_gather x6 -> x0, waiting for transfers between devices: 209 us -> none  [the longest x1 66.3 us: body(): grad_out_all = lax.all_gather(grad_out, TP, axis=0, tiled=True)]
    unnamed x2 -> x1, blocking collectives: 101 us -> 40.9 us
    all_to_all x1 -> x0, blocking collectives: 36.7 us -> none  [gather_columns(): mine = lax.all_to_all(blocks, TP, split_axis=0, concat_axis=0, tiled=True)]
    unnamed x13 -> x7, waiting for transfers between devices: 46.1 us -> 44.8 us
  transfers between devices with their start and end apart: 16 -> 9, of which waited for: 12 -> 7; matrix products, arithmetic and copies ran while one was open for 22% -> 17% of each run, Pallas kernels for 0% -> 0%
where the time goes in v2:
time: 804 us; the launch traced here: 797 us
  waiting for transfers between devices  253 us (31%)
  Pallas kernels  212 us (26%)
  matrix products  158 us (20%)
  local copies, waits for them, and re-layouts  70.8 us (9%)
  blocking collectives  48.5 us (6%)
  other arithmetic  28.2 us (4%)
  between operations  15.5 us (2%)
  starting transfers between devices  11.3 us (1%)
    pallas_call x1, Pallas kernels, weight_gather(): pl.pallas_call(lambda *refs: weight_gather_kernel(nx, *refs), name='weigh...  155 us
    reduce_scatter x1, waiting for transfers between devices, body(): out_sum = lax.psum_scatter(out_part, TP, scatter_dimension=0, tiled=True)  68.7 us
    reduce_scatter x1, waiting for transfers between devices, body(): lax.psum_scatter(jnp.concatenate([dot_tn(input_one, grad_qkv), dot_tn(att...  66.8 us
    reduce_scatter x2, waiting for transfers between devices, scatter_columns(): part = lax.psum_scatter(view, DP, scatter_dimension=0, tiled=True)  60.2 us
    pallas_call x1, Pallas kernels, token_gather(): pl.pallas_call(token_gather_kernel, name='token_gather', out_shape=jax.Sh...  57.8 us
    dot_general x5, matrix products, dot_nt(): lax.dot_general(a, b, (((1,), (1,)), ((), ())), preferred_element_type=F32)  57.1 us
    unnamed x7, waiting for transfers between devices  44.8 us
    dot_general x5, matrix products, dot_tn(): lax.dot_general(a, b, (((0,), (0,)), ((), ())), preferred_element_type=F32)  43.5 us
  transfers between devices with their start and end apart: 9, of which 7 were waited for; matrix products, arithmetic and copies ran while one was open for 17% of the time, Pallas kernels for 0%

profile of v2, /device:TPU:0, one launch (start us, length us, event | category | flops | bytes accessed | tf_op | source)
XLA Modules:
  0.0 797.4 jit_solution(6193417072811522305)
XLA Ops:
  22.3 154.5 %weight_gather.1 = (bf16[2,4,2,2,48,3712]{5,4,3,2,1,0:T(8,128)(2,1)}, bf16[2,2,4,2,2,48,1120]{6,5,4,3,2,1,0:T(8,128)(2,1)}, bf16[2,2,280,1536]{3,2,1,0:T(8,128)(2,1)}, bf16[4,2,256,1536]{3,2,1,0:T(8,128)(2,1)}) custom-call(bf16[48,3712]{1,0:T(8,128)(2,1)} %concatenate.38.refs_0_, bf16[4,2,2,48,1120]{4,3,2,1,0:T(8,128)(2,1)} %pad_maximum_fusion.1.refs_1_, ...), custom_call_target="tpu_custom_call" | custom-call | tf_op jit(solution)/shard_map/weight_gather/pallas_call | solution.py:305
  186.9 7.6 all_gather.3
  212.3 57.8 %token_gather.1 = bf16[4,2,256,1536]{3,2,1,0:T(8,128)(2,1)} custom-call(bf16[256,1536]{1,0:T(8,128)(2,1)} %multiply_convert_fusion.3.own), custom_call_target="tpu_custom_call" | custom-call | tf_op jit(solution)/shard_map/token_gather/pallas_call | solution.py:171
  274.9 10.1 %fusion.84 = f32[2048,1120]{0,1:T(8,128)} fusion(bf16[2048,1536]{1,0:T(8,128)(2,1)S(1)} %bitcast.152, bf16[1536,1120]{1,0:T(8,128)(2,1)S(1)} %bitcast.160), kind=kOutput, calls=%fused_computation.139 | convolution fusion | flops 7046430720 | bytes 18907136 | tf_op jit(solution)/shard_map/dot_general | solution.py:42
  285.0 9.9 %fusion.83 = f32[2048,1120]{0,1:T(8,128)} fusion(bf16[2048,1536]{1,0:T(8,128)(2,1)S(1)} %bitcast.153, bf16[1536,1120]{1,0:T(8,128)(2,1)S(1)} %bitcast.162), kind=kOutput, calls=%fused_computation.138 | convolution fusion | flops 7046430720 | bytes 18907136 | tf_op jit(solution)/shard_map/dot_general | solution.py:42
  294.9 20.5 %multiply_convert_fusion = (bf16[2048,1120]{0,1:T(8,128)(2,1)}, bf16[2048,1120]{0,1:T(8,128)(2,1)}, bf16[2048,1120]{0,1:T(8,128)(2,1)}) fusion(f32[2048,1120]{0,1:T(8,128)} %fusion.83, f32[2048,1120]{0,1:T(8,128)} %fusion.84, bf16[2048,1536]{1,0:T(8,128)(2,1)} %bitcast.192, bf16[1120,1536]{1,0:T(8,128)(2,1)} %bitcast.194), kind=kOutput, calls=%fused_computation.3 | convolution fusion | flops 7080837120 | bytes 41844736 | tf_op jit(solution)/shard_map/dot_general | solution.py:46
  315.4 13.3 %fusion.85 = f32[2048,1536]{1,0:T(8,128)} fusion(bf16[2048,1120]{0,1:T(8,128)(2,1)} %get-tuple-element.27, bf16[1536,1120]{1,0:T(8,128)(2,1)S(1)} %bitcast.163), kind=kOutput, calls=%fused_computation.140 | convolution fusion | flops 7046430720 | bytes 20611072 | tf_op jit(solution)/shard_map/dot_general | solution.py:46
  328.7 12.9 %add_convert_fusion = bf16[2048,1536]{1,0:T(8,128)(2,1)} fusion(f32[2048,1536]{1,0:T(8,128)} %fusion.85, bf16[2048,1120]{0,1:T(8,128)(2,1)S(1)} %copy-done.39, bf16[1536,1120]{1,0:T(8,128)(2,1)S(1)} %bitcast.161), kind=kOutput, calls=%fused_computation.1 | convolution fusion | flops 7052722176 | bytes 26902528 | tf_op jit(solution)/shard_map/dot_general | solution.py:46
  343.6 12.5 %convolution_convert_fusion = bf16[2048,1536]{1,0:T(8,128)(2,1)} fusion(bf16[2048,1120]{0,1:T(8,128)(2,1)} %get-tuple-element.28, bf16[1120,1536]{1,0:T(8,128)(2,1)S(1)} %bitcast.195), kind=kOutput, calls=%fused_computation.8 | convolution fusion | flops 7049576448 | bytes 14319616 | tf_op jit(solution)/shard_map/dot_general | solution.py:42
  356.2 12.5 %convolution_convert_fusion.3 = bf16[1536,1120]{0,1:T(8,128)(2,1)} fusion(bf16[2048,1120]{0,1:T(8,128)(2,1)} %get-tuple-element.27, bf16[2048,1536]{1,0:T(8,128)(2,1)} %bitcast.150), kind=kOutput, calls=%fused_computation.11 | convolution fusion | flops 7048151040 | bytes 14319616 | tf_op jit(solution)/shard_map/dot_general | solution.py:50
  375.3 12.1 %convolution_convert_fusion.2 = bf16[1536,1120]{0,1:T(8,128)(2,1)} fusion(bf16[2048,1120]{0,1:T(8,128)(2,1)} %get-tuple-element.26, bf16[2048,1536]{1,0:T(8,128)(2,1)} %bitcast.151), kind=kOutput, calls=%fused_computation.10 | convolution fusion | flops 7048151040 | bytes 14319616 | tf_op jit(solution)/shard_map/dot_general | solution.py:50
  394.0 12.1 %convolution_convert_fusion.4 = bf16[1120,1536]{1,0:T(8,128)(2,1)} fusion(bf16[2048,1120]{0,1:T(8,128)(2,1)} %get-tuple-element.28, bf16[2048,1536]{1,0:T(8,128)(2,1)} %bitcast.193), kind=kOutput, calls=%fused_computation.12 | convolution fusion | flops 7048151040 | bytes 14319616 | tf_op jit(solution)/shard_map/dot_general | solution.py:50
  406.4 5.9 reduce-scatter.11.cloned.1.call-done
  414.1 68.7 %reduce-scatter.9.cloned.1.call-done = bf16[256,1536]{1,0:T(8,128)(2,1)} async-done(((bf16[2048,1536]{1,0:T(8,128)(2,1)}), bf16[256,1536]{1,0:T(8,128)(2,1)}) %reduce-scatter.9.cloned.1.call-update) | async-done | bytes 786448 | tf_op jit(solution)/shard_map/reduce_scatter | solution.py:466
  506.2 6.7 collective-permute-done
  517.4 5.1 pad_maximum_fusion
  522.5 14.6 %reduce-scatter.15.cloned.1.call-done = bf16[8,48,1120]{2,1,0:T(8,128)(2,1)} async-done(((bf16[32,48,1120]{2,1,0:T(8,128)(2,1)}), bf16[8,48,1120]{2,1,0:T(8,128)(2,1)}) %reduce-scatter.15.cloned.1.call-update) | async-done | bytes 860176 | tf_op jit(solution)/shard_map/reduce_scatter | solution.py:349
  541.7 45.6 %reduce-scatter.17.cloned.1.call-done = bf16[8,48,1120]{2,1,0:T(8,128)(2,1)} async-done(((bf16[32,48,1120]{2,1,0:T(8,128)(2,1)}), bf16[8,48,1120]{2,1,0:T(8,128)(2,1)}) %reduce-scatter.17.cloned.1.call-update) | async-done | bytes 860176 | tf_op jit(solution)/shard_map/reduce_scatter | solution.py:349
  591.9 44.7 %reduce-scatter.19.cloned.1.call-done = bf16[280,1536]{1,0:T(8,128)(2,1)} async-done(((bf16[1120,1536]{1,0:T(8,128)(2,1)}), bf16[280,1536]{1,0:T(8,128)(2,1)}) %reduce-scatter.19.cloned.1.call-update) | async-done | bytes 860176
  643.6 4.9 copy.130
  657.2 5.0 copy.133
  668.5 6.6 fusion.42
  675.3 40.9 %all-reduce = f32[32,160]{1,0:T(8,128)S(1)} all-reduce(f32[32,160]{1,0:T(8,128)S(1)} %pad_maximum_fusion.8), channel_id=4, replica_groups=mesh['y'=2,'z'=4,'x'=2,'c'=2] {'y','z','x','c'}, use_global_device_ids=true, to_apply=%region_12.13.clone | all-reduce | flops 5120 | bytes 40960
  720.1 66.8 %reduce-scatter.13.cloned.1.call-done = bf16[48,3584]{1,0:T(8,128)(2,1)} async-done(((bf16[1536,3584]{1,0:T(8,128)(2,1)}), bf16[48,3584]{1,0:T(8,128)(2,1)}) %reduce-scatter.13.cloned.1.call-update) | async-done | bytes 344080 | tf_op jit(solution)/shard_map/reduce_scatter | solution.py:507
  (201 shorter events, 130.6 us)
Async XLA Ops:
  7.2 405.2 %reduce-scatter.11.cloned.1.call-start = ((), (), s32[]{:S(2)}) async-start(), calls=%async_computation.9 | async-start | bytes 7077888 | tf_op jit(solution)/shard_map/reduce_scatter | solution.py:462
  13.3 6.4 copy-start.35
  13.3 6.5 copy-start.36
  21.4 157.6 %copy-start.2 = (bf16[1,256,1536]{2,1,0:T(8,128)(2,1)S(1)}, bf16[1,256,1536]{2,1,0:T(8,128)(2,1)}, u32[]{:S(2)}) copy-start(bf16[1,256,1536]{2,1,0:T(8,128)(2,1)} %param.13) | copy-start | bytes 2359300
  185.8 10.6 %copy-start.11 = (f32[256,64]{0,1:T(8,128)}, f32[256,64]{0,1:T(8,128)S(1)}, u32[]{:S(2)}) copy-start(f32[256,64]{0,1:T(8,128)S(1)} %get-tuple-element.53) | copy-start | bytes 196612
  185.9 10.5 %copy-start.9 = (f32[256,64]{1,0:T(8,128)}, f32[256,64]{1,0:T(8,128)S(1)}, u32[]{:S(2)}) copy-start(f32[256,64]{1,0:T(8,128)S(1)} %copy.108) | copy-start | bytes 196612
  210.8 59.2 %copy-start = (f32[256,1536]{1,0:T(8,128)}, f32[256,1536]{1,0:T(8,128)S(1)}, u32[]{:S(2)}) copy-start(f32[256,1536]{1,0:T(8,128)S(1)} %get-tuple-element.57) | copy-start | bytes 4718596
  210.9 59.2 %copy-start.29 = (f32[256]{0:T(256)}, f32[256]{0:T(256)S(1)}, u32[]{:S(2)}) copy-start(f32[256]{0:T(256)S(1)} %add_rsqrt_fusion) | copy-start | bytes 3076
  211.0 59.1 %copy-start.21 = (f32[1536]{0:T(1024)}, f32[1536]{0:T(1024)S(1)}, u32[]{:S(2)}) copy-start(f32[1536]{0:T(1024)S(1)} %mul.327) | copy-start | bytes 18436
  315.4 13.3 %copy-start.39 = (bf16[2048,1120]{0,1:T(8,128)(2,1)S(1)}, bf16[2048,1120]{0,1:T(8,128)(2,1)}, u32[]{:S(2)}) copy-start(bf16[2048,1120]{0,1:T(8,128)(2,1)} %get-tuple-element.26) | copy-start | bytes 13762564
  341.6 141.2 %reduce-scatter.9.cloned.1.call-start = ((), (), s32[]{:S(2)}) async-start(), calls=%async_computation.8 | async-start | bytes 7077888 | tf_op jit(solution)/shard_map/reduce_scatter | solution.py:466
  356.1 181.0 %reduce-scatter.15.cloned.1.call-start = ((), (), s32[]{:S(2)}) async-start(), calls=%async_computation.11 | async-start | bytes 4423680 | tf_op jit(solution)/shard_map/reduce_scatter | solution.py:349
  375.3 212.0 %reduce-scatter.17.cloned.1.call-start = ((), (), s32[]{:S(2)}) async-start(), calls=%async_computation.12 | async-start | bytes 4423680 | tf_op jit(solution)/shard_map/reduce_scatter | solution.py:349
  394.0 12.4 %copy-start.17 = (f32[256,64]{0,1:T(8,128)S(1)}, f32[256,64]{0,1:T(8,128)}, u32[]{:S(2)}) copy-start(f32[256,64]{0,1:T(8,128)} %get-tuple-element.51) | copy-start | bytes 196612
  394.0 242.7 %reduce-scatter.19.cloned.1.call-start = ((), (), s32[]{:S(2)}) async-start(), calls=%async_computation.13 | async-start | bytes 4300800
  406.1 6.3 copy-start.22
  406.1 6.3 copy-start.30
  406.1 380.8 %reduce-scatter.13.cloned.1.call-start = ((), (), s32[]{:S(2)}) async-start(), calls=%async_computation.10 | async-start | bytes 11354112 | tf_op jit(solution)/shard_map/reduce_scatter | solution.py:507
  499.1 13.8 %collective-permute-start = (bf16[256,512]{0,1:T(8,128)(2,1)S(1)}, bf16[256,512]{0,1:T(8,128)(2,1)S(1)}, u32[]{:S(2)}, u32[]{:S(2)}) collective-permute-start(bf16[256,512]{0,1:T(8,128)(2,1)S(1)} %fusion.66), channel_id=1, source_target_pairs={{0,16},{16,0},{1,17},{17,1},{2,18},{18,2},{3,19},{19,3},{4,20},{20... | collective-permute-start | bytes 786440 | tf_op jit(solution)/shard_map/ppermute | solution.py:501
  505.0 8.4 %copy-start.10 = (f32[256,64]{1,0:T(8,128)S(1)}, f32[256,64]{1,0:T(8,128)}, u32[]{:S(2)}) copy-start(f32[256,64]{1,0:T(8,128)} %copy-done.9) | copy-start | bytes 196612
  505.2 8.9 %copy-start.3 = (bf16[1,256,1536]{2,1,0:T(8,128)(2,1)S(1)}, bf16[1,256,1536]{2,1,0:T(8,128)(2,1)}, u32[]{:S(2)}) copy-start(bf16[1,256,1536]{2,1,0:T(8,128)(2,1)} %param.13) | copy-start | bytes 2359300
  505.2 8.9 %copy-start.24 = (f32[1536]{0:T(1024)S(1)}, f32[1536]{0:T(1024)}, u32[]{:S(2)}) copy-start(f32[1536]{0:T(1024)} %copy-done.23) | copy-start | bytes 18436
  537.1 50.2 %all-to-all-start = ((bf16[8,48,1120]{2,1,0:T(8,128)(2,1)}), bf16[8,48,1120]{2,1,0:T(8,128)(2,1)}, u32[]{:S(2)}, u32[]{:S(2)}) async-start(bf16[8,48,1120]{2,1,0:T(8,128)(2,1)} %reduce-scatter.15.cloned.1.call-done), calls=%async_computation.4 | async-start | bytes 1769472 | tf_op jit(solution)/shard_map/all_to_all | solution.py:350
  587.3 65.5 %all-to-all-start.1 = ((bf16[8,48,1120]{2,1,0:T(8,128)(2,1)}), bf16[8,48,1120]{2,1,0:T(8,128)(2,1)}, u32[]{:S(2)}, u32[]{:S(2)}) async-start(bf16[8,48,1120]{2,1,0:T(8,128)(2,1)} %reduce-scatter.17.cloned.1.call-done), calls=%async_computation.6 | async-start | bytes 1769472 | tf_op jit(solution)/shard_map/all_to_all | solution.py:350
  (29 other events, 109.4 us)
Sparse Core Ops, SparseCore 0:
  341.8 70.5 reduce-scatter.10
  414.7 68.1 reduce-scatter.8
  486.0 51.1 reduce-scatter.14
  540.1 47.2 reduce-scatter.16
  590.2 46.3 reduce-scatter.18
  642.5 144.3 reduce-scatter.12

commit v3 on v2

--- a/solution.py
+++ b/solution.py
@@ -150,44 +150,17 @@
         w.arrived(self.out.at[zq, 1 - c], self.recv.at[zq, 1 - c], {"c": 1 - c})
 
 
-def token_gather_kernel(own, out, send_sems, local_sem, recv):
-    y, z, x, c = place()
-    greet(line_peers(z, c))
-    keep = pltpu.make_async_copy(own, out.at[z, c], local_sem)
-    keep.start()
-    wires = Wires(send_sems)
-    line = LineGather(wires, own, out, recv, z, c)
-    line.begin()
-    for k in range(NZ - 1):
-        line.event(k)
-    for zq in range(NZ):
-        line.sibling(zq)
-    wires.finish()
-    keep.wait()
-
-
-def token_gather(own, collective_id):
-    shape = (NZ, NC) + own.shape
-    out = pl.pallas_call(
-        token_gather_kernel,
-        name="token_gather",
-        out_shape=jax.ShapeDtypeStruct(shape, own.dtype),
-        in_specs=[pl.BlockSpec(memory_space=pl.ANY)],
-        out_specs=pl.BlockSpec(memory_space=pl.ANY),
-        scratch_shapes=[
-            pltpu.SemaphoreType.DMA((9,)),
-            pltpu.SemaphoreType.DMA,
-            pltpu.SemaphoreType.DMA((NZ, NC)),
-        ],
-        compiler_params=pltpu.CompilerParams(
-            collective_id=collective_id, has_side_effects=True
-        ),
-    )(own)
-    return out.reshape(-1, own.shape[1])
+def segments(nx, fs):
+    for yq in range(2):
+        for zq in range(NZ):
+            for xq in range(nx):
+                for cq in range(NC):
+                    first = (((yq * NZ + zq) * nx + xq) * NC + cq) * fs
+                    yield zq, cq, (yq * nx + xq) * fs, first
 
 
 def weight_gather_kernel(
-    nx, a, gu, d, tok, ao, guo, do, co, send_sems, local_sems, ra, rt, rw, rd, rc
+    nx, a, g, u, d, tok, ao, guo, do, co, gu, send_sems, local_sems, ra, rt, rw, rd, rc
 ):
     y, z, x, c = place()
     sib = {"c": 1 - c}
@@ -198,10 +171,10 @@
     greet(line_peers(z, c) + cross + planes)
     locals_ = [
         pltpu.make_async_copy(a, ao.at[y, z, x, c], local_sems.at[0]),
-        pltpu.make_async_copy(gu.at[z, c], guo.at[:, y, z, x, c], local_sems.at[1]),
-        pltpu.make_async_copy(d, do.at[y, x], local_sems.at[2]),
-        pltpu.make_async_copy(tok, co.at[z, c], local_sems.at[3]),
+        pltpu.make_async_copy(d, do.at[y, x], local_sems.at[1]),
+        pltpu.make_async_copy(tok, co.at[z, c], local_sems.at[2]),
     ]
+    keep = pltpu.make_async_copy(gu.at[z, c], guo.at[:, y, z, x, c], local_sems.at[3])
     for copy in locals_:
         copy.start()
     wires = Wires(send_sems)
@@ -215,6 +188,11 @@
     wires.send(a, own_slot, own_sem, {"z": jnp.maximum(z - 1, 0)}, z > 0)
     both_ways(a, own_slot, own_sem)
     wires.send(a, own_slot, own_sem, sib)
+    fs = gu.shape[-1] // (2 * nx)
+    for m, shard in enumerate((g, u)):
+        for zq, cq, run, first in segments(nx, fs):
+            gu[zq, cq, m, :, run : run + fs] = shard[:, first : first + fs]
+    keep.start()
     for k in range(NZ - 1):
         zq = line_order(z, k)
         slot, sem = ao.at[y, zq, x, c], ra.at[y, zq, x, c]
@@ -253,7 +231,7 @@
         step = k + 1
         zp, cp = (z + step // NC) % NZ, (c + step) % NC
         wires.arrived(guo.at[:, y, zp, x, cp], rt.at[zp, cp], sib)
-    locals_[1].wait()
+    keep.wait()
     for m in range(2):
         plane = guo.at[m, y, :, x]
         both_ways(plane, plane, rw.at[m, y, x])
@@ -291,29 +269,32 @@
             for xq in range(nx):
                 wires.arrived(ao.at[yq, zq, xq, 1 - c], ra.at[yq, zq, xq, 1 - c], sib)
     wires.finish()
-    for i in (0, 2, 3):
-        locals_[i].wait()
-
-
-def weight_gather(ny, nx, a, gu, d, tok, collective_id):
+    for copy in locals_:
+        copy.wait()
+
+
+def weight_gather(ny, nx, a, g, u, d, tok, collective_id):
     sends = 3 + (nx + 1) + 3 * (nx + 2)
     sends += 7 + 9 + 2 * nx
     sends += 4 * nx + 2 * (nx - 1) + 2 * (nx - 1)
     sends += 2 * nx + 2 * (nx - 1) + 4 * (nx - 1) + 2 * (nx - 1)
     hbm = pl.BlockSpec(memory_space=pl.ANY)
+    vmem = pl.BlockSpec(memory_space=pltpu.VMEM)
     grid = (ny, NZ, nx, NC)
+    block = g.shape[:1] + (g.shape[1] // (NZ * NC),)
     return pl.pallas_call(
         lambda *refs: weight_gather_kernel(nx, *refs),
         name="weight_gather",
         out_shape=(
             jax.ShapeDtypeStruct(grid + a.shape, BF16),
-            jax.ShapeDtypeStruct((2,) + grid + gu.shape[3:], BF16),
+            jax.ShapeDtypeStruct((2,) + grid + block, BF16),
             jax.ShapeDtypeStruct((ny, nx) + d.shape, BF16),
             jax.ShapeDtypeStruct((NZ, NC) + tok.shape, BF16),
         ),
-        in_specs=[hbm] * 4,
+        in_specs=[hbm, vmem, vmem, hbm, hbm],
         out_specs=(hbm,) * 4,
         scratch_shapes=[
+            pltpu.VMEM((NZ, NC, 2) + block, BF16),
             pltpu.SemaphoreType.DMA((sends + 16,)),
             pltpu.SemaphoreType.DMA((4,)),
             pltpu.SemaphoreType.DMA(grid),
@@ -325,31 +306,670 @@
         compiler_params=pltpu.CompilerParams(
             collective_id=collective_id, has_side_effects=True
         ),
-    )(a, gu, d, tok)
+    )(a, g, u, d, tok)
+
+
+def total_into(dst, refs):
+    flat = len(dst.shape) == 2
+
+    def entry(i, carry):
+        here = (slice(None), pl.ds(pl.multiple_of(i * 128, 128), 128)) if flat else i
+        total = refs[0][here].astype(F32)
+        for ref in refs[1:]:
+            total = total + ref[here].astype(F32)
+        dst[here] = total.astype(dst.dtype)
+        return carry
+
+    lax.fori_loop(0, dst.shape[1] // 128 if flat else dst.shape[0], entry, 0)
+
+
+class PlaneScatter:
+    def __init__(self, wires, src, first, second, bufs, loaded=False):
+        self.wires, self.src = wires, src
+        self.name_a, self.size_a, self.a = first
+        self.name_b, self.size_b, self.b = second
+        self.r1, self.own, self.r2, self.s1, self.sl, self.s2 = bufs
+        self.loaded = loaded
+
+    def mine(self, b):
+        return self.src(self.a, b) if self.loaded else self.own.at[b]
+
+    def order(self):
+        return [(self.b + i + 1) % self.size_b for i in range(self.size_b)]
+
+    def begin(self):
+        for b in self.order():
+            for i in range(self.size_a - 1):
+                peer, j = (self.a + i + 1) % self.size_a, self.size_a - 2 - i
+                self.wires.send(
+                    self.src(peer, b), self.r1.at[j, b], self.s1.at[j, b], {self.name_a: peer}
+                )
+            if not self.loaded:
+                self.load(b).start()
+
+    def load(self, b):
+        return pltpu.make_async_copy(self.src(self.a, b), self.own.at[b], self.sl.at[b])
+
+    def gathered(self, b):
+        if not self.loaded:
+            self.load(b).wait()
+        for j in range(self.size_a - 1):
+            self.wires.arrived(self.r1.at[j, b], self.s1.at[j, b], {self.name_a: self.a})
+        return [self.mine(b)] + [self.r1.at[j, b] for j in range(self.size_a - 1)]
+
+    def relay(self):
+        for i, b in enumerate(self.order()[:-1]):
+            j = self.size_b - 2 - i
+            total_into(self.mine(b), self.gathered(b))
+            self.wires.send(self.mine(b), self.r2.at[j], self.s2.at[j], {self.name_b: b})
+
+    def finish(self, dst):
+        refs = self.gathered(self.b)
+        for j in range(self.size_b - 1):
+            self.wires.arrived(self.r2.at[j], self.s2.at[j], {self.name_b: self.b})
+            refs.append(self.r2.at[j])
+        total_into(dst, refs)
+
+
+def plane_scratch(slot, size_a, size_b, loaded=False):
+    own = (1,) * (1 + len(slot)) if loaded else (size_b,) + slot
+    return [
+        pltpu.VMEM((size_a - 1, size_b) + slot, BF16),
+        pltpu.VMEM(own, BF16),
+        pltpu.VMEM((size_b - 1,) + slot, BF16),
+        pltpu.SemaphoreType.DMA((size_a - 1, size_b)),
+        pltpu.SemaphoreType.DMA((size_b,)),
+        pltpu.SemaphoreType.DMA((size_b - 1,)),
+    ]
+
+
+class LineScatter:
+    def __init__(self, wires, part, bufs, z, c):
+        self.wires, self.part, self.z, self.c = wires, part, z, c
+        self.own, self.sib, self.left, self.right = bufs[:4]
+        self.s_own, self.s_sib, self.s_left, self.s_right = bufs[4:]
+
+    def order(self):
+        return [line_order(self.z, k) for k in (2, 1, 0)] + [self.z]
+
+    def load(self, zq):
+        return pltpu.make_async_copy(
+            self.part.at[zq, self.c], self.own.at[zq], self.s_own.at[zq]
+        )
+
+    def begin(self):
+        for zq in self.order():
+            self.wires.send(
+                self.part.at[zq, 1 - self.c],
+                self.sib.at[zq],
+                self.s_sib.at[zq],
+                {"c": 1 - self.c},
+            )
+            self.load(zq).start()
+
+    def ready(self, zq):
+        self.load(zq).wait()
+        self.wires.arrived(self.sib.at[zq], self.s_sib.at[zq], {"c": 1 - self.c})
+
+    def hop(self, k):
+        z = self.z
+        for sign, buf, sems in ((1, self.left, self.s_left), (-1, self.right, self.s_right)):
+            target = z + sign * k
+            inside = (target < NZ) if sign > 0 else (target >= 0)
+            behind = (z > 0) if sign > 0 else (z < NZ - 1)
+            target = jnp.clip(target, 0, NZ - 1)
+            own, sib = self.own.at[target], self.sib.at[target]
+
+            @pl.when(inside)
+            def _():
+                self.ready(target)
+
+            if k < NZ - 1:
+
+                @pl.when(inside & behind)
+                def _():
+                    self.wires.arrived(buf.at[k], sems.at[k], {"z": z})
+                    total_into(own, [own, sib, buf.at[k]])
+
+                @pl.when(inside & jnp.logical_not(behind))
+                def _():
+                    total_into(own, [own, sib])
+
+            else:
+
+                @pl.when(inside)
+                def _():
+                    total_into(own, [own, sib])
+
+            onward = jnp.clip(z + sign, 0, NZ - 1)
+            self.wires.send(own, buf.at[k - 1], sems.at[k - 1], {"z": onward}, inside)
+
+    def finish(self, dst):
+        z = self.z
+        self.ready(z)
+        own, sib = self.own.at[z], self.sib.at[z]
+
+        @pl.when(z > 0)
+        def _():
+            self.wires.arrived(self.left.at[0], self.s_left.at[0], {"z": z})
+
+        @pl.when(z < NZ - 1)
+        def _():
+            self.wires.arrived(self.right.at[0], self.s_right.at[0], {"z": z})
+
+        @pl.when(z == 0)
+        def _():
+            total_into(dst, [own, sib, self.right.at[0]])
+
+        @pl.when(z == NZ - 1)
+        def _():
+            total_into(dst, [own, sib, self.left.at[0]])
+
+        @pl.when((z > 0) & (z < NZ - 1))
+        def _():
+            total_into(dst, [own, sib, self.left.at[0], self.right.at[0]])
+
+
+def line_scratch(slot):
+    return [
+        pltpu.VMEM((NZ,) + slot, BF16),
+        pltpu.VMEM((NZ,) + slot, BF16),
+        pltpu.VMEM((NZ - 1,) + slot, BF16),
+        pltpu.VMEM((NZ - 1,) + slot, BF16),
+        pltpu.SemaphoreType.DMA((NZ,)),
+        pltpu.SemaphoreType.DMA((NZ,)),
+        pltpu.SemaphoreType.DMA((NZ - 1,)),
+        pltpu.SemaphoreType.DMA((NZ - 1,)),
+    ]
+
+
+TILES = ((0, 640), (640, None))
+
+
+def remote(src, dst, send_sem, recv_sem, device):
+    return pltpu.make_async_remote_copy(
+        src_ref=src,
+        dst_ref=dst,
+        send_sem=send_sem,
+        recv_sem=recv_sem,
+        device_id=device,
+        device_id_type=pl.DeviceIdType.MESH,
+    )
+
+
+def mlp_kernel(
+    h,
+    wg,
+    wu,
+    wd,
+    cot,
+    dh,
+    out_part,
+    grad_g,
+    grad_u,
+    grad_d,
+    hv,
+    cv,
+    wgv,
+    wuv,
+    wdv,
+    av,
+    dgv,
+    duv,
+    part,
+    sib,
+    ring,
+    ob,
+    s_load,
+    s_cot,
+    s_ob,
+    s_out,
+    h_send,
+    h_on,
+    h_sib,
+    h_recv,
+    p_send,
+    p_recv,
+    r_send,
+    r_recv,
+):
+    y, z, x, c = place()
+    rows, wide = h.shape
+    units = wg.shape[1]
+    other = 1 - c
+    inner = (z > 0) & (z < NZ - 1)
+    greet(line_peers(z, c))
+
+    def block(zq, cq):
+        return pl.ds(pl.multiple_of((zq * NC + cq) * rows, rows), rows)
+
+    loads = [
+        pltpu.make_async_copy(h, hv.at[block(z, c)], s_load.at[0]),
+        pltpu.make_async_copy(wg, wgv, s_load.at[1]),
+        pltpu.make_async_copy(wu, wuv, s_load.at[2]),
+        pltpu.make_async_copy(wd, wdv, s_load.at[3]),
+    ]
+
+    def load_cot(zq, cq):
+        return pltpu.make_async_copy(
+            cot.at[block(zq, cq)], cv.at[block(zq, cq)], s_cot.at[zq, cq]
+        )
+
+    def send_own(i):
+        there = hv.at[block(z, c)]
+        device = (
+            {"z": jnp.minimum(z + 1, NZ - 1)},
+            {"z": jnp.maximum(z - 1, 0)},
+            {"c": other},
+        )[i]
+        return remote(h, there, h_send.at[i], h_recv.at[z, c], device)
+
+    pl.when(z < NZ - 1)(send_own(0).start)
+    pl.when(z > 0)(send_own(1).start)
+    send_own(2).start()
+    for copy in loads[:3]:
+        copy.start()
+    load_cot(z, c).start()
+    loads[3].start()
+    load_cot(z, other).start()
+    for k in range(NZ - 1):
+        for i in range(NC):
+            load_cot(line_order(z, k), (c + i) % NC).start()
+
+    def arrival(zq, cq):
+        here = hv.at[block(zq, cq)]
+        return remote(here, here, h_send.at[0], h_recv.at[zq, cq], {"c": other})
+
+    def onward(k):
+        zq = line_order(z, k)
+        here = hv.at[block(zq, c)]
+        device = {"z": jnp.where(zq < z, jnp.minimum(z + 1, NZ - 1), jnp.maximum(z - 1, 0))}
+        return remote(here, here, h_on.at[k], h_recv.at[zq, c], device)
+
+    def to_sibling(k):
+        zq = line_order(z, k)
+        here = hv.at[block(zq, c)]
+        return remote(here, here, h_sib.at[k], h_recv.at[zq, c], {"c": other})
+
+    def take(k):
+        arrival(line_order(z, k), c).wait_recv()
+        pl.when(inner)(onward(k).start)
+        to_sibling(k).start()
+
+    def output(zq, cq):
+        return pltpu.make_async_copy(ob.at[cq], out_part.at[block(zq, cq)], s_ob.at[cq])
+
+    def partial_over(zq):
+        return remote(
+            part.at[block(zq, other)], sib.at[zq], p_send.at[zq], p_recv.at[zq], {"c": other}
+        )
+
+    def partial_home(zq):
+        j = (z - zq + NZ) % NZ - 1
+        return remote(
+            part.at[block(zq, c)], ring.at[j], r_send.at[zq], r_recv.at[j], {"z": zq}
+        )
+
+    piece = rows // 8
+
+    def combine(zq):
+        remote(sib.at[zq], sib.at[zq], p_send.at[0], p_recv.at[zq], {"c": other}).wait_recv()
+
+        def step(i, carry):
+            here = pl.ds(pl.multiple_of((zq * NC + c) * rows + i * piece, piece), piece)
+            there = pl.ds(pl.multiple_of(i * piece, piece), piece)
+            total = part[here].astype(F32) + sib[zq, there].astype(F32)
+            part[here] = total.astype(BF16)
+            return carry
+
+        lax.fori_loop(0, 8, step, 0)
+
+    def place_of(k):
+        near = line_order(z, 0)
+        mid = line_order(z, 1)
+        far = line_order(z, 2)
+        return jnp.where(k == 0, z, jnp.where(k == 1, near, jnp.where(k == 2, mid, far)))
+
+    def pair(k, carry):
+        zq = place_of(k)
+
+        @pl.when(k == 1)
+        def _():
+            take(0)
+            pl.when(inner)(lambda: take(1))
+
+        @pl.when(k == 2)
+        def _():
+            pl.when(jnp.logical_not(inner))(lambda: take(1))
+            pl.when(inner)(lambda: take(2))
+
+        @pl.when((k == 3) & jnp.logical_not(inner))
+        def _():
+            take(2)
+
+        def one(j, carry):
+            cq = (c + j) % NC
+            here = block(zq, cq)
+
+            @pl.when((k == 0) & (j == 0))
+            def _():
+                for copy in loads:
+                    copy.wait()
+
+            @pl.when(j == 1)
+            def _():
+                arrival(zq, cq).wait_recv()
+
+            load_cot(zq, cq).wait()
+            for low, high in TILES:
+                high = units if high is None else high
+                gate = dot(hv[here], wgv[:, low:high])
+                up = dot(hv[here], wuv[:, low:high])
+                grad = dot_nt(cv[here], wdv[low:high])
+                sig = jax.nn.sigmoid(gate)
+                act = gate * sig
+                av[here, low:high] = (act * up).astype(BF16)
+                duv[here, low:high] = (grad * act).astype(BF16)
+                dgv[here, low:high] = (
+                    grad * up * (sig * (1.0 + gate * (1.0 - sig)))
+                ).astype(BF16)
+
+            @pl.when(k > 0)
+            def _():
+                output(zq, cq).wait()
+
+            ob[cq] = dot(av[here], wdv[...]).astype(BF16)
+            output(zq, cq).start()
+            part[here] = (dot_nt(dgv[here], wgv[...]) + dot_nt(duv[here], wuv[...])).astype(BF16)
+            return carry
+
+        lax.fori_loop(0, NC, one, 0)
+        partial_over(zq).start()
+
+        @pl.when(k > 1)
+        def _():
+            before = place_of(k - 1)
+            combine(before)
+            partial_home(before).start()
+
+        return carry
+
+    lax.fori_loop(0, NZ, pair, 0)
+    last = line_order(z, NZ - 2)
+    step_d = wide // 6
+
+    def down_grad(t, carry):
+        cols = pl.ds(pl.multiple_of(t * step_d, step_d), step_d)
+        wdv[:, cols] = dot_tn(av[...], cv[:, cols]).astype(BF16)
+
+        @pl.when(t == 0)
+        def _():
+            combine(last)
+            partial_home(last).start()
+
+        return carry
+
+    lax.fori_loop(0, 6, down_grad, 0)
+    outs = [
+        pltpu.make_async_copy(wdv, grad_d, s_out.at[0]),
+        pltpu.make_async_copy(wgv, grad_g, s_out.at[1]),
+        pltpu.make_async_copy(wuv, grad_u, s_out.at[2]),
+    ]
+    outs[0].start()
+
+    def gate_grad(t, carry):
+        cols = pl.ds(pl.multiple_of(t * step_d, step_d), step_d)
+        wgv[cols] = dot_tn(hv[:, cols], dgv[...]).astype(BF16)
+        wuv[cols] = dot_tn(hv[:, cols], duv[...]).astype(BF16)
+        return carry
+
+    lax.fori_loop(0, 6, gate_grad, 0)
+    outs[1].start()
+    outs[2].start()
+    combine(z)
+    for j in range(NZ - 1):
+        remote(ring.at[j], ring.at[j], r_send.at[0], r_recv.at[j], {"c": other}).wait_recv()
+
+    def final(i, carry):
+        here = pl.ds(pl.multiple_of((z * NC + c) * rows + i * piece, piece), piece)
+        there = pl.ds(pl.multiple_of(i * piece, piece), piece)
+        total = part[here].astype(F32)
+        for j in range(NZ - 1):
+            total = total + ring[j, there].astype(F32)
+        dh[there] = total
+        return carry
+
+    lax.fori_loop(0, 8, final, 0)
+    pl.when(z < NZ - 1)(send_own(0).wait_send)
+    pl.when(z > 0)(send_own(1).wait_send)
+    send_own(2).wait_send()
+    for k in range(NZ - 1):
+        pl.when(inner)(onward(k).wait_send)
+        to_sibling(k).wait_send()
+        partial_home(line_order(z, k)).wait_send()
+    for zq in range(NZ):
+        partial_over(zq).wait_send()
+    for cq in range(NC):
+        output(z, cq).wait()
+    for copy in outs:
+        copy.wait()
+
+
+def mlp(h, wg, wu, wd, cot, collective_id):
+    hbm = pl.BlockSpec(memory_space=pl.ANY)
+    vmem = pl.BlockSpec(memory_space=pltpu.VMEM)
+    rows, wide = h.shape
+    units = wg.shape[1]
+    every = NZ * NC * rows
+    dma = pltpu.SemaphoreType.DMA
+    return pl.pallas_call(
+        mlp_kernel,
+        name="mlp",
+        out_shape=(
+            jax.ShapeDtypeStruct((rows, wide), F32),
+            jax.ShapeDtypeStruct((every, wide), BF16),
+            jax.ShapeDtypeStruct((wide, units), BF16),
+            jax.ShapeDtypeStruct((wide, units), BF16),
+            jax.ShapeDtypeStruct((units, wide), BF16),
+        ),
+        in_specs=[hbm] * 5,
+        out_specs=(vmem, hbm, hbm, hbm, hbm),
+        scratch_shapes=[
+            pltpu.VMEM((every, wide), BF16),
+            pltpu.VMEM((every, wide), BF16),
+            pltpu.VMEM((wide, units), BF16),
+            pltpu.VMEM((wide, units), BF16),
+            pltpu.VMEM((units, wide), BF16),
+            pltpu.VMEM((every, units), BF16),
+            pltpu.VMEM((every, units), BF16),
+            pltpu.VMEM((every, units), BF16),
+            pltpu.VMEM((every, wide), BF16),
+            pltpu.VMEM((NZ, rows, wide), BF16),
+            pltpu.VMEM((NZ - 1, rows, wide), BF16),
+            pltpu.VMEM((NC, rows, wide), BF16),
+            dma((4,)),
+            dma((NZ, NC)),
+            dma((NC,)),
+            dma((3,)),
+            dma((3,)),
+            dma((NZ - 1,)),
+            dma((NZ - 1,)),
+            dma((NZ, NC)),
+            dma((NZ,)),
+            dma((NZ,)),
+            dma((NZ,)),
+            dma((NZ - 1,)),
+        ],
+        compiler_params=pltpu.CompilerParams(
+            collective_id=collective_id, has_side_effects=True, vmem_limit_bytes=63 << 20
+        ),
+    )(h, wg, wu, wd, cot)
+
+
+def plane_peers(nx, y, x):
+    return [{"x": (x + i + 1) % nx} for i in range(nx - 1)] + [{"y": 1 - y}]
+
+
+def last_scatter_kernel(nx, widths, grads, gate, up, down, result, *rest):
+    y, z, x, c = place()
+    outs, rest = rest[: len(widths)], rest[len(widths) :]
+    gate_out, up_out, down_out, result_out, rest = rest[:4] + (rest[4:],)
+    send_sems, blocks, own, sib, line_sum, line_in = rest[:6]
+    s_block, s_keep, s_own, s_sib, s_line = rest[6:11]
+    half_x, half_y = rest[11:17], rest[17:23]
+    gate_bufs, up_bufs, gu = rest[23:29], rest[29:35], rest[35]
+    left_bufs, right_bufs, line_bufs = rest[36:42], rest[42:48], rest[48:56]
+    cross = [{"z": (z + k + 1) % NZ, "c": 1 - c} for k in range(NZ - 1)]
+    greet(line_peers(z, c) + cross + plane_peers(nx, y, x))
+    wires = Wires(send_sems)
+    along_x, along_y = ("x", nx, x), ("y", 2, y)
+    gate_plane = PlaneScatter(
+        wires, lambda xq, yq: gate.at[yq, :, xq], along_x, along_y, gate_bufs
+    )
+    up_plane = PlaneScatter(wires, lambda yq, xq: up.at[yq, :, xq], along_y, along_x, up_bufs)
+    cols = down.shape[-1] // 2
+    left, right = pl.ds(0, cols), pl.ds(cols, cols)
+    left_plane = PlaneScatter(
+        wires, lambda xq, yq: down.at[yq, xq, :, left], along_x, along_y, left_bufs
+    )
+    right_plane = PlaneScatter(
+        wires, lambda yq, xq: down.at[yq, xq, :, right], along_y, along_x, right_bufs
+    )
+    line = LineScatter(wires, result, line_bufs, z, c)
+    gate_plane.begin()
+    up_plane.begin()
+    line.begin()
+    n = NZ // 2
+    halves = [pl.ds(0, n), pl.ds(n, n)]
+
+    def load(h, yq):
+        return pltpu.make_async_copy(
+            grads.at[yq, halves[h], :, c], own.at[yq, halves[h]], s_own.at[h, yq]
+        )
+
+    for h in range(2):
+        for yq in range(2):
+            wires.send(
+                grads.at[yq, halves[h], :, 1 - c],
+                sib.at[yq, halves[h]],
+                s_sib.at[h, yq],
+                {"c": 1 - c},
+            )
+            load(h, yq).start()
+
+    def combine(h):
+        for yq in range(2):
+            load(h, yq).wait()
+            wires.arrived(sib.at[yq, halves[h]], s_sib.at[h, yq], {"c": 1 - c})
+            for i in range(n):
+                zq = h * n + i
+                total_into(own.at[yq, zq], [own.at[yq, zq], sib.at[yq, zq]])
+
+    by_x = PlaneScatter(
+        wires, lambda xq, yq: own.at[yq, halves[0], xq], along_x, along_y, half_x, True
+    )
+    by_y = PlaneScatter(
+        wires, lambda yq, xq: own.at[yq, halves[1], xq], along_y, along_x, half_y, True
+    )
+    combine(0)
+    by_x.begin()
+    combine(1)
+    by_y.begin()
+    line.hop(3)
+    left_plane.begin()
+    right_plane.begin()
+    line.hop(2)
+    gate_plane.relay()
+    up_plane.relay()
+    line.hop(1)
+    by_x.relay()
+    by_y.relay()
+    left_plane.relay()
+    right_plane.relay()
+    gate_plane.finish(gu.at[0])
+    up_plane.finish(gu.at[1])
+    keep = pltpu.make_async_copy(gu.at[:, z, c], blocks.at[z, c], s_keep)
+    keep.start()
+    for k in range(NZ * NC - 1):
+        step = k + 1
+        zp, cp = (z + step // NC) % NZ, (c + step) % NC
+        wires.send(gu.at[:, zp, cp], blocks.at[z, c], s_block.at[z, c], {"z": zp, "c": cp})
+    by_x.finish(line_sum.at[halves[0]])
+    by_y.finish(line_sum.at[halves[1]])
+    for k in range(NZ - 1):
+        zp = (z + k + 1) % NZ
+        wires.send(line_sum.at[zp], line_in.at[NZ - 2 - k], s_line.at[NZ - 2 - k], {"z": zp})
+    line.finish(result_out)
+    left_plane.finish(down_out.at[:, left])
+    right_plane.finish(down_out.at[:, right])
+    keep.wait()
+    for k in range(NZ * NC - 1):
+        step = k + 1
+        zp, cp = (z + step // NC) % NZ, (c + step) % NC
+        wires.arrived(blocks.at[zp, cp], s_block.at[zp, cp], {"c": 1 - c})
+    fs = blocks.shape[-1] // (2 * nx)
+    for m, out in enumerate((gate_out, up_out)):
+        for zq, cq, run, first in segments(nx, fs):
+            out[:, first : first + fs] = blocks[zq, cq, m, :, run : run + fs].astype(F32)
+    for k in range(NZ - 1):
+        wires.arrived(line_in.at[k], s_line.at[k], {"c": 1 - c})
+    first = 0
+    for out, width in zip(outs, widths):
+        columns = slice(first, first + width)
+        total = line_sum[z, :, columns].astype(F32)
+        for k in range(NZ - 1):
+            total = total + line_in[k, :, columns].astype(F32)
+        out[...] = total
+        first += width
+    wires.finish()
+
+
+def last_scatter(ny, nx, grads, widths, gate, up, down, result, collective_id):
+    hbm = pl.BlockSpec(memory_space=pl.ANY)
+    vmem = pl.BlockSpec(memory_space=pltpu.VMEM)
+    rows, width = grads.shape[4:]
+    block = gate.shape[4:]
+    slot = (NZ // 2, rows, width)
+    gate_slot = (NZ, NC) + block
+    down_slot = (down.shape[2], down.shape[3] // 2)
+    sends = 4 + 7 + NZ - 1 + 3 * ((nx - 1) * 2 + 1 + nx + (nx - 1)) + NZ + 2 * (NZ - 1)
+    spread = block[1] * NZ * NC
+    shapes = [(rows, w) for w in widths] + [(rows, spread)] * 2
+    shapes += [down.shape[2:], result.shape[2:]]
+    return pl.pallas_call(
+        lambda *refs: last_scatter_kernel(nx, widths, *refs),
+        name="last_scatter",
+        out_shape=tuple(jax.ShapeDtypeStruct(shape, F32) for shape in shapes),
+        in_specs=[hbm] * 5,
+        out_specs=(vmem,) * len(shapes),
+        scratch_shapes=[
+            pltpu.SemaphoreType.DMA((sends,)),
+            pltpu.VMEM((NZ, NC, 2) + block, BF16),
+            pltpu.VMEM((ny, NZ, nx, rows, width), BF16),
+            pltpu.VMEM((ny, NZ, nx, rows, width), BF16),
+            pltpu.VMEM((NZ, rows, width), BF16),
+            pltpu.VMEM((NZ - 1, rows, width), BF16),
+            pltpu.SemaphoreType.DMA((NZ, NC)),
+            pltpu.SemaphoreType.DMA,
+            pltpu.SemaphoreType.DMA((2, 2)),
+            pltpu.SemaphoreType.DMA((2, 2)),
+            pltpu.SemaphoreType.DMA((NZ - 1,)),
+        ]
+        + plane_scratch(slot, nx, ny, True)
+        + plane_scratch(slot, ny, nx, True)
+        + plane_scratch(gate_slot, nx, ny)
+        + plane_scratch(gate_slot, ny, nx)
+        + [pltpu.VMEM((2,) + gate_slot, BF16)]
+        + plane_scratch(down_slot, nx, ny)
+        + plane_scratch(down_slot, ny, nx)
+        + line_scratch(result.shape[2:]),
+        compiler_params=pltpu.CompilerParams(
+            collective_id=collective_id, has_side_effects=True, vmem_limit_bytes=60 << 20
+        ),
+    )(grads, gate, up, down, result)
 
 
 def make_body(ny, nx):
-    def spread_columns(shard):
-        rows, cols = shard.shape
-        fs = cols // (ny * NZ * nx * NC)
-        view = shard.reshape(rows, ny, NZ, nx, NC, fs)
-        return view.transpose(2, 4, 0, 1, 3, 5).reshape(NZ * NC, rows, ny * nx * fs)
-
-    def unspread_columns(blocks):
-        _, rows, width = blocks.shape
-        fs = width // (ny * nx)
-        view = blocks.reshape(NZ, NC, rows, ny, nx, fs)
-        return view.transpose(2, 3, 0, 4, 1, 5).reshape(rows, -1)
-
-    def scatter_columns(grad):
-        width = grad.shape[1]
-        rows = grad.shape[0] // (ny * NZ * nx * NC)
-        view = grad.reshape(ny, NZ, nx, NC, rows, width).transpose(0, 2, 1, 3, 4, 5)
-        view = view.reshape(ny * nx * NZ * NC, rows, width)
-        part = lax.psum_scatter(view, DP, scatter_dimension=0, tiled=True)
-        back = lax.all_to_all(part, TP, split_axis=0, concat_axis=0, tiled=True)
-        return unspread_columns(back).astype(F32)
-
     def body(
         inputs,
         segment_ids,
@@ -392,12 +1012,12 @@
             axis=1,
         )
         packed = jnp.concatenate([q_weight, k_weight, v_weight, o_weight, extra], axis=1)
-        columns = jnp.stack([spread_columns(gate_weight), spread_columns(up_weight)], axis=1)
         attn_all, columns_all, down_all, grad_out_all = weight_gather(
             ny,
             nx,
             packed,
-            columns.reshape((NZ, NC) + columns.shape[1:]),
+            gate_weight,
+            up_weight,
             down_weight,
             grad_out,
             0,
@@ -409,7 +1029,7 @@
         gain_one = tail[..., 0].reshape(-1)
         gain_two = tail[..., 1].reshape(-1)
         bias = tail[..., 0, 2 : 2 + b_rows].reshape(-1)
-        width = columns.shape[-1]
+        width = gate_weight.shape[1] // (NZ * NC)
         full_gate = columns_all[0].reshape(-1, width)
         full_up = columns_all[1].reshape(-1, width)
         full_down = down_all.reshape(width, -1)
@@ -447,31 +1067,10 @@
         rescale_two = lax.rsqrt(jnp.mean(middle * middle, axis=-1, keepdims=True) + EPS)
         normed_two = middle * rescale_two
         input_two = (normed_two * gain_two).astype(BF16)
-        input_all = token_gather(input_two, 1)
-        gate_pre = dot(input_all, full_gate)
-        up_pre = dot(input_all, full_up)
-        gate_sig = jax.nn.sigmoid(gate_pre)
-        gate_act = gate_pre * gate_sig
-        inner = (gate_act * up_pre).astype(BF16)
-        grad_inner = dot_nt(grad_out_all, full_down)
-        grad_gate = (
-            grad_inner * up_pre * gate_sig * (1.0 + gate_pre * (1.0 - gate_sig))
-        ).astype(BF16)
-        grad_up = (grad_inner * gate_act).astype(BF16)
-        grad_in_part = (dot_nt(grad_gate, full_gate) + dot_nt(grad_up, full_up)).astype(BF16)
-        grad_input_two = lax.psum_scatter(
-            grad_in_part, TP, scatter_dimension=0, tiled=True
-        ).astype(F32)
-        out_part = dot(inner, full_down).astype(BF16)
-        out_sum = lax.psum_scatter(out_part, TP, scatter_dimension=0, tiled=True)
-        output = (middle + out_sum.astype(F32)).astype(BF16)[None]
-
-        grad_gate_w = scatter_columns(dot_tn(input_all, grad_gate).astype(BF16))
-        grad_up_w = scatter_columns(dot_tn(input_all, grad_up).astype(BF16))
-        grad_down_w = lax.psum_scatter(
-            dot_tn(inner, grad_out_all).astype(BF16), DP, scatter_dimension=0, tiled=True
-        ).astype(F32)
-
+        by_shard = (ny, NZ, nx, NC, g_rows, width)
+        grad_input_two, out_part, part_gate, part_up, part_down = mlp(
+            input_two, full_gate, full_up, full_down, grad_out_all, 1
+        )
         grad_gain_two, grad_mid = norm_back(grad_input_two, normed_two, rescale_two, gain_two)
         grad_mid = grad_mid + grad_out.astype(F32)
         grad_branch = grad_mid.astype(BF16)
@@ -504,38 +1103,56 @@
         grad_key_pre = rotate(grad_kv_tok[:, :key_width], cos_tok, -sin_tok).astype(BF16)
         grad_value_pre = grad_kv_tok[:, key_width:].astype(BF16)
         grad_qkv = jnp.concatenate([grad_query_pre, grad_key_pre, grad_value_pre], axis=1)
-        grad_attn_w = lax.psum_scatter(
-            jnp.concatenate(
-                [dot_tn(input_one, grad_qkv), dot_tn(attn_tok, grad_branch)], axis=1
-            ).astype(BF16),
-            ALL,
-            scatter_dimension=0,
-            tiled=True,
-        ).astype(F32)
         grad_qkv_sum = jnp.sum(grad_qkv.astype(F32), axis=0)
         grad_input_one = dot_nt(grad_qkv, full_qkv)
         grad_gain_one, grad_first = norm_back(grad_input_one, normed_one, rescale_one, gain_one)
         grad_total = grad_mid + grad_first
         shards = ny * NZ * nx * NC
-        small_grads = jnp.concatenate(
+        tail_grads = jnp.concatenate(
             [
-                grad_gain_one.reshape(shards, -1),
-                grad_qkv_sum.reshape(shards, -1),
-                grad_gain_two.reshape(shards, -1),
+                grad_gain_one[:, None],
+                grad_gain_two[:, None],
+                jnp.broadcast_to(
+                    grad_qkv_sum.reshape(shards, 1, b_rows), (shards, g_rows, b_rows)
+                ).reshape(-1, b_rows),
+                jnp.zeros((shards * g_rows, HD - 2 - b_rows), F32),
             ],
             axis=1,
         )
-        small_sums = lax.psum_scatter(small_grads, ALL, scatter_dimension=0, tiled=True)[0]
+        grad_attn_w = jnp.concatenate(
+            [
+                dot_tn(input_one, grad_qkv).astype(BF16),
+                dot_tn(attn_tok, grad_branch).astype(BF16),
+                tail_grads.astype(BF16),
+            ],
+            axis=1,
+        )
+        widths = (query_width, key_width, key_width, query_width, HD)
+        pieces = (NZ, NC, tok_rows // 32, 32, hidden_in.shape[1])
+        outs = last_scatter(
+            ny,
+            nx,
+            grad_attn_w.reshape((ny, NZ, nx, NC, g_rows, -1)),
+            widths,
+            part_gate.reshape(by_shard),
+            part_up.reshape(by_shard),
+            part_down.reshape((ny, nx) + down_weight.shape),
+            out_part.reshape(pieces),
+            3,
+        )
+        grad_q, grad_k, grad_v, grad_o, tail_sum = outs[:5]
+        grad_gate_w, grad_up_w, grad_down_w, out_sum = outs[5:]
+        output = (middle + out_sum.reshape(middle.shape)).astype(BF16)[None]
         return (
             output,
             grad_total.astype(BF16)[None],
-            small_sums[:g_rows],
-            grad_attn_w[:, :query_width],
-            grad_attn_w[:, query_width : query_width + key_width],
-            grad_attn_w[:, query_width + key_width : qkv_width],
-            small_sums[g_rows : g_rows + b_rows],
-            grad_attn_w[:, qkv_width:],
-            small_sums[g_rows + b_rows :],
+            tail_sum[:, 0],
+            grad_q,
+            grad_k,
+            grad_v,
+            tail_sum[0, 2 : 2 + b_rows],
+            grad_o,
+            tail_sum[:, 1],
             grad_gate_w,
             grad_up_w,
             grad_down_w,

time: 804 us -> 610 us (0.76)
  Pallas kernels: 212 us -> 471 us
  waiting for transfers between devices: 253 us -> 0.01 us
  matrix products: 158 us -> 47.2 us
  blocking collectives: 48.5 us -> 7.57 us
  local copies, waits for them, and re-layouts: 70.8 us -> 47.9 us
  between operations: 15.5 us -> 1.56 us
  starting transfers between devices: 11.3 us -> 1.77 us
    pallas_call x1 -> x2, Pallas kernels: 57.8 us -> 315 us  [the longest x1 178 us: last_scatter(): pl.pallas_call(lambda *refs: last_scatter_kernel(nx, widths, *refs), name...]
    reduce_scatter x5 -> x0, waiting for transfers between devices: 202 us -> none  [the longest x1 68.7 us: body(): out_sum = lax.psum_scatter(out_part, TP, scatter_dimension=0, tiled=True)]
    dot_general x5 -> x2, matrix products: 57.1 us -> 10.7 us  [dot_nt(): lax.dot_general(a, b, (((1,), (1,)), ((), ())), preferred_element_type=F32)]
    unnamed x7 -> x0, waiting for transfers between devices: 44.8 us -> none
    unnamed x1 -> x0, blocking collectives: 40.9 us -> none
    convert_element_type x8 -> x0, local copies, waits for them, and re-layouts: 36.2 us -> none  [the longest x6 27.6 us: scatter_columns(): return unspread_columns(back).astype(F32)]
    dot_general x5 -> x2, matrix products: 43.5 us -> 8.37 us  [dot_tn(): lax.dot_general(a, b, (((0,), (0,)), ((), ())), preferred_element_type=F32)]
    dot_general x5 -> x2, matrix products: 41.2 us -> 8.74 us  [dot(): return jnp.dot(a, b, preferred_element_type=F32)]
  transfers between devices with their start and end apart: 9 -> 1, of which waited for: 7 -> 0; matrix products, arithmetic and copies ran while one was open for 17% -> 1% of each run, Pallas kernels for 0% -> 0%
where the time goes in v3:
time: 610 us; the launch traced here: 601 us
  Pallas kernels  471 us (77%)
  local copies, waits for them, and re-layouts  47.9 us (8%)
  matrix products  47.2 us (8%)
  other arithmetic  24.1 us (4%)
  blocking collectives  7.57 us (1%)
    pallas_call x1, Pallas kernels, last_scatter(): pl.pallas_call(lambda *refs: last_scatter_kernel(nx, widths, *refs), name...  178 us
    pallas_call x1, Pallas kernels, weight_gather(): pl.pallas_call(lambda *refs: weight_gather_kernel(nx, *refs), name='weigh...  156 us
    pallas_call x1, Pallas kernels, mlp(): pl.pallas_call(mlp_kernel, name='mlp', out_shape=(jax.ShapeDtypeStruct((r...  136 us
    concatenate x1, local copies, waits for them, and re-layouts, body(): jnp.concatenate([dot_tn(input_one, grad_qkv).astype(BF16), dot_tn(attn_to...  17 us
  transfers between devices with their start and end apart: 1, of which 0 were waited for; matrix products, arithmetic and copies ran while one was open for 1% of the time, Pallas kernels for 0%

profile of v3, /device:TPU:0, one launch (start us, length us, event | category | flops | bytes accessed | tf_op | source)
XLA Modules:
  0.0 600.7 jit_solution(4904652544471686860)
XLA Ops:
  2.8 1.8 concatenate.36.refs_0_
  4.7 155.9 %weight_gather.1 = (bf16[2,4,2,2,48,3712]{5,4,3,2,1,0:T(8,128)(2,1)}, bf16[2,2,4,2,2,48,1120]{6,5,4,3,2,1,0:T(8,128)(2,1)}, bf16[2,2,280,1536]{3,2,1,0:T(8,128)(2,1)}, bf16[4,2,256,1536]{3,2,1,0:T(8,128)(2,1)}) custom-call(bf16[48,3712]{1,0:T(8,128)(2,1)} %concatenate.36.refs_0_, bf16[48,8960]{1,0:T(8,128)(2,1)} %refs_1_.1, bf16[48,8960]{1,0:T(8,128)(2,1)} %refs_2_.1, ...), custom_call_target="tpu_custom_call" | custom-call | tf_op jit(solution)/shard_map/weight_gather/pallas_call | solution.py:285
  163.5 4.6 fusion.19
  173.1 7.6 %all_gather.3 = bf16[512,512]{1,0:T(8,128)(2,1)S(1)} all-gather(bf16[256,512]{1,0:T(8,128)(2,1)S(1)} %pad_maximum_fusion.3), channel_id=1, replica_groups=mesh['y'=2,'z'=4,'x'=2,'c'=2] {'y'}, dimensions={0}, use_global_device_ids=true | all-gather | bytes 786432 | tf_op jit(solution)/shard_map/all_gather | solution.py:1045
  181.0 1.6 copy.48
  182.6 1.6 subtract_convert_fusion.1
  184.7 4.9 fusion.74
  189.5 3.5 fusion.42
  193.0 4.1 multiply_reduce_fusion.2
  197.3 7.1 %fusion.71 = (bf16[1,2,4,2,2,48,1120]{6,5,4,3,2,1,0:T(8,128)(2,1)}, bf16[1,2,4,2,2,48,1120]{6,5,4,3,2,1,0:T(8,128)(2,1)}) fusion(bf16[2,2,4,2,2,48,1120]{6,5,4,3,2,1,0:T(8,128)(2,1)} %get-tuple-element.31), kind=kLoop, calls=%fused_computation.112 | loop fusion | bytes 13762560 | tf_op jit(solution)/shard_map/slice | solution.py:1034
  205.5 136.4 %mlp.1 = (f32[256,1536]{1,0:T(8,128)}, bf16[2048,1536]{1,0:T(8,128)(2,1)}, bf16[1536,1120]{1,0:T(8,128)(2,1)}, bf16[1536,1120]{1,0:T(8,128)(2,1)}, bf16[1120,1536]{1,0:T(8,128)(2,1)}) custom-call(bf16[256,1536]{1,0:T(8,128)(2,1)} %multiply_convert_fusion.h, bf16[1536,1120]{1,0:T(8,128)(2,1)} %bitcast.110, bf16[1536,1120]{1,0:T(8,128)(2,1)} %bitcast.109, ...), custom_call_target="tpu_custom_call" | custom-call | tf_op jit(solution)/shard_map/mlp/pallas_call | solution.py:765
  341.9 2.5 multiply_reduce_fusion
  346.3 4.7 fusion.22
  352.6 6.5 %fusion.1 = (f32[2,6,256]{2,1,0:T(8,128)S(1)}, f32[2,512,256,6]{2,1,3,0:T(8,128)}) fusion(f32[2,6,256,512]{2,3,1,0:T(8,128)} %get-tuple-element.74, f32[2,6,256]{2,1,0:T(8,128)S(1)} %get-tuple-element.73, bf16[256,2,6,128]{0,3,2,1:T(8,128)(2,1)S(1)} %bitcast.139, bf16[512,2,128,1]{2,1,0,3:T(2,128)(2,1)S(1)} %bitcast.145), kind=kOutput, calls=%fused_computation.5 | convolution fusion | flops 407368704 | bytes 13656064 | tf_op jit(solution)/shard_map/qkgd,pkd->kgqp/dot_general | solution.py:1079
  359.2 1.9 fusion.49
  361.0 5.7 fusion.3
  367.9 1.6 fusion.59
  369.6 1.8 collective-permute-start
  372.9 3.5 convolution_convert_fusion.1
  379.9 6.0 fusion.31
  385.9 4.9 convolution_convert_fusion
  391.2 17.0 %concatenate.44 = bf16[1536,3712]{1,0:T(8,128)(2,1)} concatenate(bf16[1536,2048]{1,0:T(8,128)(2,1)} %convolution_convert_fusion, bf16[1536,1536]{1,0:T(8,128)(2,1)} %convolution_convert_fusion.1, bf16[1536,1]{1,0:T(8,128)(2,1)S(1)} %broadcast_in_dim.85, bf16[1536,1]{1,0:T(8,128)(2,1)S(1)} %broadcast_in_dim.86, bf16[1536,64]{1,0:T(8,128)(2,1)S(1)} %bitcast.131, ...), dimensions={1} | concatenate | bytes 22806528 | tf_op jit(solution)/shard_map/concatenate | solution.py:1122
  408.3 178.2 %last_scatter.1 = (f32[48,1536]{1,0:T(8,128)}, f32[48,256]{1,0:T(8,128)}, f32[48,256]{1,0:T(8,128)}, f32[48,1536]{1,0:T(8,128)}, f32[48,128]{1,0:T(8,128)}, /*in...) custom-call(bf16[2,4,2,2,48,3712]{5,4,3,2,1,0:T(8,128)(2,1)} %bitcast.108, ...), custom_call_target="tpu_custom_call" | custom-call | tf_op jit(solution)/shard_map/last_scatter/pallas_call | solution.py:939
  589.4 2.5 fusion.37
  (141 shorter events, 33.1 us)
Async XLA Ops:
  171.1 11.6 %copy-start.19 = (f32[256,64]{0,1:T(8,128)}, f32[256,64]{0,1:T(8,128)S(1)}, u32[]{:S(2)}) copy-start(f32[256,64]{0,1:T(8,128)S(1)} %get-tuple-element.72) | copy-start | bytes 196612
  171.7 9.3 %slice-start = ((f32[256,2048]{1,0:T(8,128)}), f32[256,1536]{1,0:T(8,128)S(1)}, s32[]{:S(2)}) async-start(f32[256,2048]{1,0:T(8,128)} %copy-done.8), calls=%async_computation | async-start | bytes 3145728 | tf_op jit(solution)/shard_map/slice | solution.py:1042
  181.0 3.6 copy-start.21
  184.3 5.2 copy-start.26
  184.4 5.1 copy-start.10
  193.0 4.1 copy-start.13
  193.0 4.2 copy-start.28
  197.2 7.2 %copy-start = (f32[256,1536]{1,0:T(8,128)}, f32[256,1536]{1,0:T(8,128)S(1)}, u32[]{:S(2)}) copy-start(f32[256,1536]{1,0:T(8,128)S(1)} %get-tuple-element.76) | copy-start | bytes 4718596
  205.5 139.0 %copy-start.12 = (bf16[1,256,1536]{2,1,0:T(8,128)(2,1)S(1)}, bf16[1,256,1536]{2,1,0:T(8,128)(2,1)}, u32[]{:S(2)}) copy-start(bf16[1,256,1536]{2,1,0:T(8,128)(2,1)} %param.25) | copy-start | bytes 2359300
  346.3 6.2 %copy-start.27 = (bf16[512,2,128]{2,1,0:T(2,128)(2,1)S(1)}, bf16[512,2,128]{2,1,0:T(2,128)(2,1)}, u32[]{:S(2)}) copy-start(bf16[512,2,128]{2,1,0:T(2,128)(2,1)} %copy-done.26) | copy-start | bytes 786436
  351.0 8.1 %slice-start.1 = ((s8[6291456]{0:T(1024)(128)(4,1)}), s8[2097152]{0:T(1024)(128)(4,1)S(1)}, s32[]{:S(2)}) async-start(s8[6291456]{0:T(1024)(128)(4,1)} %bitcast.118), calls=%async_computation.1 | async-start | bytes 4194304
  352.6 6.6 %slice-start.2 = ((s8[6291456]{0:T(1024)(128)(4,1)}), s8[4194304]{0:T(1024)(128)(4,1)S(1)}, s32[]{:S(2)}) async-start(s8[6291456]{0:T(1024)(128)(4,1)} %bitcast.118), calls=%async_computation.2 | async-start | bytes 8388608
  361.0 5.7 copy-start.11
  369.6 3.3 copy-start.4
  369.6 3.3 copy-start.14
  369.6 7.5 %collective-permute-start = (bf16[256,512]{0,1:T(8,128)(2,1)}, bf16[256,512]{0,1:T(8,128)(2,1)}, u32[]{:S(2)}, u32[]{:S(2)}) collective-permute-start(bf16[256,512]{0,1:T(8,128)(2,1)} %fusion.59), channel_id=1, source_target_pairs={{0,16},{16,0},{1,17},{17,1},{2,18},{18,2},{3,19},{19,3},{4,20},{20... | collective-permute-start | bytes 786440 | tf_op jit(solution)/shard_map/ppermute | solution.py:1100
  372.9 3.5 copy-start.20
  372.9 3.5 copy-start.23
  408.3 181.1 %copy-start.2 = (f32[256,1536]{1,0:T(8,128)S(1)}, f32[256,1536]{1,0:T(8,128)}, u32[]{:S(2)}) copy-start(f32[256,1536]{1,0:T(8,128)} %copy-done) | copy-start | bytes 4718596
  586.5 5.4 copy-start.5
  586.5 5.4 copy-start.18
  591.8 3.4 copy-start.24
  591.9 4.1 copy-start.17
  594.0 3.2 copy-start.16
  (13 other events, 25.0 us)

commit v4 on v3

--- a/solution.py
+++ b/solution.py
@@ -309,7 +309,7 @@
     )(a, g, u, d, tok)
 
 
-def total_into(dst, refs):
+def total_into(dst, refs, flat=None):
     flat = len(dst.shape) == 2
 
     def entry(i, carry):
@@ -498,6 +498,8 @@
 
 
 def mlp_kernel(
+    nx,
+    with_down,
     h,
     wg,
     wu,
@@ -508,37 +510,45 @@
     grad_g,
     grad_u,
     grad_d,
-    hv,
-    cv,
-    wgv,
-    wuv,
-    wdv,
-    av,
-    dgv,
-    duv,
-    part,
-    sib,
-    ring,
-    ob,
-    s_load,
-    s_cot,
-    s_ob,
-    s_out,
-    h_send,
-    h_on,
-    h_sib,
-    h_recv,
-    p_send,
-    p_recv,
-    r_send,
-    r_recv,
+    *scratch,
 ):
+    if with_down:
+        down_out, out_sib, scratch = scratch[0], scratch[1], scratch[2:]
+    (
+        hv,
+        cv,
+        wgv,
+        wuv,
+        wdv,
+        av,
+        dgv,
+        duv,
+        part,
+        sib,
+        ring,
+        ob,
+        s_load,
+        s_cot,
+        s_ob,
+        s_out,
+        h_send,
+        h_on,
+        h_sib,
+        h_recv,
+        p_send,
+        p_recv,
+        r_send,
+        r_recv,
+    ) = scratch[: 24]
+    scratch = scratch[24:]
+    if with_down:
+        o_send, o_recv, scratch = scratch[0], scratch[1], scratch[2:]
     y, z, x, c = place()
     rows, wide = h.shape
     units = wg.shape[1]
     other = 1 - c
     inner = (z > 0) & (z < NZ - 1)
-    greet(line_peers(z, c))
+    greet(line_peers(z, c) + (plane_peers(nx, y, x) if with_down else []))
 
     def block(zq, cq):
         return pl.ds(pl.multiple_of((zq * NC + cq) * rows, rows), rows)
@@ -597,7 +607,16 @@
         to_sibling(k).start()
 
     def output(zq, cq):
+        if with_down:
+            here = pl.ds(pl.multiple_of(zq * rows, rows), rows)
+            return pltpu.make_async_copy(ob.at[cq], out_part.at[here], s_ob.at[0])
         return pltpu.make_async_copy(ob.at[cq], out_part.at[block(zq, cq)], s_ob.at[cq])
+
+    def output_over(zq):
+        here = pl.ds(pl.multiple_of(zq * rows, rows), rows)
+        return remote(
+            ob.at[other], out_sib.at[here], o_send.at[zq], o_recv.at[zq], {"c": other}
+        )
 
     def partial_over(zq):
         return remote(
@@ -674,12 +693,28 @@
                     grad * up * (sig * (1.0 + gate * (1.0 - sig)))
                 ).astype(BF16)
 
-            @pl.when(k > 0)
-            def _():
-                output(zq, cq).wait()
+            if with_down:
+
+                @pl.when((k > 0) & (j == 0))
+                def _():
+                    output(zq, cq).wait()
+
+                @pl.when((k > 0) & (j == 1))
+                def _():
+                    output_over(place_of(k - 1)).wait_send()
+
+            else:
+
+                @pl.when(k > 0)
+                def _():
+                    output(zq, cq).wait()
 
             ob[cq] = dot(av[here], wdv[...]).astype(BF16)
-            output(zq, cq).start()
+            if with_down:
+                pl.when(j == 0)(output(zq, cq).start)
+                pl.when(j == 1)(output_over(zq).start)
+            else:
+                output(zq, cq).start()
             part[here] = (dot_nt(dgv[here], wgv[...]) + dot_nt(duv[here], wuv[...])).astype(BF16)
             return carry
 
@@ -716,16 +751,43 @@
         pltpu.make_async_copy(wuv, grad_u, s_out.at[2]),
     ]
     outs[0].start()
-
-    def gate_grad(t, carry):
-        cols = pl.ds(pl.multiple_of(t * step_d, step_d), step_d)
-        wgv[cols] = dot_tn(hv[:, cols], dgv[...]).astype(BF16)
-        wuv[cols] = dot_tn(hv[:, cols], duv[...]).astype(BF16)
-        return carry
-
-    lax.fori_loop(0, 6, gate_grad, 0)
+    if with_down:
+        wires = Wires(scratch[0])
+        half, shard = wide // 2, units // (2 * nx)
+        left, right = pl.ds(0, half), pl.ds(half, half)
+
+        def term(yq, xq, cols):
+            first = (yq * nx + xq) * shard
+            return grad_d.at[pl.ds(pl.multiple_of(first, 8), shard), cols]
+
+        along_x, along_y = ("x", nx, x), ("y", 2, y)
+        by_x = PlaneScatter(
+            wires, lambda xq, yq: term(yq, xq, left), along_x, along_y, scratch[1:7]
+        )
+        by_y = PlaneScatter(
+            wires, lambda yq, xq: term(yq, xq, right), along_y, along_x, scratch[7:13]
+        )
+
+    def turned(src, dst, first, last):
+        def step(t, carry):
+            cols = pl.ds(pl.multiple_of(t * step_d, step_d), step_d)
+            dst[cols] = dot_tn(hv[:, cols], src[...]).astype(BF16)
+            return carry
+
+        lax.fori_loop(first, last, step, 0)
+
+    turned(dgv, wgv, 0, 1)
+    if with_down:
+        outs[0].wait()
+        by_x.begin()
+        by_y.begin()
+    turned(dgv, wgv, 1, 6)
     outs[1].start()
+    turned(duv, wuv, 0, 6)
     outs[2].start()
+    if with_down:
+        by_x.relay()
+        by_y.relay()
     combine(z)
     for j in range(NZ - 1):
         remote(ring.at[j], ring.at[j], r_send.at[0], r_recv.at[j], {"c": other}).wait_recv()
@@ -740,6 +802,10 @@
         return carry
 
     lax.fori_loop(0, 8, final, 0)
+    if with_down:
+        by_x.finish(down_out.at[:, left])
+        by_y.finish(down_out.at[:, right])
+        wires.finish()
     pl.when(z < NZ - 1)(send_own(0).wait_send)
     pl.when(z > 0)(send_own(1).wait_send)
     send_own(2).wait_send()
@@ -749,31 +815,54 @@
         partial_home(line_order(z, k)).wait_send()
     for zq in range(NZ):
         partial_over(zq).wait_send()
-    for cq in range(NC):
-        output(z, cq).wait()
-    for copy in outs:
+    if with_down:
+        output(z, c).wait()
+        output_over(last).wait_send()
+        for zq in range(NZ):
+            there = out_sib.at[pl.ds(zq * rows, rows)]
+            remote(there, there, o_send.at[0], o_recv.at[zq], {"c": other}).wait_recv()
+    else:
+        for cq in range(NC):
+            output(z, cq).wait()
+    for copy in outs[1 if with_down else 0 :]:
         copy.wait()
 
 
-def mlp(h, wg, wu, wd, cot, collective_id):
+def mlp(ny, nx, with_down, h, wg, wu, wd, cot, collective_id):
     hbm = pl.BlockSpec(memory_space=pl.ANY)
     vmem = pl.BlockSpec(memory_space=pltpu.VMEM)
     rows, wide = h.shape
     units = wg.shape[1]
     every = NZ * NC * rows
     dma = pltpu.SemaphoreType.DMA
+    shard = units // (ny * nx)
+    down_scratch = []
+    if with_down:
+        sends = 2 * ((nx - 1) * 2 + 1 + nx + (nx - 1))
+        down_scratch = [dma((NZ,)), dma((NZ,)), dma((sends,))]
+        down_scratch += plane_scratch((shard, wide // 2), nx, ny)
+        down_scratch += plane_scratch((shard, wide // 2), ny, nx)
+    extra_shape, extra_specs, kept = (), (), every
+    if with_down:
+        kept = NZ * rows
+        extra_shape = (
+            jax.ShapeDtypeStruct((shard, wide), BF16),
+            jax.ShapeDtypeStruct((kept, wide), BF16),
+        )
+        extra_specs = (vmem, hbm)
     return pl.pallas_call(
-        mlp_kernel,
+        lambda *refs: mlp_kernel(nx, with_down, *refs),
         name="mlp",
         out_shape=(
             jax.ShapeDtypeStruct((rows, wide), F32),
-            jax.ShapeDtypeStruct((every, wide), BF16),
+            jax.ShapeDtypeStruct((kept, wide), BF16),
             jax.ShapeDtypeStruct((wide, units), BF16),
             jax.ShapeDtypeStruct((wide, units), BF16),
             jax.ShapeDtypeStruct((units, wide), BF16),
-        ),
+        )
+        + extra_shape,
         in_specs=[hbm] * 5,
-        out_specs=(vmem, hbm, hbm, hbm, hbm),
+        out_specs=(vmem, hbm, hbm, hbm, hbm) + extra_specs,
         scratch_shapes=[
             pltpu.VMEM((every, wide), BF16),
             pltpu.VMEM((every, wide), BF16),
@@ -799,7 +888,8 @@
             dma((NZ,)),
             dma((NZ,)),
             dma((NZ - 1,)),
-        ],
+        ]
+        + down_scratch,
         compiler_params=pltpu.CompilerParams(
             collective_id=collective_id, has_side_effects=True, vmem_limit_bytes=63 << 20
         ),
@@ -969,6 +1059,368 @@
     )(grads, gate, up, down, result)
 
 
+def back_kernel(
+    nx,
+    key_width,
+    b_rows,
+    gate,
+    up,
+    ao,
+    kept,
+    given,
+    mid,
+    branch,
+    tokens,
+    gain,
+    attn,
+    query,
+    kv,
+    mask,
+    turn_c,
+    turn_s,
+    gain_term,
+    out_q,
+    out_k,
+    out_v,
+    out_o,
+    out_tail,
+    out_gate,
+    out_up,
+    out_in,
+    out_ring,
+    send_sems,
+    weights,
+    term_o,
+    term_q,
+    sib_o,
+    sib_q,
+    line_sum,
+    line_in,
+    blocks,
+    gu,
+    d_attn,
+    d_qkv,
+    d_kv,
+    kv_send,
+    kv_recv,
+    first_in,
+    s_weights,
+    s_sib,
+    s_line,
+    s_block,
+    s_kv,
+    result,
+    s_result,
+    s_ring,
+    *bufs,
+):
+    y, z, x, c = place()
+    sib = {"c": 1 - c}
+    cross = [{"z": (z + k + 1) % NZ, "c": 1 - c} for k in range(NZ - 1)]
+    greet(line_peers(z, c) + cross + plane_peers(nx, y, x))
+    wires = Wires(send_sems)
+    along_x, along_y = ("x", nx, x), ("y", 2, y)
+    gate_plane = PlaneScatter(
+        wires, lambda xq, yq: gate.at[yq, :, xq], along_x, along_y, bufs[0:6]
+    )
+    up_plane = PlaneScatter(wires, lambda yq, xq: up.at[yq, :, xq], along_y, along_x, bufs[6:12])
+    gate_plane.begin()
+    up_plane.begin()
+    rows, wide = branch.shape
+    q_width = query.shape[1]
+    qkv_width = q_width + 2 * key_width
+    heads, kv_heads = q_width // HD, key_width // HD
+    n = NZ // 2
+    halves = [pl.ds(0, n), pl.ds(n, n)]
+    tile = n * nx * NC * out_q.shape[0]
+    shard = out_q.shape[0]
+
+    def fetch(first, width):
+        return pltpu.make_async_copy(
+            ao.at[:, :, pl.ds(first, width)], weights.at[:, :, pl.ds(0, width)], s_weights
+        )
+
+    fetch(qkv_width, wide).start()
+
+    def fill(term, yq, h, first, value):
+        value = value.reshape((n, nx, NC, shard, value.shape[1]))
+        term[yq, halves[h], :, :, :, first : first + value.shape[4]] = value.astype(BF16)
+
+    def over(i, term, other, yq, h):
+        wires.send(
+            term.at[yq, halves[h], :, 1 - c],
+            other.at[yq, halves[h]],
+            s_sib.at[i, yq, h],
+            sib,
+        )
+
+    def combine(i, term, other):
+        for h in range(2):
+            for yq in range(2):
+                here = other.at[yq, halves[h]]
+                wires.arrived(here, s_sib.at[i, yq, h], sib)
+                for zq in range(h * n, h * n + n):
+                    for xq in range(nx):
+                        mine = term.at[yq, zq, xq, c]
+                        total_into(mine, [mine, other.at[yq, zq, xq]], True)
+
+    def planes(term, first):
+        return (
+            PlaneScatter(
+                wires,
+                lambda xq, yq: term.at[yq, halves[0], xq, c],
+                along_x,
+                along_y,
+                bufs[first : first + 6],
+                True,
+            ),
+            PlaneScatter(
+                wires,
+                lambda yq, xq: term.at[yq, halves[1], xq, c],
+                along_y,
+                along_x,
+                bufs[first + 6 : first + 12],
+                True,
+            ),
+        )
+
+    for yq in range(2):
+        for h in range(2):
+            i = yq * 2 + h
+            fill(term_o, yq, h, 0, dot_tn(attn[:, i * tile : (i + 1) * tile], branch[...]))
+            over(0, term_o, sib_o, yq, h)
+
+    for i, k in enumerate((2, 0, 1)):
+        zq = line_order(z, k)
+        here = pl.ds(pl.multiple_of(zq * rows, rows), rows)
+        loads = [
+            pltpu.make_async_copy(kept.at[here], result.at[i], s_result.at[0]),
+            pltpu.make_async_copy(given.at[here], first_in, s_result.at[1]),
+        ]
+        for copy in loads:
+            copy.start()
+        for copy in loads:
+            copy.wait()
+        total_into(result.at[i], [result.at[i], first_in])
+        j = (z - zq + NZ) % NZ - 1
+        wires.send(result.at[i], out_ring.at[j], s_ring.at[j], {"z": zq})
+
+    fetch(qkv_width, wide).wait()
+    for_out = weights[:, :, :wide].reshape(q_width, wide)
+    d_attn[...] = dot_nt(branch[...], for_out).astype(BF16)
+    fetch(0, qkv_width).start()
+    d_kv[...] = jnp.zeros_like(d_kv)
+    scale = HD ** (-0.5)
+
+    def turn_back(value):
+        return value * turn_c[...] + pltpu.roll(value, HD // 2, 1) * turn_s[...]
+
+    group = heads // kv_heads
+    for kv_head in range(kv_heads):
+        k_cols = pl.ds(kv_head * HD, HD)
+        v_cols = pl.ds(key_width + kv_head * HD, HD)
+
+        def head(i, carry):
+            cols = pl.ds(pl.multiple_of((kv_head * group + i) * HD, HD), HD)
+            q_h, do_h = query[:, cols], d_attn[:, cols]
+            scores = jnp.where(mask[...] > 0, dot_nt(q_h, kv[:, k_cols]) * scale, MASKED)
+            exponent = jnp.exp(scores - jnp.max(scores, axis=-1, keepdims=True))
+            probs = exponent / jnp.sum(exponent, axis=-1, keepdims=True)
+            d_probs = dot_nt(do_h, kv[:, v_cols])
+            inner = jnp.sum(probs * d_probs, axis=-1, keepdims=True)
+            d_scores = (probs * (d_probs - inner)).astype(BF16)
+            d_qkv[:, cols] = turn_back(dot(d_scores, kv[:, k_cols]) * scale).astype(BF16)
+            d_kv[:, k_cols] += dot_tn(d_scores, q_h) * scale
+            d_kv[:, v_cols] += dot_tn(probs.astype(BF16), do_h)
+            return carry
+
+        lax.fori_loop(0, group, head, 0)
+
+    other_rows = pl.ds(pl.multiple_of((1 - y) * rows, rows), rows)
+    own_rows = pl.ds(pl.multiple_of(y * rows, rows), rows)
+    kv_send[...] = d_kv[other_rows].astype(BF16)
+    gate_plane.relay()
+    wires.send(kv_send, kv_recv, s_kv, {"y": 1 - y})
+    up_plane.relay()
+    combine(0, term_o, sib_o)
+    o_planes = planes(term_o, 12)
+    for plane in o_planes:
+        plane.begin()
+    x32 = tokens[...].astype(F32)
+    rescale = lax.rsqrt(jnp.mean(x32 * x32, axis=-1, keepdims=True) + EPS)
+    first_in[...] = (x32 * rescale * gain[...]).astype(BF16)
+    wires.arrived(kv_recv, s_kv, {"y": 1 - y})
+    for kv_head in range(2 * kv_heads):
+        cols = pl.ds(kv_head * HD, HD)
+        total = d_kv[own_rows, cols] + kv_recv[:, cols].astype(F32)
+        if kv_head < kv_heads:
+            total = turn_back(total)
+        d_qkv[:, pl.ds(q_width + kv_head * HD, HD)] = total.astype(BF16)
+    fetch(0, qkv_width).wait()
+    for_in = weights[...].reshape(wide, qkv_width)
+    d_first = dot_nt(d_qkv[...], for_in)
+    normed = x32 * rescale
+    scaled = d_first * gain[...]
+    d_x = rescale * (scaled - normed * jnp.mean(scaled * normed, axis=-1, keepdims=True))
+    out_in[...] = (mid[...] + d_x).astype(BF16)
+    first_term = (d_first * normed).astype(BF16)
+    lane = lax.broadcasted_iota(jnp.int32, (rows, HD), 1)
+    pick_one = (lane == 0).astype(F32).astype(BF16)
+    pick_two = (lane == 1).astype(F32).astype(BF16)
+    bias_sum = jnp.sum(d_qkv[...].astype(F32), axis=0, keepdims=True)
+    top = lax.broadcasted_iota(jnp.int32, (shard, HD), 0) == 0
+    wide_bias = jnp.concatenate([bias_sum, bias_sum[:, :HD]], axis=1)
+    for yq in range(2):
+        for h in range(2):
+            i = yq * 2 + h
+            cols = slice(i * tile, (i + 1) * tile)
+            fill(term_q, yq, h, 0, dot_tn(first_in[:, cols], d_qkv[...]))
+            tail = dot_tn(first_term[:, cols], pick_one) + dot_tn(gain_term[:, cols], pick_two)
+            for zi in range(n):
+                for xq in range(nx):
+                    for cq in range(NC):
+                        part = ((zi * nx + xq) * NC + cq) * shard
+                        place_at = i * (tile // shard) + (zi * nx + xq) * NC + cq
+                        first = place_at * b_rows
+                        base = (first // HD) * HD
+                        bias = wide_bias[:, base : base + HD]
+                        bias = pltpu.roll(
+                            jnp.broadcast_to(bias, (8, HD)), (HD // 2 - (first - base)) % HD, 1
+                        )[:1]
+                        keep = lax.broadcasted_iota(jnp.int32, (shard, HD), 1) >= HD // 2
+                        mixed = tail[part : part + shard] + jnp.where(top & keep, bias, 0.0)
+                        term_q[yq, h * n + zi, xq, cq, :, qkv_width:] = mixed.astype(BF16)
+            over(1, term_q, sib_q, yq, h)
+    combine(1, term_q, sib_q)
+    q_planes = planes(term_q, 24)
+    for plane in q_planes:
+        plane.begin()
+    gate_plane.finish(gu.at[0])
+    up_plane.finish(gu.at[1])
+    keep_block = pltpu.make_async_copy(gu.at[:, z, c], blocks.at[z, c], s_block.at[z, c])
+    keep_block.start()
+    for k in range(NZ * NC - 1):
+        step = k + 1
+        zp, cp = (z + step // NC) % NZ, (c + step) % NC
+        wires.send(gu.at[:, zp, cp], blocks.at[z, c], s_block.at[z, c], {"z": zp, "c": cp})
+    for plane in o_planes:
+        plane.relay()
+    for plane in q_planes:
+        plane.relay()
+
+    def along_line(i, first, width, pair):
+        cols = pl.ds(first, width)
+        pair[0].finish(line_sum.at[halves[0], :, cols])
+        pair[1].finish(line_sum.at[halves[1], :, cols])
+        for k in range(NZ - 1):
+            zp, j = (z + k + 1) % NZ, NZ - 2 - k
+            wires.send(
+                line_sum.at[zp, :, cols], line_in.at[j, :, cols], s_line.at[i, j], {"z": zp}
+            )
+
+    q_all = qkv_width + HD
+    along_line(0, q_all, wide, o_planes)
+    along_line(1, 0, q_all, q_planes)
+    keep_block.wait()
+    for k in range(NZ * NC - 1):
+        step = k + 1
+        zp, cp = (z + step // NC) % NZ, (c + step) % NC
+        wires.arrived(blocks.at[zp, cp], s_block.at[zp, cp], sib)
+    fs = blocks.shape[-1] // (2 * nx)
+    for m, out in enumerate((out_gate, out_up)):
+        for zq, cq, run, first in segments(nx, fs):
+            out[:, first : first + fs] = blocks[zq, cq, m, :, run : run + fs]
+
+    def last(i, out, first, width):
+        if i is not None:
+            begin, size = (q_all, wide) if i == 0 else (0, q_all)
+            for j in range(NZ - 1):
+                wires.arrived(line_in.at[j, :, pl.ds(begin, size)], s_line.at[i, j], sib)
+        columns = slice(first, first + width)
+        total = line_sum[z, :, columns].astype(F32)
+        for j in range(NZ - 1):
+            total = total + line_in[j, :, columns].astype(F32)
+        out[...] = total
+
+    last(0, out_o, q_all, wide)
+    last(1, out_q, 0, q_width)
+    last(None, out_k, q_width, key_width)
+    last(None, out_v, q_width + key_width, key_width)
+    last(None, out_tail, qkv_width, HD)
+    for j in range(NZ - 1):
+        wires.arrived(out_ring.at[j], s_ring.at[j], sib)
+    wires.finish()
+
+
+def back(ny, nx, b_rows, gate, up, ao, kept, given, args, collective_id):
+    hbm = pl.BlockSpec(memory_space=pl.ANY)
+    vmem = pl.BlockSpec(memory_space=pltpu.VMEM)
+    mid, branch, tokens, gain, attn, query, kv, mask, turn_c, turn_s, gain_term = args
+    dma = pltpu.SemaphoreType.DMA
+    shard = ao.shape[1]
+    block = gate.shape[4:]
+    rows, wide = branch.shape
+    q_width = query.shape[1]
+    key_width = kv.shape[1] // 2
+    qkv_width = q_width + 2 * key_width
+    q_all = qkv_width + HD
+    spread = block[1] * NZ * NC
+    one_plane = (nx - 1) * 2 + 1 + nx + (nx - 1)
+    sends = 3 * one_plane + 8 + 1 + 7 + 3 * (NZ - 1)
+    slot_o, slot_q = (NZ // 2, shard, wide), (NZ // 2, shard, q_all)
+    gate_slot = (NZ, NC) + block
+    place_all = (ny, NZ, nx, NC, shard)
+    shapes = [(shard, q_width), (shard, key_width), (shard, key_width), (shard, wide), (shard, HD)]
+    return pl.pallas_call(
+        lambda *refs: back_kernel(nx, key_width, b_rows, *refs),
+        name="back",
+        cost_estimate=pl.CostEstimate(
+            flops=100_000_000_000, bytes_accessed=100_000_000, transcendentals=0
+        ),
+        out_shape=tuple(jax.ShapeDtypeStruct(shape, F32) for shape in shapes)
+        + (jax.ShapeDtypeStruct((shard, spread), BF16),) * 2
+        + (jax.ShapeDtypeStruct((rows, wide), BF16),)
+        + (jax.ShapeDtypeStruct((NZ - 1, rows, wide), BF16),),
+        in_specs=[hbm] * 5 + [vmem] * len(args),
+        out_specs=(vmem,) * 8 + (hbm,),
+        scratch_shapes=[
+            dma((sends,)),
+            pltpu.VMEM((ny * NZ * nx * NC, shard, qkv_width), BF16),
+            pltpu.VMEM(place_all + (wide,), BF16),
+            pltpu.VMEM(place_all + (q_all,), BF16),
+            pltpu.VMEM((ny, NZ, nx, shard, wide), BF16),
+            pltpu.VMEM((ny, NZ, nx, shard, q_all), BF16),
+            pltpu.VMEM((NZ, shard, q_all + wide), BF16),
+            pltpu.VMEM((NZ - 1, shard, q_all + wide), BF16),
+            pltpu.VMEM((NZ, NC, 2) + block, BF16),
+            pltpu.VMEM((2,) + gate_slot, BF16),
+            pltpu.VMEM((rows, q_width), BF16),
+            pltpu.VMEM((rows, qkv_width), BF16),
+            pltpu.VMEM((2 * rows, 2 * key_width), F32),
+            pltpu.VMEM((rows, 2 * key_width), BF16),
+            pltpu.VMEM((rows, 2 * key_width), BF16),
+            pltpu.VMEM((rows, wide), BF16),
+            dma,
+            dma((2, 2, 2)),
+            dma((2, NZ - 1)),
+            dma((NZ, NC)),
+            dma,
+            pltpu.VMEM((NZ - 1, rows, wide), BF16),
+            dma((2,)),
+            dma((NZ - 1,)),
+        ]
+        + plane_scratch(gate_slot, nx, ny)
+        + plane_scratch(gate_slot, ny, nx)
+        + plane_scratch(slot_o, nx, ny, True)
+        + plane_scratch(slot_o, ny, nx, True)
+        + plane_scratch(slot_q, nx, ny, True)
+        + plane_scratch(slot_q, ny, nx, True),
+        compiler_params=pltpu.CompilerParams(
+            collective_id=collective_id, has_side_effects=True, vmem_limit_bytes=67_043_328
+        ),
+    )(gate, up, ao, kept, given, *args)
+
+
 def make_body(ny, nx):
     def body(
         inputs,
@@ -1068,12 +1520,60 @@
         normed_two = middle * rescale_two
         input_two = (normed_two * gain_two).astype(BF16)
         by_shard = (ny, NZ, nx, NC, g_rows, width)
-        grad_input_two, out_part, part_gate, part_up, part_down = mlp(
-            input_two, full_gate, full_up, full_down, grad_out_all, 1
+        fused = g_rows % 16 == 0
+        grad_input_two, out_part, part_gate, part_up, *downs = mlp(
+            ny, nx, fused, input_two, full_gate, full_up, full_down, grad_out_all, 1
         )
         grad_gain_two, grad_mid = norm_back(grad_input_two, normed_two, rescale_two, gain_two)
         grad_mid = grad_mid + grad_out.astype(F32)
         grad_branch = grad_mid.astype(BF16)
+        if fused:
+            args = (
+                grad_mid,
+                grad_branch,
+                inputs[0],
+                gain_one[None],
+                attn_tok,
+                query,
+                kv_all,
+                allowed.astype(F32),
+                jnp.concatenate([cos_tok, cos_tok], axis=1),
+                jnp.concatenate([sin_tok, -sin_tok], axis=1),
+                (grad_input_two * normed_two).astype(BF16),
+            )
+            outs = back(
+                ny,
+                nx,
+                b_rows,
+                part_gate.reshape(by_shard),
+                part_up.reshape(by_shard),
+                attn_all.reshape((-1,) + packed.shape),
+                out_part,
+                downs[2],
+                args,
+                3,
+            )
+            grad_q, grad_k, grad_v, grad_o, tail_sum, grad_gate_w, grad_up_w = outs[:7]
+            grad_in, ring = outs[7:]
+            first_row = lax.axis_index("z") * tok_rows
+            out_sum = jnp.sum(ring.astype(F32), axis=0)
+            for half in (out_part, downs[2]):
+                out_sum += lax.dynamic_slice_in_dim(half, first_row, tok_rows).astype(F32)
+            output = (middle + out_sum).astype(BF16)[None]
+            return (
+                output,
+                grad_in[None],
+                tail_sum[:, 0],
+                grad_q,
+                grad_k,
+                grad_v,
+                tail_sum[0, HD // 2 : HD // 2 + b_rows],
+                grad_o,
+                tail_sum[:, 1],
+                grad_gate_w.astype(F32),
+                grad_up_w.astype(F32),
+                downs[1].astype(F32),
+            )
         grad_attn = dot_nt(grad_branch, full_out).astype(BF16)
         grad_heads = grad_attn.reshape(tok_rows, kv_heads, group, HD)
         grad_probs = jnp.einsum(
@@ -1136,7 +1636,7 @@
             widths,
             part_gate.reshape(by_shard),
             part_up.reshape(by_shard),
-            part_down.reshape((ny, nx) + down_weight.shape),
+            downs[0].reshape((ny, nx) + down_weight.shape),
             out_part.reshape(pieces),
             3,
         )

time: 610 us -> 536 us (0.88)
  matrix products: 47.2 us -> 16.6 us
  Pallas kernels: 471 us -> 442 us
  local copies, waits for them, and re-layouts: 47.9 us -> 27.1 us
  blocking collectives: 7.57 us -> 17.8 us
    dot_general x8 -> x0, matrix products: 30.1 us -> none  [the longest x2 10.7 us: dot_nt(): lax.dot_general(a, b, (((1,), (1,)), ((), ())), preferred_element_type=F32)]
    pallas_call x2, Pallas kernels: 315 us -> 287 us  [the longest x1 151 us: back(): pl.pallas_call(lambda *refs: back_kernel(nx, key_width, b_rows, *refs), n...]
    concatenate x2 -> x0, local copies, waits for them, and re-layouts: 17.2 us -> none  [the longest x1 17 us: body(): jnp.concatenate([dot_tn(input_one, grad_qkv).astype(BF16), dot_tn(attn_to...]
    all_gather x1, blocking collectives: 7.57 us -> 17.8 us  [body(): kv_all = lax.all_gather(kv, 'y', axis=0, tiled=True)]
  transfers between devices with their start and end apart: 1 -> 0, of which waited for: 0 -> 0; matrix products, arithmetic and copies ran while one was open for 1% -> 0% of each run, Pallas kernels for 0% -> 0%
where the time goes in v4:
time: 536 us; the launch traced here: 528 us
  Pallas kernels  442 us (82%)
  local copies, waits for them, and re-layouts  27.1 us (5%)
  other arithmetic  22.4 us (4%)
  blocking collectives  17.8 us (3%)
  matrix products  16.6 us (3%)
    pallas_call x1, Pallas kernels, weight_gather(): pl.pallas_call(lambda *refs: weight_gather_kernel(nx, *refs), name='weigh...  156 us
    pallas_call x1, Pallas kernels, back(): pl.pallas_call(lambda *refs: back_kernel(nx, key_width, b_rows, *refs), n...  151 us
    pallas_call x1, Pallas kernels, mlp(): pl.pallas_call(lambda *refs: mlp_kernel(nx, with_down, *refs), name='mlp'...  136 us
    all_gather x1, blocking collectives, body(): kv_all = lax.all_gather(kv, 'y', axis=0, tiled=True)  17.8 us

profile of v4, /device:TPU:0, one launch (start us, length us, event | category | flops | bytes accessed | tf_op | source)
XLA Modules:
  0.0 527.8 jit_solution(2407675638518821888)
XLA Ops:
  1.4 1.4 fusion.16
  5.0 1.8 concatenate.20.refs_0_
  12.1 155.9 %weight_gather.1 = (bf16[2,4,2,2,48,3712]{5,4,3,2,1,0:T(8,128)(2,1)}, bf16[2,2,4,2,2,48,1120]{6,5,4,3,2,1,0:T(8,128)(2,1)}, bf16[2,2,280,1536]{3,2,1,0:T(8,128)(2,1)}, bf16[4,2,256,1536]{3,2,1,0:T(8,128)(2,1)}) custom-call(bf16[48,3712]{1,0:T(8,128)(2,1)} %concatenate.20.refs_0_, bf16[48,8960]{1,0:T(8,128)(2,1)} %refs_1_.1, bf16[48,8960]{1,0:T(8,128)(2,1)} %refs_2_.1, ...), custom_call_target="tpu_custom_call" | custom-call | tf_op jit(solution)/shard_map/weight_gather/pallas_call | solution.py:285
  168.1 6.7 %fusion.41 = (bf16[1,2,4,2,2,48,1120]{6,5,4,3,2,1,0:T(8,128)(2,1)}, bf16[1,2,4,2,2,48,1120]{6,5,4,3,2,1,0:T(8,128)(2,1)}) fusion(bf16[2,2,4,2,2,48,1120]{6,5,4,3,2,1,0:T(8,128)(2,1)} %get-tuple-element.32), kind=kLoop, calls=%fused_computation.70 | loop fusion | bytes 13762560 | tf_op jit(solution)/shard_map/slice | solution.py:1486
  174.8 1.1 slice_convert_fusion
  177.8 4.6 fusion.13
  183.8 1.1 multiply_subtract_fusion
  186.1 17.8 %all_gather.3.refs_11_ = bf16[512,512]{1,0:T(8,128)(2,1)S(1)} all-gather(bf16[256,512]{1,0:T(8,128)(2,1)S(1)} %pad_maximum_fusion), channel_id=1, replica_groups=mesh['y'=2,'z'=4,'x'=2,'c'=2] {'y'}, dimensions={0}, use_global_device_ids=true | all-gather | bytes 786432 | tf_op jit(solution)/shard_map/all_gather | solution.py:1497
  205.0 1.2 copy.44.refs_10_
  206.2 4.8 fusion.43
  211.0 3.4 fusion.19
  214.4 1.2 copy.43.refs_9_
  215.5 3.8 multiply_reduce_fusion.1
  219.4 1.1 copy-done
  220.5 1.1 multiply_convert_fusion.1.refs_0_
  221.6 135.9 %mlp.1 = (f32[256,1536]{1,0:T(8,128)}, bf16[1024,1536]{1,0:T(8,128)(2,1)}, bf16[1536,1120]{1,0:T(8,128)(2,1)}, bf16[1536,1120]{1,0:T(8,128)(2,1)}, bf16[1120,153...) custom-call(bf16[256,1536]{1,0:T(8,128)(2,1)} %multiply_convert_fusion.1.refs_0_, ...), custom_call_target="tpu_custom_call" | custom-call | tf_op jit(solution)/shard_map/mlp/pallas_call | solution.py:853
  357.6 2.4 multiply_reduce_fusion
  360.4 2.2 fusion.40
  362.6 150.6 %back.1 = (f32[48,1536]{1,0:T(8,128)}, f32[48,256]{1,0:T(8,128)}, f32[48,256]{1,0:T(8,128)}, f32[48,1536]{1,0:T(8,128)}, f32[48,128]{1,0:T(8,128)}, /*index=5*/b...) custom-call(bf16[2,4,2,2,48,1120]{5,4,3,2,1,0:T(8,128)(2,1)} %bitcast.82, ...), custom_call_target="tpu_custom_call" | custom-call | flops 99999997952 | bytes 100000000 | tf_op jit(solution)/shard_map/back/pallas_call | solution.py:1374
  513.2 2.3 convert_reduce_fusion
  515.6 2.8 fusion.20
  519.6 1.3 convert_element_type.96
  520.9 1.3 convert_element_type.97
  522.4 1.4 convert_element_type.98
  (82 shorter events, 19.1 us)
Async XLA Ops:
  0.6 9.7 %copy-start.19 = (s32[1,512]{1,0:T(1,128)S(1)}, s32[1,512]{1,0:T(1,128)}, u32[]{:S(2)}) copy-start(s32[1,512]{1,0:T(1,128)} %param.14) | copy-start | bytes 6148
  174.8 3.0 copy-start.10
  183.8 1.2 copy-start.6
  203.9 0.8 copy-start.5
  204.8 1.4 copy-start.15
  214.4 1.2 copy-start.11
  219.4 1.1 copy-start
  221.6 138.3 %copy-start.4 = (bf16[1,256,1536]{2,1,0:T(8,128)(2,1)S(1)}, bf16[1,256,1536]{2,1,0:T(8,128)(2,1)}, u32[]{:S(2)}) copy-start(bf16[1,256,1536]{2,1,0:T(8,128)(2,1)} %param.25) | copy-start | bytes 2359300
  357.5 2.4 copy-start.1
  357.5 2.8 copy-start.3
  513.2 2.3 copy-start.2
  515.5 2.8 copy-start.16
  515.6 4.1 copy-start.9
  518.3 2.6 copy-start.8
  520.9 1.5 copy-start.7
  522.4 1.4 copy-start.12
  522.4 2.3 copy-start.14
  523.8 1.6 copy-start.18
  523.8 2.2 copy-start.17
  523.8 2.9 copy-start.13

commit v5 on v4

--- a/solution.py
+++ b/solution.py
@@ -1,3 +1,5 @@
+import types
+
 import jax
 import jax.numpy as jnp
 from jax import lax
@@ -72,12 +74,12 @@
             device_id=device,
             device_id_type=pl.DeviceIdType.MESH,
         )
-        self.used += 1
         if cond is None:
             copy.start()
         else:
-            pl.when(cond)(copy.start)
-        self.started.append((copy, cond))
+            pl.when(cond())(copy.start)
+        self.started.append((still(src), self.used, cond))
+        self.used += 1
 
     def arrived(self, dst, recv_sem, device):
         pltpu.make_async_remote_copy(
@@ -89,12 +91,35 @@
             device_id_type=pl.DeviceIdType.MESH,
         ).wait_recv()
 
-    def finish(self):
-        for copy, cond in self.started:
+    def finish(self, sent=None):
+        for src, used, cond in self.started if sent is None else sent:
+            sem = self.sems.at[used]
+            src = taken(*src)
+            copy = pltpu.make_async_remote_copy(
+                src_ref=src,
+                dst_ref=src,
+                send_sem=sem,
+                recv_sem=sem,
+                device_id={"c": 1 - lax.axis_index("c")},
+                device_id_type=pl.DeviceIdType.MESH,
+            )
             if cond is None:
                 copy.wait_send()
             else:
-                pl.when(cond)(copy.wait_send)
+                pl.when(cond())(copy.wait_send)
+
+
+def still(ref):
+    steps = []
+    for step in getattr(ref, "transforms", ()):
+        steps.append([i.size if isinstance(i, pl.Slice) else None for i in step.indices])
+    return getattr(ref, "ref", ref), steps
+
+
+def taken(view, steps):
+    for step in steps:
+        view = view.at[tuple(0 if size is None else pl.ds(0, size) for size in step)]
+    return view
 
 
 def line_order(z, k):
@@ -132,8 +157,8 @@
     def begin(self):
         w, z, c = self.wires, self.z, self.c
         dst, sem = self.out.at[z, c], self.recv.at[z, c]
-        w.send(self.own, dst, sem, {"z": jnp.minimum(z + 1, NZ - 1)}, z < NZ - 1)
-        w.send(self.own, dst, sem, {"z": jnp.maximum(z - 1, 0)}, z > 0)
+        w.send(self.own, dst, sem, {"z": jnp.minimum(z + 1, NZ - 1)}, lambda: z < NZ - 1)
+        w.send(self.own, dst, sem, {"z": jnp.maximum(z - 1, 0)}, lambda: z > 0)
         w.send(self.own, dst, sem, {"c": 1 - c})
 
     def event(self, k):
@@ -142,7 +167,7 @@
         slot, sem = self.out.at[zq, c], self.recv.at[zq, c]
         w.arrived(slot, sem, {"c": 1 - c})
         onward = jnp.where(zq < z, jnp.minimum(z + 1, NZ - 1), jnp.maximum(z - 1, 0))
-        w.send(slot, slot, sem, {"z": onward}, (z > 0) & (z < NZ - 1))
+        w.send(slot, slot, sem, {"z": onward}, lambda: (z > 0) & (z < NZ - 1))
         w.send(slot, slot, sem, {"c": 1 - c})
 
     def sibling(self, zq):
@@ -184,8 +209,8 @@
             wires.send(src, dst, sem, peer)
 
     own_slot, own_sem = ao.at[y, z, x, c], ra.at[y, z, x, c]
-    wires.send(a, own_slot, own_sem, {"z": jnp.minimum(z + 1, NZ - 1)}, z < NZ - 1)
-    wires.send(a, own_slot, own_sem, {"z": jnp.maximum(z - 1, 0)}, z > 0)
+    wires.send(a, own_slot, own_sem, {"z": jnp.minimum(z + 1, NZ - 1)}, lambda: z < NZ - 1)
+    wires.send(a, own_slot, own_sem, {"z": jnp.maximum(z - 1, 0)}, lambda: z > 0)
     both_ways(a, own_slot, own_sem)
     wires.send(a, own_slot, own_sem, sib)
     fs = gu.shape[-1] // (2 * nx)
@@ -198,7 +223,7 @@
         slot, sem = ao.at[y, zq, x, c], ra.at[y, zq, x, c]
         wires.arrived(slot, sem, sib)
         onward = jnp.where(zq < z, jnp.minimum(z + 1, NZ - 1), jnp.maximum(z - 1, 0))
-        wires.send(slot, slot, sem, {"z": onward}, (z > 0) & (z < NZ - 1))
+        wires.send(slot, slot, sem, {"z": onward}, lambda: (z > 0) & (z < NZ - 1))
         both_ways(slot, slot, sem)
         wires.send(slot, slot, sem, sib)
 
@@ -442,7 +467,7 @@
                     total_into(own, [own, sib])
 
             onward = jnp.clip(z + sign, 0, NZ - 1)
-            self.wires.send(own, buf.at[k - 1], sems.at[k - 1], {"z": onward}, inside)
+            self.wires.send(own, buf.at[k - 1], sems.at[k - 1], {"z": onward}, lambda: inside)
 
     def finish(self, dst):
         z = self.z
@@ -894,6 +919,627 @@
             collective_id=collective_id, has_side_effects=True, vmem_limit_bytes=63 << 20
         ),
     )(h, wg, wu, wd, cot)
+
+
+def forward_kernel(nx, b_rows, names, *refs):
+    r = types.SimpleNamespace(**dict(zip(names, refs)))
+    y, z, x, c = place()
+    other = 1 - c
+    sib, ypeer = {"c": other}, {"y": 1 - y}
+    xpeers = [(x + i + 1) % nx for i in range(nx - 1)]
+    planes = [{"x": xp} for xp in xpeers] + [ypeer]
+    cross = [{"z": (z + k + 1) % NZ, "c": other} for k in range(NZ - 1)]
+    inner = (z > 0) & (z < NZ - 1)
+    rows, wide = r.tok.shape
+    shard = r.a.shape[0]
+    key_width = r.kv_out.shape[1] // 2
+    q_width = r.q_out.shape[1]
+    qkv_width = q_width + 2 * key_width
+    units = r.grad_d.shape[0]
+    fs = units // (2 * nx)
+    down_rows = r.d.shape[0]
+    greet(line_peers(z, c) + cross + planes)
+    ao, guo, co = r.ao, r.guo, r.co
+
+    def down_at(yq, xq, cols):
+        first = pl.multiple_of((yq * nx + xq) * down_rows, 8)
+        return r.do.at[pl.ds(first, down_rows), cols]
+
+    def remote_order(k):
+        step = k + 1
+        return (z + step // NC) % NZ, (c + step) % NC
+
+    half = wide // 2
+    parts = [pl.ds(0, half), pl.ds(half, half)]
+    locals_ = [
+        pltpu.make_async_copy(r.a, ao.at[y, z, x, c], r.s_local.at[0]),
+        pltpu.make_async_copy(r.d, down_at(y, x, pl.ds(0, wide)), r.s_local.at[1]),
+        pltpu.make_async_copy(r.tok, co.at[z, c], r.s_local.at[2]),
+    ]
+    for copy in locals_:
+        copy.start()
+    wires = Wires(r.send_sems)
+
+    def both_ways(src, dst, sem):
+        for peer in planes:
+            wires.send(src, dst, sem, peer)
+
+    def relay(ref, sem, peers):
+        wires.arrived(ref, sem, sib)
+        for peer in peers:
+            wires.send(ref, ref, sem, peer)
+
+    own_slot, own_sem = ao.at[y, z, x, c], r.ra.at[y, z, x, c]
+    wires.send(r.a, own_slot, own_sem, {"z": jnp.minimum(z + 1, NZ - 1)}, lambda: z < NZ - 1)
+    wires.send(r.a, own_slot, own_sem, {"z": jnp.maximum(z - 1, 0)}, lambda: z > 0)
+    both_ways(r.a, own_slot, own_sem)
+    wires.send(r.a, own_slot, own_sem, sib)
+    line = LineGather(wires, r.tok, co, r.rc, z, c)
+
+    def block(zq, cq):
+        return pl.ds(pl.multiple_of((zq * NC + cq) * rows, rows), rows)
+
+    hv = r.hv
+
+    def send_own(i):
+        here = hv.at[block(z, c)]
+        device = (
+            {"z": jnp.minimum(z + 1, NZ - 1)},
+            {"z": jnp.maximum(z - 1, 0)},
+            {"c": other},
+        )[i]
+        return remote(here, here, r.h_send.at[i], r.h_recv.at[z, c], device)
+
+    def relay_attn(yq, xq, zq, peers):
+        slot, sem = ao.at[yq, zq, xq, c], r.ra.at[yq, zq, xq, c]
+        wires.arrived(slot, sem, sib)
+        for peer in peers:
+            wires.send(slot, slot, sem, peer)
+        wires.send(slot, slot, sem, sib)
+
+    def attention(gs, us, gu, weights, tail, first_in, qs, os, mid, s_in):
+        loads = [
+            pltpu.make_async_copy(r.g, gs, s_in.at[0]),
+            pltpu.make_async_copy(r.u, us, s_in.at[1]),
+        ]
+        for copy in loads:
+            copy.start()
+        for m, (copy, ref) in enumerate(zip(loads, (gs, us))):
+            copy.wait()
+            for zq, cq, run, first in segments(nx, fs):
+                gu[zq, cq, m, :, run : run + fs] = ref[:, first : first + fs]
+        keep = pltpu.make_async_copy(gu.at[z, c], guo.at[:, y, z, x, c], r.s_local.at[3])
+        keep.start()
+        for k in range(NZ - 1):
+            zq = line_order(z, k)
+            slot, sem = ao.at[y, zq, x, c], r.ra.at[y, zq, x, c]
+            wires.arrived(slot, sem, sib)
+            onward = jnp.where(zq < z, jnp.minimum(z + 1, NZ - 1), jnp.maximum(z - 1, 0))
+            wires.send(slot, slot, sem, {"z": onward}, lambda: inner)
+            both_ways(slot, slot, sem)
+            wires.send(slot, slot, sem, sib)
+        mark = len(wires.started)
+        for k in range(NZ * NC - 1):
+            zp, cp = remote_order(k)
+            wires.send(
+                gu.at[zp, cp], guo.at[:, y, z, x, c], r.rt.at[z, c], {"z": zp, "c": cp}
+            )
+        block_sends = wires.started[mark:]
+        del wires.started[mark:]
+        line.begin()
+        for zq in range(NZ):
+            for xp in xpeers:
+                relay_attn(y, xp, zq, [ypeer] if zq < NZ // 2 else [])
+            relay_attn(1 - y, x, zq, planes[:-1] if zq >= NZ // 2 else [])
+        both_ways(r.d.at[:, parts[0]], down_at(y, x, parts[0]), r.rd.at[0, y, x])
+        for xp in xpeers:
+            for zq in range(NZ):
+                relay_attn(1 - y, xp, zq, [])
+        locals_[0].wait()
+        for yq in range(2):
+            for zq in range(NZ):
+                for xq in range(nx):
+                    wires.arrived(ao.at[yq, zq, xq, other], r.ra.at[yq, zq, xq, other], sib)
+
+        def fetch(first, width):
+            return pltpu.make_async_copy(
+                ao.at[:, :, :, :, :, pl.ds(first, width)],
+                weights.at[:, :, :, :, :, pl.ds(0, width)],
+                s_in.at[0],
+            )
+
+        tail_copy = pltpu.make_async_copy(
+            ao.at[:, :, :, :, :, pl.ds(qkv_width + wide, HD)], tail, s_in.at[1]
+        )
+        tail_copy.start()
+        fetch(0, qkv_width).start()
+        x32 = r.x[...].astype(F32)
+        tail_copy.wait()
+        lane = lax.broadcasted_iota(jnp.int32, (16, HD), 1)
+        row = lax.broadcasted_iota(jnp.int32, (16, HD), 0)
+        pick = (lane == row).astype(F32).astype(BF16)
+        flat_tail = tail[...].reshape(-1, HD)
+        gains = dot_nt(pick, flat_tail)
+        gain_one, gain_two = gains[0:1], gains[1:2]
+        low = lax.broadcasted_iota(jnp.int32, (8, HD), 1) < HD // 2
+        pieces = []
+        tops = [
+            tail[yq, zq, xq, cq, 0:8].astype(F32)
+            for yq in range(2)
+            for zq in range(NZ)
+            for xq in range(nx)
+            for cq in range(NC)
+        ]
+        for i in range(0, len(tops), 2):
+            pieces.append(jnp.where(low, pltpu.roll(tops[i], HD // 2, 1), tops[i + 1])[0:1])
+        bias = jnp.concatenate(pieces, axis=1)
+        rescale = lax.rsqrt(jnp.mean(x32 * x32, axis=-1, keepdims=True) + EPS)
+        first_in[...] = (x32 * rescale * gain_one).astype(BF16)
+        fetch(0, qkv_width).wait()
+
+        def turn(value):
+            return value * r.turn_c[...] - pltpu.roll(value, HD // 2, 1) * r.turn_s[...]
+
+        kv_own = pl.ds(pl.multiple_of(y * rows, rows), rows)
+        pre = dot(first_in[...], weights[:, :, :, :, :, q_width:].reshape(wide, 2 * key_width))
+        pre = pre + bias[:, q_width:]
+        kv_heads = key_width // HD
+        for i in range(2 * kv_heads):
+            value = pre[:, i * HD : (i + 1) * HD]
+            if i < kv_heads:
+                value = turn(value)
+            r.kvs[kv_own, i * HD : (i + 1) * HD] = value.astype(BF16)
+        wires.send(r.kvs.at[kv_own], r.kvs.at[kv_own], r.s_kv, ypeer)
+        pre = dot(first_in[...], weights[:, :, :, :, :, :q_width].reshape(wide, q_width))
+        pre = pre + bias[:, :q_width]
+        heads = q_width // HD
+        for i in range(heads):
+            cols = slice(i * HD, (i + 1) * HD)
+            qs[:, cols] = turn(pre[:, cols]).astype(BF16)
+        fetch(qkv_width, wide).start()
+        for k in range(NZ * NC - 1):
+            zp, cp = remote_order(k)
+            wires.arrived(guo.at[:, y, zp, x, cp], r.rt.at[zp, cp], sib)
+        keep.wait()
+        for m in range(2):
+            plane = guo.at[m, y, :, x]
+            both_ways(plane, plane, r.rw.at[m, y, x])
+        both_ways(r.d.at[:, parts[1]], down_at(y, x, parts[1]), r.rd.at[1, y, x])
+        kv_other = r.kvs.at[pl.ds(pl.multiple_of((1 - y) * rows, rows), rows)]
+        wires.arrived(kv_other, r.s_kv, ypeer)
+        saves = [
+            pltpu.make_async_copy(qs, r.q_out, s_in.at[1]),
+            pltpu.make_async_copy(r.kvs, r.kv_out, s_in.at[2]),
+            pltpu.make_async_copy(os, r.o_out, s_in.at[3]),
+            pltpu.make_async_copy(mid, r.mid_out, s_in.at[4]),
+        ]
+        saves[0].start()
+        saves[1].start()
+        scale = HD ** (-0.5)
+        group = heads // kv_heads
+        for kv_head in range(kv_heads):
+            k_cols = pl.ds(kv_head * HD, HD)
+            v_cols = pl.ds(key_width + kv_head * HD, HD)
+
+            def head(i, carry):
+                cols = pl.ds(pl.multiple_of((kv_head * group + i) * HD, HD), HD)
+                scores = dot_nt(qs[:, cols], r.kvs[:, k_cols]) * scale
+                scores = jnp.where(r.mask[...] > 0, scores, MASKED)
+                exponent = jnp.exp(scores - jnp.max(scores, axis=-1, keepdims=True))
+                probs = exponent / jnp.sum(exponent, axis=-1, keepdims=True)
+                os[:, cols] = dot(probs.astype(BF16), r.kvs[:, v_cols]).astype(BF16)
+                return carry
+
+            lax.fori_loop(0, group, head, 0)
+            if kv_head == 0:
+                line.event(0)
+                for xp in xpeers:
+                    relay(down_at(y, xp, parts[0]), r.rd.at[0, y, xp], [ypeer])
+                relay(down_at(1 - y, x, parts[0]), r.rd.at[0, 1 - y, x], [])
+        saves[2].start()
+        fetch(qkv_width, wide).wait()
+        for_out = weights[:, :, :, :, :, :wide].reshape(q_width, wide)
+        middle = x32 + dot(os[...], for_out)
+        mid[...] = middle
+        saves[3].start()
+        rescale_two = lax.rsqrt(jnp.mean(middle * middle, axis=-1, keepdims=True) + EPS)
+        hv[block(z, c)] = (middle * rescale_two * gain_two).astype(BF16)
+        pl.when(z < NZ - 1)(send_own(0).start)
+        pl.when(z > 0)(send_own(1).start)
+        send_own(2).start()
+        wires.finish(block_sends)
+        for copy in saves:
+            copy.wait()
+
+    block_shape = (shard, units)
+    grid = (2, NZ, nx, NC)
+    pl.run_scoped(
+        attention,
+        pltpu.VMEM(r.g.shape, BF16),
+        pltpu.VMEM(r.u.shape, BF16),
+        pltpu.VMEM((NZ, NC, 2) + block_shape, BF16),
+        pltpu.VMEM(grid + (shard, qkv_width), BF16),
+        pltpu.VMEM(grid + (shard, HD), BF16),
+        pltpu.VMEM((rows, wide), BF16),
+        pltpu.VMEM((rows, q_width), BF16),
+        pltpu.VMEM((rows, q_width), BF16),
+        pltpu.VMEM((rows, wide), F32),
+        pltpu.SemaphoreType.DMA((5,)),
+    )
+
+    def feed_forward(cv, wgv, wuv, wdv, av, dgv, duv, part, ob, *half_own):
+        line.event(1)
+        for xp in xpeers:
+            relay(guo.at[0, y, :, xp], r.rw.at[0, y, xp], [ypeer])
+        relay(guo.at[1, 1 - y, :, x], r.rw.at[1, 1 - y, x], planes[:-1])
+        for xp in xpeers:
+            relay(down_at(y, xp, parts[1]), r.rd.at[1, y, xp], [])
+        relay(down_at(1 - y, x, parts[1]), r.rd.at[1, 1 - y, x], planes[:-1])
+        for copy in locals_[1:]:
+            copy.wait()
+
+        def load_cot(zq, cq):
+            return pltpu.make_async_copy(co.at[zq, cq], cv.at[block(zq, cq)], r.s_cot.at[zq, cq])
+
+        load_cot(z, c).start()
+        line.sibling(z)
+        load_cot(z, other).start()
+        for xp in xpeers:
+            relay(guo.at[1, y, :, xp], r.rw.at[1, y, xp], [])
+        relay(guo.at[0, 1 - y, :, x], r.rw.at[0, 1 - y, x], [])
+        for xp in xpeers:
+            for h in range(2):
+                relay(guo.at[h, 1 - y, :, xp], r.rw.at[h, 1 - y, xp], [])
+                relay(down_at(1 - y, xp, parts[h]), r.rd.at[h, 1 - y, xp], [])
+        loads = [
+            pltpu.make_async_copy(guo.at[0], wgv, r.s_load.at[0]),
+            pltpu.make_async_copy(guo.at[1], wuv, r.s_load.at[1]),
+            pltpu.make_async_copy(r.do, wdv, r.s_load.at[2]),
+        ]
+        for copy in loads:
+            copy.start()
+        line.event(2)
+
+        def arrival(zq, cq):
+            here = hv.at[block(zq, cq)]
+            return remote(here, here, r.h_send.at[0], r.h_recv.at[zq, cq], sib)
+
+        def onward(k):
+            zq = line_order(z, k)
+            here = hv.at[block(zq, c)]
+            device = {
+                "z": jnp.where(zq < z, jnp.minimum(z + 1, NZ - 1), jnp.maximum(z - 1, 0))
+            }
+            return remote(here, here, r.h_on.at[k], r.h_recv.at[zq, c], device)
+
+        def to_sibling(k):
+            zq = line_order(z, k)
+            here = hv.at[block(zq, c)]
+            return remote(here, here, r.h_sib.at[k], r.h_recv.at[zq, c], sib)
+
+        def take(k):
+            arrival(line_order(z, k), c).wait_recv()
+            pl.when(inner)(onward(k).start)
+            to_sibling(k).start()
+
+        def output(zq):
+            here = pl.ds(pl.multiple_of(zq * rows, rows), rows)
+            return pltpu.make_async_copy(ob.at[c], r.out_own.at[here], r.s_ob)
+
+        def output_over(zq):
+            here = pl.ds(pl.multiple_of(zq * rows, rows), rows)
+            return remote(ob.at[other], r.out_sib.at[here], r.o_send.at[zq], r.o_recv.at[zq], sib)
+
+        def partial_over(zq):
+            return remote(
+                part.at[block(zq, other)], r.sib.at[zq], r.p_send.at[zq], r.p_recv.at[zq], sib
+            )
+
+        def partial_home(zq):
+            j = (z - zq + NZ) % NZ - 1
+            return remote(
+                part.at[block(zq, c)], r.ring.at[j], r.r_send.at[zq], r.r_recv.at[j], {"z": zq}
+            )
+
+        piece = rows // 8
+
+        def combine(zq):
+            remote(r.sib.at[zq], r.sib.at[zq], r.p_send.at[0], r.p_recv.at[zq], sib).wait_recv()
+
+            def step(i, carry):
+                here = pl.ds(pl.multiple_of((zq * NC + c) * rows + i * piece, piece), piece)
+                there = pl.ds(pl.multiple_of(i * piece, piece), piece)
+                total = part[here].astype(F32) + r.sib[zq, there].astype(F32)
+                part[here] = total.astype(BF16)
+                return carry
+
+            lax.fori_loop(0, 8, step, 0)
+
+        def place_of(k):
+            far = jnp.where(k == 2, line_order(z, 1), line_order(z, 2))
+            return jnp.where(k == 0, z, jnp.where(k == 1, line_order(z, 0), far))
+
+        def flat(ref, low, high):
+            return ref[:, :, :, :, :, low:high].reshape(wide, high - low)
+
+        def pair(k, carry):
+            zq = place_of(k)
+
+            @pl.when(k == 0)
+            def _():
+                for i in range(NZ - 1):
+                    near = line_order(z, i)
+                    load_cot(near, c).start()
+                    line.sibling(near)
+                    load_cot(near, other).start()
+
+            @pl.when(k == 1)
+            def _():
+                take(0)
+                pl.when(inner)(lambda: take(1))
+
+            @pl.when(k == 2)
+            def _():
+                pl.when(jnp.logical_not(inner))(lambda: take(1))
+                pl.when(inner)(lambda: take(2))
+
+            @pl.when((k == 3) & jnp.logical_not(inner))
+            def _():
+                take(2)
+
+            def one(j, carry):
+                cq = (c + j) % NC
+                here = block(zq, cq)
+
+                @pl.when((k == 0) & (j == 0))
+                def _():
+                    for copy in loads:
+                        copy.wait()
+
+                @pl.when(j == 1)
+                def _():
+                    arrival(zq, cq).wait_recv()
+
+                load_cot(zq, cq).wait()
+                for low, high in TILES:
+                    high = units if high is None else high
+                    gate = dot(hv[here], flat(wgv, low, high))
+                    up = dot(hv[here], flat(wuv, low, high))
+                    grad = dot_nt(cv[here], wdv[low:high])
+                    sig = jax.nn.sigmoid(gate)
+                    act = gate * sig
+                    av[here, low:high] = (act * up).astype(BF16)
+                    duv[here, low:high] = (grad * act).astype(BF16)
+                    dgv[here, low:high] = (
+                        grad * up * (sig * (1.0 + gate * (1.0 - sig)))
+                    ).astype(BF16)
+
+                @pl.when((k > 0) & (j == 0))
+                def _():
+                    output(zq).wait()
+
+                @pl.when((k > 0) & (j == 1))
+                def _():
+                    output_over(place_of(k - 1)).wait_send()
+
+                ob[cq] = dot(av[here], wdv[...]).astype(BF16)
+                pl.when(j == 0)(output(zq).start)
+                pl.when(j == 1)(output_over(zq).start)
+                part[here] = (
+                    dot_nt(dgv[here], flat(wgv, 0, units)) + dot_nt(duv[here], flat(wuv, 0, units))
+                ).astype(BF16)
+                return carry
+
+            lax.fori_loop(0, NC, one, 0)
+            partial_over(zq).start()
+
+            @pl.when(k > 1)
+            def _():
+                before = place_of(k - 1)
+                combine(before)
+                partial_home(before).start()
+
+            return carry
+
+        lax.fori_loop(0, NZ, pair, 0)
+        last = line_order(z, NZ - 2)
+        step_d = wide // 6
+
+        def down_grad(t, carry):
+            cols = pl.ds(pl.multiple_of(t * step_d, step_d), step_d)
+            wdv[:, cols] = dot_tn(av[...], cv[:, cols]).astype(BF16)
+
+            @pl.when(t == 0)
+            def _():
+                combine(last)
+                partial_home(last).start()
+
+            return carry
+
+        lax.fori_loop(0, 6, down_grad, 0)
+        outs = [
+            pltpu.make_async_copy(wdv, r.grad_d, r.s_out.at[0]),
+            pltpu.make_async_copy(wgv, r.grad_g, r.s_out.at[1]),
+            pltpu.make_async_copy(wuv, r.grad_u, r.s_out.at[2]),
+        ]
+        outs[0].start()
+
+        def term(yq, xq, cols):
+            first = pl.multiple_of((yq * nx + xq) * down_rows, 8)
+            return r.grad_d.at[pl.ds(first, down_rows), cols]
+
+        along_x, along_y = ("x", nx, x), ("y", 2, y)
+        by_x = PlaneScatter(
+            wires,
+            lambda xq, yq: term(yq, xq, parts[0]),
+            along_x,
+            along_y,
+            (r.xr1, half_own[0], r.xr2, r.xs1, r.xsl, r.xs2),
+        )
+        by_y = PlaneScatter(
+            wires,
+            lambda yq, xq: term(yq, xq, parts[1]),
+            along_y,
+            along_x,
+            (r.yr1, half_own[1], r.yr2, r.ys1, r.ysl, r.ys2),
+        )
+        step_g = wide // NZ
+
+        def turned(src, dst, first, last):
+            def step(t, carry):
+                cols = pl.ds(pl.multiple_of(t * step_g, step_g), step_g)
+                value = dot_tn(hv[:, cols], src[...]).astype(BF16)
+                here = pl.ds((t % 2) * (NZ // 2), NZ // 2)
+                dst[t // 2, here] = value.reshape((NZ // 2, nx, NC, shard, units))
+                return carry
+
+            lax.fori_loop(first, last, step, 0)
+
+        turned(dgv, wgv, 0, 1)
+        outs[0].wait()
+        by_x.begin()
+        by_y.begin()
+        turned(dgv, wgv, 1, NZ)
+        outs[1].start()
+        turned(duv, wuv, 0, NZ)
+        outs[2].start()
+        by_x.relay()
+        by_y.relay()
+        combine(z)
+        for j in range(NZ - 1):
+            here = r.ring.at[j]
+            remote(here, here, r.r_send.at[0], r.r_recv.at[j], sib).wait_recv()
+
+        def final(i, carry):
+            here = pl.ds(pl.multiple_of((z * NC + c) * rows + i * piece, piece), piece)
+            there = pl.ds(pl.multiple_of(i * piece, piece), piece)
+            total = part[here].astype(F32)
+            for j in range(NZ - 1):
+                total = total + r.ring[j, there].astype(F32)
+            r.dh[there] = total
+            return carry
+
+        lax.fori_loop(0, 8, final, 0)
+        by_x.finish(r.down_out.at[:, parts[0]])
+        by_y.finish(r.down_out.at[:, parts[1]])
+        wires.finish()
+        pl.when(z < NZ - 1)(send_own(0).wait_send)
+        pl.when(z > 0)(send_own(1).wait_send)
+        send_own(2).wait_send()
+        for k in range(NZ - 1):
+            pl.when(inner)(onward(k).wait_send)
+            to_sibling(k).wait_send()
+            partial_home(line_order(z, k)).wait_send()
+        for zq in range(NZ):
+            partial_over(zq).wait_send()
+        output(last).wait()
+        output_over(last).wait_send()
+        for zq in range(NZ):
+            there = r.out_sib.at[pl.ds(zq * rows, rows)]
+            remote(there, there, r.o_send.at[0], r.o_recv.at[zq], sib).wait_recv()
+        for copy in outs[1:]:
+            copy.wait()
+
+    every = NZ * NC * rows
+    pl.run_scoped(
+        feed_forward,
+        pltpu.VMEM((every, wide), BF16),
+        pltpu.VMEM(grid + block_shape, BF16),
+        pltpu.VMEM(grid + block_shape, BF16),
+        pltpu.VMEM((units, wide), BF16),
+        pltpu.VMEM((every, units), BF16),
+        pltpu.VMEM((every, units), BF16),
+        pltpu.VMEM((every, units), BF16),
+        pltpu.VMEM((every, wide), BF16),
+        pltpu.VMEM((NC, rows, wide), BF16),
+        pltpu.VMEM((2, down_rows, half), BF16),
+        pltpu.VMEM((nx, down_rows, half), BF16),
+    )
+
+
+def forward(ny, nx, b_rows, a, g, u, d, tok, x, mask, turn_c, turn_s, widths, collective_id):
+    hbm = pl.BlockSpec(memory_space=pl.ANY)
+    vmem = pl.BlockSpec(memory_space=pltpu.VMEM)
+    dma = pltpu.SemaphoreType.DMA
+    rows, wide = tok.shape
+    q_width, key_width = widths
+    shard = a.shape[0]
+    units = g.shape[1] // (NZ * NC)
+    grid = (ny, NZ, nx, NC)
+    half_slot = (d.shape[0], wide // 2)
+    ins = dict(a=a, g=g, u=u, d=d, tok=tok, x=x, mask=mask, turn_c=turn_c, turn_s=turn_s)
+    outs = dict(
+        ao=(grid + a.shape, BF16),
+        guo=((2,) + grid + (shard, units), BF16),
+        do=((units, wide), BF16),
+        co=((NZ, NC, rows, wide), BF16),
+        q_out=((rows, q_width), BF16),
+        kv_out=((2 * rows, 2 * key_width), BF16),
+        o_out=((rows, q_width), BF16),
+        mid_out=((rows, wide), F32),
+        out_own=((NZ * rows, wide), BF16),
+        out_sib=((NZ * rows, wide), BF16),
+        grad_g=(grid + (shard, units), BF16),
+        grad_u=(grid + (shard, units), BF16),
+        grad_d=((units, wide), BF16),
+        dh=((rows, wide), F32),
+        down_out=(d.shape, BF16),
+    )
+    plane_x = plane_scratch(half_slot, nx, ny)
+    plane_y = plane_scratch(half_slot, ny, nx)
+    one_plane = (nx - 1) * 2 + 1 + nx + (nx - 1)
+    sends = 3 + nx + 3 * (nx + 2) + 7 + 9 + 4 * (2 * nx - 1) + 4 * nx + 6 * nx
+    scratch = dict(
+        send_sems=dma((sends + 2 * one_plane + 24,)),
+        s_local=dma((4,)),
+        ra=dma(grid),
+        rt=dma((NZ, NC)),
+        rw=dma((2, ny, nx)),
+        rd=dma((2, ny, nx)),
+        rc=dma((NZ, NC)),
+        s_kv=dma,
+        kvs=pltpu.VMEM((2 * rows, 2 * key_width), BF16),
+        hv=pltpu.VMEM((NZ * NC * rows, wide), BF16),
+        sib=pltpu.VMEM((NZ, rows, wide), BF16),
+        ring=pltpu.VMEM((NZ - 1, rows, wide), BF16),
+        s_load=dma((3,)),
+        s_cot=dma((NZ, NC)),
+        s_ob=dma,
+        s_out=dma((3,)),
+        h_send=dma((3,)),
+        h_on=dma((NZ - 1,)),
+        h_sib=dma((NZ - 1,)),
+        h_recv=dma((NZ, NC)),
+        p_send=dma((NZ,)),
+        p_recv=dma((NZ,)),
+        r_send=dma((NZ,)),
+        r_recv=dma((NZ - 1,)),
+        o_send=dma((NZ,)),
+        o_recv=dma((NZ,)),
+        xr1=plane_x[0],
+        xr2=plane_x[2],
+        xs1=plane_x[3],
+        xsl=plane_x[4],
+        xs2=plane_x[5],
+        yr1=plane_y[0],
+        yr2=plane_y[2],
+        ys1=plane_y[3],
+        ysl=plane_y[4],
+        ys2=plane_y[5],
+    )
+    names = tuple(ins) + tuple(outs) + tuple(scratch)
+    results = pl.pallas_call(
+        lambda *refs: forward_kernel(nx, b_rows, names, *refs),
+        name="forward",
+        out_shape=tuple(jax.ShapeDtypeStruct(*shape) for shape in outs.values()),
+        in_specs=[hbm] * 5 + [vmem] * 4,
+        out_specs=(hbm,) * 13 + (vmem,) * 2,
+        scratch_shapes=list(scratch.values()),
+        compiler_params=pltpu.CompilerParams(
+            collective_id=collective_id, has_side_effects=True, vmem_limit_bytes=67_043_328
+        ),
+    )(*ins.values())
+    return types.SimpleNamespace(**dict(zip(outs, results)))
 
 
 def plane_peers(nx, y, x):
@@ -1422,6 +2068,76 @@
 
 
 def make_body(ny, nx):
+    def fused_layer(packed, x, seg_all, gate, up, down, grad_out, widths, b_rows):
+        tok_rows = x.shape[0]
+        length = seg_all.shape[0]
+        seq_place = lax.axis_index("y")
+        tok_pos = seq_place * tok_rows + jnp.arange(tok_rows)
+        cos_tok, sin_tok = tables(tok_pos)
+        all_pos = jnp.arange(length)
+        seg_tok = lax.dynamic_slice(seg_all, (seq_place * tok_rows,), (tok_rows,))
+        allowed = (tok_pos[:, None] >= all_pos[None, :]) & (seg_tok[:, None] == seg_all[None, :])
+        mask = allowed.astype(F32)
+        turn_c = jnp.concatenate([cos_tok, cos_tok], axis=1)
+        turn_s = jnp.concatenate([sin_tok, -sin_tok], axis=1)
+        made = forward(
+            ny, nx, b_rows, packed, gate, up, down, grad_out, x, mask, turn_c, turn_s, widths, 0
+        )
+        lanes = sum(widths) + widths[1] + x.shape[1]
+        tail = made.ao[..., lanes : lanes + 2].astype(F32).reshape(-1, 2)
+        gain_one, gain_two = tail[:, 0], tail[:, 1]
+        middle = made.mid_out
+        rescale_two = lax.rsqrt(jnp.mean(middle * middle, axis=-1, keepdims=True) + EPS)
+        normed_two = middle * rescale_two
+        scaled = made.dh * gain_two
+        grad_mid = grad_out.astype(F32) + rescale_two * (
+            scaled - normed_two * jnp.mean(scaled * normed_two, axis=-1, keepdims=True)
+        )
+        args = (
+            grad_mid,
+            grad_mid.astype(BF16),
+            x,
+            gain_one[None],
+            made.o_out,
+            made.q_out,
+            made.kv_out,
+            mask,
+            turn_c,
+            turn_s,
+            (made.dh * normed_two).astype(BF16),
+        )
+        outs = back(
+            ny,
+            nx,
+            b_rows,
+            made.grad_g,
+            made.grad_u,
+            made.ao.reshape((-1,) + packed.shape),
+            made.out_own,
+            made.out_sib,
+            args,
+            1,
+        )
+        grad_q, grad_k, grad_v, grad_o, tail_sum, grad_gate_w, grad_up_w, grad_in, ring = outs
+        first_row = lax.axis_index("z") * tok_rows
+        out_sum = jnp.sum(ring.astype(F32), axis=0)
+        for half in (made.out_own, made.out_sib):
+            out_sum += lax.dynamic_slice_in_dim(half, first_row, tok_rows).astype(F32)
+        return (
+            (middle + out_sum).astype(BF16)[None],
+            grad_in[None],
+            tail_sum[:, 0],
+            grad_q,
+            grad_k,
+            grad_v,
+            tail_sum[0, HD // 2 : HD // 2 + b_rows],
+            grad_o,
+            tail_sum[:, 1],
+            grad_gate_w.astype(F32),
+            grad_up_w.astype(F32),
+            made.down_out.astype(F32),
+        )
+
     def body(
         inputs,
         segment_ids,
@@ -1458,12 +2174,26 @@
             [
                 attn_gain[:, None],
                 mlp_gain[:, None],
+                jnp.zeros((g_rows, HD // 2 - 2), BF16),
                 jnp.broadcast_to(qkv_bias[None], (g_rows, b_rows)),
-                jnp.zeros((g_rows, HD - 2 - b_rows), BF16),
+                jnp.zeros((g_rows, HD // 2 - b_rows), BF16),
             ],
             axis=1,
         )
         packed = jnp.concatenate([q_weight, k_weight, v_weight, o_weight, extra], axis=1)
+        fused = g_rows % 16 == 0 and b_rows == HD // 2
+        if fused:
+            return fused_layer(
+                packed,
+                inputs[0],
+                seg_all,
+                gate_weight,
+                up_weight,
+                down_weight,
+                grad_out,
+                (query_width, key_width),
+                b_rows,
+            )
         attn_all, columns_all, down_all, grad_out_all = weight_gather(
             ny,
             nx,
@@ -1480,7 +2210,7 @@
         tail = attn_all[..., qkv_width + query_width :].astype(F32)
         gain_one = tail[..., 0].reshape(-1)
         gain_two = tail[..., 1].reshape(-1)
-        bias = tail[..., 0, 2 : 2 + b_rows].reshape(-1)
+        bias = tail[..., 0, HD // 2 : HD // 2 + b_rows].reshape(-1)
         width = gate_weight.shape[1] // (NZ * NC)
         full_gate = columns_all[0].reshape(-1, width)
         full_up = columns_all[1].reshape(-1, width)
@@ -1520,60 +2250,12 @@
         normed_two = middle * rescale_two
         input_two = (normed_two * gain_two).astype(BF16)
         by_shard = (ny, NZ, nx, NC, g_rows, width)
-        fused = g_rows % 16 == 0
         grad_input_two, out_part, part_gate, part_up, *downs = mlp(
-            ny, nx, fused, input_two, full_gate, full_up, full_down, grad_out_all, 1
+            ny, nx, False, input_two, full_gate, full_up, full_down, grad_out_all, 1
         )
         grad_gain_two, grad_mid = norm_back(grad_input_two, normed_two, rescale_two, gain_two)
         grad_mid = grad_mid + grad_out.astype(F32)
         grad_branch = grad_mid.astype(BF16)
-        if fused:
-            args = (
-                grad_mid,
-                grad_branch,
-                inputs[0],
-                gain_one[None],
-                attn_tok,
-                query,
-                kv_all,
-                allowed.astype(F32),
-                jnp.concatenate([cos_tok, cos_tok], axis=1),
-                jnp.concatenate([sin_tok, -sin_tok], axis=1),
-                (grad_input_two * normed_two).astype(BF16),
-            )
-            outs = back(
-                ny,
-                nx,
-                b_rows,
-                part_gate.reshape(by_shard),
-                part_up.reshape(by_shard),
-                attn_all.reshape((-1,) + packed.shape),
-                out_part,
-                downs[2],
-                args,
-                3,
-            )
-            grad_q, grad_k, grad_v, grad_o, tail_sum, grad_gate_w, grad_up_w = outs[:7]
-            grad_in, ring = outs[7:]
-            first_row = lax.axis_index("z") * tok_rows
-            out_sum = jnp.sum(ring.astype(F32), axis=0)
-            for half in (out_part, downs[2]):
-                out_sum += lax.dynamic_slice_in_dim(half, first_row, tok_rows).astype(F32)
-            output = (middle + out_sum).astype(BF16)[None]
-            return (
-                output,
-                grad_in[None],
-                tail_sum[:, 0],
-                grad_q,
-                grad_k,
-                grad_v,
-                tail_sum[0, HD // 2 : HD // 2 + b_rows],
-                grad_o,
-                tail_sum[:, 1],
-                grad_gate_w.astype(F32),
-                grad_up_w.astype(F32),
-                downs[1].astype(F32),
-            )
         grad_attn = dot_nt(grad_branch, full_out).astype(BF16)
         grad_heads = grad_attn.reshape(tok_rows, kv_heads, group, HD)
         grad_probs = jnp.einsum(

time: 536 us -> 471 us (0.88); the launches traced: 528 us -> 468 us
  blocking collectives: 17.8 us -> 0 us
  matrix products: 16.6 us -> 0 us
  local copies, waits for them, and re-layouts: 27.1 us -> 15.1 us
  other arithmetic: 22.4 us -> 16.3 us
  Pallas kernels: 442 us -> 436 us
    all_gather x1 -> x0, blocking collectives: 17.8 us -> none  [body(): kv_all = lax.all_gather(kv, 'y', axis=0, tiled=True)]
    dot_general x3 -> x0, matrix products: 11.8 us -> none  [the longest x2 8.45 us: dot(): return jnp.dot(a, b, preferred_element_type=F32)]
    slice x9 -> x4, local copies, waits for them, and re-layouts: 9.66 us -> 3.16 us  [the longest x2 1.43 us: fused_layer(): gain_one, gain_two = (tail[:, 0], tail[:, 1])]
    pallas_call x2 -> x1, Pallas kernels: 292 us -> 288 us  [forward(): pl.pallas_call(lambda *refs: forward_kernel(nx, b_rows, names, *refs), na...]
where the time goes in v5:
time: 471 us; the launch traced here: 468 us
  Pallas kernels  436 us (93%)
  other arithmetic  16.3 us (3%)
  local copies, waits for them, and re-layouts  15.1 us (3%)
    pallas_call x1, Pallas kernels, forward(): pl.pallas_call(lambda *refs: forward_kernel(nx, b_rows, names, *refs), na...  288 us
    pallas_call x1, Pallas kernels, back(): pl.pallas_call(lambda *refs: back_kernel(nx, key_width, b_rows, *refs), n...  148 us

profile of v5, /device:TPU:0, one launch (start us, length us, event | category | flops | bytes accessed | tf_op | source)
XLA Modules:
  0.0 468.2 jit_solution(4322694646311440837)
XLA Ops:
  0.7 0.7 constant_dynamic-slice_fusion
  1.4 0.8 copy.27
  2.8 0.8 copy.28
  3.6 1.8 concatenate.9.refs_0_
  6.0 0.8 pad_maximum_fusion.1.refs_8_.refs_14_
  6.7 0.8 pad_maximum_fusion.refs_7_.refs_13_
  7.5 0.9 fusion.2.refs_6_.refs_12_
  8.4 288.5 %forward.1 = (bf16[2,4,2,2,48,3712]{5,4,3,2,1,0:T(8,128)(2,1)}, bf16[2,2,4,2,2,48,1120]{6,5,4,3,2,1,0:T(8,128)(2,1)}, bf16[1120,1536]{1,0:T(8,128)(2,1)}, bf16[4...) custom-call(bf16[48,3712]{1,0:T(8,128)(2,1)} %concatenate.9.refs_0_,, ...), custom_call_target="tpu_custom_call" | custom-call | tf_op jit(solution)/shard_map/forward/pallas_call | solution.py:1531
  296.9 1.6 multiply_reduce_fusion.1
  298.5 1.0 slice.18
  299.6 0.9 slice.25
  300.5 2.1 copy.32
  303.6 0.8 copy-done.3
  304.3 2.2 fusion.5
  306.6 147.5 %back.1 = (f32[48,1536]{1,0:T(8,128)}, f32[48,256]{1,0:T(8,128)}, f32[48,256]{1,0:T(8,128)}, f32[48,1536]{1,0:T(8,128)}, f32[48,128]{1,0:T(8,128)}, /*index=5*/b...) custom-call(bf16[2,4,2,2,48,1120]{5,4,3,2,1,0:T(8,128)(2,1)} %get-tuple-elem, ...), custom_call_target="tpu_custom_call" | custom-call | flops 99999997952 | bytes 100000000 | tf_op jit(solution)/shard_map/back/pallas_call | solution.py:2020
  454.1 2.3 convert_reduce_fusion
  456.5 2.8 fusion
  459.8 0.7 slice_reduce_fusion.1
  460.5 1.3 convert_element_type.58
  461.8 1.3 convert_element_type.59
  463.3 1.4 convert_element_type.60
  464.7 0.9 copy.39
  465.6 0.7 copy.40
  467.5 0.7 copy.43
  (40 shorter events, 4.1 us)
Async XLA Ops:
  0.6 6.9 %copy-start.13 = (s32[1,512]{1,0:T(1,128)S(1)}, s32[1,512]{1,0:T(1,128)}, u32[]{:S(2)}) copy-start(s32[1,512]{1,0:T(1,128)} %param.14) | copy-start | bytes 6148
  299.6 3.6 copy-start.2
  300.5 2.7 copy-start
  303.2 1.1 copy-start.3
  454.1 2.3 copy-start.1
  456.4 2.8 copy-start.10
  456.4 4.1 copy-start.6
  459.2 2.6 copy-start.5
  461.8 1.5 copy-start.4
  463.3 1.4 copy-start.7
  463.3 2.3 copy-start.9
  464.7 1.6 copy-start.12
  464.7 2.2 copy-start.11
  464.7 2.9 copy-start.8

commit v6 on v5

--- a/solution.py
+++ b/solution.py
@@ -1031,7 +1031,8 @@
             for xp in xpeers:
                 relay_attn(y, xp, zq, [ypeer] if zq < NZ // 2 else [])
             relay_attn(1 - y, x, zq, planes[:-1] if zq >= NZ // 2 else [])
-        both_ways(r.d.at[:, parts[0]], down_at(y, x, parts[0]), r.rd.at[0, y, x])
+        for h in range(2):
+            both_ways(r.d.at[:, parts[h]], down_at(y, x, parts[h]), r.rd.at[h, y, x])
         for xp in xpeers:
             for zq in range(NZ):
                 relay_attn(1 - y, xp, zq, [])
@@ -1104,7 +1105,6 @@
         for m in range(2):
             plane = guo.at[m, y, :, x]
             both_ways(plane, plane, r.rw.at[m, y, x])
-        both_ways(r.d.at[:, parts[1]], down_at(y, x, parts[1]), r.rd.at[1, y, x])
         kv_other = r.kvs.at[pl.ds(pl.multiple_of((1 - y) * rows, rows), rows)]
         wires.arrived(kv_other, r.s_kv, ypeer)
         saves = [
@@ -1135,6 +1135,8 @@
                 line.event(0)
                 for xp in xpeers:
                     relay(down_at(y, xp, parts[0]), r.rd.at[0, y, xp], [ypeer])
+                    relay(down_at(y, xp, parts[1]), r.rd.at[1, y, xp], [])
+                relay(down_at(1 - y, x, parts[1]), r.rd.at[1, 1 - y, x], planes[:-1])
                 relay(down_at(1 - y, x, parts[0]), r.rd.at[0, 1 - y, x], [])
         saves[2].start()
         fetch(qkv_width, wide).wait()
@@ -1168,15 +1170,36 @@
     )
 
     def feed_forward(cv, wgv, wuv, wdv, av, dgv, duv, part, ob, *half_own):
+        def arrival(zq, cq):
+            here = hv.at[block(zq, cq)]
+            return remote(here, here, r.h_send.at[0], r.h_recv.at[zq, cq], sib)
+
+        def onward(k):
+            zq = line_order(z, k)
+            here = hv.at[block(zq, c)]
+            device = {
+                "z": jnp.where(zq < z, jnp.minimum(z + 1, NZ - 1), jnp.maximum(z - 1, 0))
+            }
+            return remote(here, here, r.h_on.at[k], r.h_recv.at[zq, c], device)
+
+        def to_sibling(k):
+            zq = line_order(z, k)
+            here = hv.at[block(zq, c)]
+            return remote(here, here, r.h_sib.at[k], r.h_recv.at[zq, c], sib)
+
+        def take(k):
+            arrival(line_order(z, k), c).wait_recv()
+            pl.when(inner)(onward(k).start)
+            to_sibling(k).start()
+
         line.event(1)
         for xp in xpeers:
             relay(guo.at[0, y, :, xp], r.rw.at[0, y, xp], [ypeer])
         relay(guo.at[1, 1 - y, :, x], r.rw.at[1, 1 - y, x], planes[:-1])
-        for xp in xpeers:
-            relay(down_at(y, xp, parts[1]), r.rd.at[1, y, xp], [])
-        relay(down_at(1 - y, x, parts[1]), r.rd.at[1, 1 - y, x], planes[:-1])
         for copy in locals_[1:]:
             copy.wait()
+        take(0)
+        pl.when(inner)(lambda: take(1))
 
         def load_cot(zq, cq):
             return pltpu.make_async_copy(co.at[zq, cq], cv.at[block(zq, cq)], r.s_cot.at[zq, cq])
@@ -1200,28 +1223,6 @@
             copy.start()
         line.event(2)
 
-        def arrival(zq, cq):
-            here = hv.at[block(zq, cq)]
-            return remote(here, here, r.h_send.at[0], r.h_recv.at[zq, cq], sib)
-
-        def onward(k):
-            zq = line_order(z, k)
-            here = hv.at[block(zq, c)]
-            device = {
-                "z": jnp.where(zq < z, jnp.minimum(z + 1, NZ - 1), jnp.maximum(z - 1, 0))
-            }
-            return remote(here, here, r.h_on.at[k], r.h_recv.at[zq, c], device)
-
-        def to_sibling(k):
-            zq = line_order(z, k)
-            here = hv.at[block(zq, c)]
-            return remote(here, here, r.h_sib.at[k], r.h_recv.at[zq, c], sib)
-
-        def take(k):
-            arrival(line_order(z, k), c).wait_recv()
-            pl.when(inner)(onward(k).start)
-            to_sibling(k).start()
-
         def output(zq):
             here = pl.ds(pl.multiple_of(zq * rows, rows), rows)
             return pltpu.make_async_copy(ob.at[c], r.out_own.at[here], r.s_ob)
@@ -1256,8 +1257,8 @@
             lax.fori_loop(0, 8, step, 0)
 
         def place_of(k):
-            far = jnp.where(k == 2, line_order(z, 1), line_order(z, 2))
-            return jnp.where(k == 0, z, jnp.where(k == 1, line_order(z, 0), far))
+            late = jnp.where(k == 2, line_order(z, 2), line_order(z, 0))
+            return jnp.where(k == 0, z, jnp.where(k == 1, line_order(z, 1), late))
 
         def flat(ref, low, high):
             return ref[:, :, :, :, :, low:high].reshape(wide, high - low)
@@ -1273,22 +1274,8 @@
                     line.sibling(near)
                     load_cot(near, other).start()
 
-            @pl.when(k == 1)
-            def _():
-                take(0)
-                pl.when(inner)(lambda: take(1))
-
-            @pl.when(k == 2)
-            def _():
-                pl.when(jnp.logical_not(inner))(lambda: take(1))
-                pl.when(inner)(lambda: take(2))
-
-            @pl.when((k == 3) & jnp.logical_not(inner))
-            def _():
-                take(2)
-
             def one(j, carry):
-                cq = (c + j) % NC
+                cq = (other + j) % NC
                 here = block(zq, cq)
 
                 @pl.when((k == 0) & (j == 0))
@@ -1296,9 +1283,18 @@
                     for copy in loads:
                         copy.wait()
 
-                @pl.when(j == 1)
+                @pl.when(j == 0)
                 def _():
                     arrival(zq, cq).wait_recv()
+
+                @pl.when((k == 0) & (j == 1))
+                def _():
+                    pl.when(jnp.logical_not(inner))(lambda: take(1))
+                    pl.when(inner)(lambda: take(2))
+
+                @pl.when((k == 1) & (j == 1) & jnp.logical_not(inner))
+                def _():
+                    take(2)
 
                 load_cot(zq, cq).wait()
                 for low, high in TILES:
@@ -1314,46 +1310,39 @@
                         grad * up * (sig * (1.0 + gate * (1.0 - sig)))
                     ).astype(BF16)
 
+                @pl.when((k > 0) & (j == 1))
+                def _():
+                    output(zq).wait()
+
                 @pl.when((k > 0) & (j == 0))
                 def _():
-                    output(zq).wait()
-
-                @pl.when((k > 0) & (j == 1))
-                def _():
                     output_over(place_of(k - 1)).wait_send()
 
                 ob[cq] = dot(av[here], wdv[...]).astype(BF16)
-                pl.when(j == 0)(output(zq).start)
-                pl.when(j == 1)(output_over(zq).start)
+                pl.when(j == 1)(output(zq).start)
+                pl.when(j == 0)(output_over(zq).start)
                 part[here] = (
                     dot_nt(dgv[here], flat(wgv, 0, units)) + dot_nt(duv[here], flat(wuv, 0, units))
                 ).astype(BF16)
+                pl.when(j == 0)(partial_over(zq).start)
                 return carry
 
             lax.fori_loop(0, NC, one, 0)
-            partial_over(zq).start()
-
-            @pl.when(k > 1)
+
+            @pl.when(k > 0)
             def _():
-                before = place_of(k - 1)
-                combine(before)
-                partial_home(before).start()
+                combine(zq)
+                partial_home(zq).start()
 
             return carry
 
         lax.fori_loop(0, NZ, pair, 0)
-        last = line_order(z, NZ - 2)
+        last = place_of(NZ - 1)
         step_d = wide // 6
 
         def down_grad(t, carry):
             cols = pl.ds(pl.multiple_of(t * step_d, step_d), step_d)
             wdv[:, cols] = dot_tn(av[...], cv[:, cols]).astype(BF16)
-
-            @pl.when(t == 0)
-            def _():
-                combine(last)
-                partial_home(last).start()
-
             return carry
 
         lax.fori_loop(0, 6, down_grad, 0)
@@ -1401,10 +1390,11 @@
         by_y.begin()
         turned(dgv, wgv, 1, NZ)
         outs[1].start()
-        turned(duv, wuv, 0, NZ)
-        outs[2].start()
+        turned(duv, wuv, 0, NZ // 2)
         by_x.relay()
         by_y.relay()
+        turned(duv, wuv, NZ // 2, NZ)
+        outs[2].start()
         combine(z)
         for j in range(NZ - 1):
             here = r.ring.at[j]

time: 471 us -> 455 us (0.966)
  Pallas kernels: 436 us -> 420 us
    pallas_call x1, Pallas kernels: 288 us -> 271 us  [forward(): pl.pallas_call(lambda *refs: forward_kernel(nx, b_rows, names, *refs), na...]
where the time goes in v6:
time: 455 us; the launch traced here: 452 us
  Pallas kernels  420 us (92%)
  other arithmetic  16.3 us (4%)
  local copies, waits for them, and re-layouts  15.1 us (3%)
    pallas_call x1, Pallas kernels, forward(): pl.pallas_call(lambda *refs: forward_kernel(nx, b_rows, names, *refs), na...  271 us
    pallas_call x1, Pallas kernels, back(): pl.pallas_call(lambda *refs: back_kernel(nx, key_width, b_rows, *refs), n...  149 us

profile of v6, /device:TPU:0, one launch (start us, length us, event | category | flops | bytes accessed | tf_op | source)
XLA Modules:
  0.0 452.0 jit_solution(359277014884469039)
XLA Ops:
  0.7 0.7 constant_dynamic-slice_fusion
  1.4 0.8 copy.27
  2.8 0.8 copy.28
  3.6 1.8 concatenate.9.refs_0_
  6.0 0.8 pad_maximum_fusion.1.refs_8_.refs_14_
  6.7 0.8 pad_maximum_fusion.refs_7_.refs_13_
  7.5 0.9 fusion.2.refs_6_.refs_12_
  8.4 270.9 %forward.1 = (bf16[2,4,2,2,48,3712]{5,4,3,2,1,0:T(8,128)(2,1)}, bf16[2,2,4,2,2,48,1120]{6,5,4,3,2,1,0:T(8,128)(2,1)}, bf16[1120,1536]{1,0:T(8,128)(2,1)}, bf16[4...) custom-call(bf16[48,3712]{1,0:T(8,128)(2,1)} %concatenate.9.refs_0_,, ...), custom_call_target="tpu_custom_call" | custom-call | tf_op jit(solution)/shard_map/forward/pallas_call | solution.py:1521
  279.3 1.6 multiply_reduce_fusion.1
  280.9 1.0 slice.18
  282.0 0.9 slice.25
  282.9 2.1 copy.32
  285.9 0.8 copy-done.3
  286.7 2.2 fusion.5
  288.9 148.9 %back.1 = (f32[48,1536]{1,0:T(8,128)}, f32[48,256]{1,0:T(8,128)}, f32[48,256]{1,0:T(8,128)}, f32[48,1536]{1,0:T(8,128)}, f32[48,128]{1,0:T(8,128)}, /*index=5*/b...) custom-call(bf16[2,4,2,2,48,1120]{5,4,3,2,1,0:T(8,128)(2,1)} %get-tuple-elem, ...), custom_call_target="tpu_custom_call" | custom-call | flops 99999997952 | bytes 100000000 | tf_op jit(solution)/shard_map/back/pallas_call | solution.py:2010
  437.9 2.3 convert_reduce_fusion
  440.3 2.8 fusion
  443.6 0.7 slice_reduce_fusion.1
  444.3 1.3 convert_element_type.58
  445.6 1.3 convert_element_type.59
  447.1 1.4 convert_element_type.60
  448.5 0.9 copy.39
  449.4 0.7 copy.40
  451.3 0.7 copy.43
  (40 shorter events, 4.1 us)
Async XLA Ops:
  0.6 6.9 %copy-start.13 = (s32[1,512]{1,0:T(1,128)S(1)}, s32[1,512]{1,0:T(1,128)}, u32[]{:S(2)}) copy-start(s32[1,512]{1,0:T(1,128)} %param.14) | copy-start | bytes 6148
  282.0 3.6 copy-start.2
  282.9 2.7 copy-start
  285.6 1.1 copy-start.3
  437.9 2.3 copy-start.1
  440.2 2.8 copy-start.10
  440.2 4.1 copy-start.6
  443.0 2.6 copy-start.5
  445.6 1.5 copy-start.4
  447.1 1.4 copy-start.7
  447.1 2.3 copy-start.9
  448.5 1.6 copy-start.12
  448.5 2.2 copy-start.11
  448.5 2.9 copy-start.8

commit v7 on v6

--- a/solution.py
+++ b/solution.py
@@ -1748,6 +1748,7 @@
     result,
     s_result,
     s_ring,
+    s_toward,
     *bufs,
 ):
     y, z, x, c = place()
@@ -1826,21 +1827,61 @@
             fill(term_o, yq, h, 0, dot_tn(attn[:, i * tile : (i + 1) * tile], branch[...]))
             over(0, term_o, sib_o, yq, h)
 
-    for i, k in enumerate((2, 0, 1)):
-        zq = line_order(z, k)
-        here = pl.ds(pl.multiple_of(zq * rows, rows), rows)
-        loads = [
-            pltpu.make_async_copy(kept.at[here], result.at[i], s_result.at[0]),
-            pltpu.make_async_copy(given.at[here], first_in, s_result.at[1]),
-        ]
-        for copy in loads:
-            copy.start()
-        for copy in loads:
-            copy.wait()
-        total_into(result.at[i], [result.at[i], first_in])
-        j = (z - zq + NZ) % NZ - 1
-        wires.send(result.at[i], out_ring.at[j], s_ring.at[j], {"z": zq})
-
+    def landing(sign, k):
+        return NZ if k == NZ - 2 else (k if sign > 0 else 2 + k)
+
+    def inside(sign, k):
+        return z + k < NZ if sign > 0 else z >= k
+
+    def toward(sign, k):
+        at = landing(sign, k - 1)
+        return remote(
+            result.at[int(sign < 0)],
+            out_ring.at[at],
+            s_toward.at[2 * (k - 1) + (sign < 0)],
+            s_ring.at[at],
+            {"z": jnp.clip(z + sign, 0, NZ - 1)},
+        )
+
+    def landed(at):
+        here = out_ring.at[at]
+        remote(here, here, s_toward.at[0], s_ring.at[at], sib).wait_recv()
+
+    def hop(k):
+        for sign in (1, -1):
+            behind = z > 0 if sign > 0 else z < NZ - 1
+            held = result.at[int(sign < 0)]
+            if k < NZ - 1:
+                pl.when(inside(sign, k + 1))(toward(sign, k + 1).wait_send)
+
+            @pl.when(inside(sign, k))
+            def _():
+                first = jnp.clip(z + sign * k, 0, NZ - 1) * rows
+                here = pl.ds(pl.multiple_of(first, rows), rows)
+                loads = [
+                    pltpu.make_async_copy(kept.at[here], held, s_result.at[0]),
+                    pltpu.make_async_copy(given.at[here], first_in, s_result.at[1]),
+                ]
+                for copy in loads:
+                    copy.start()
+                for copy in loads:
+                    copy.wait()
+                total_into(held, [held, first_in])
+
+            if k < NZ - 1:
+
+                @pl.when(inside(sign, k) & behind)
+                def _():
+                    at = landing(sign, k)
+                    landed(at)
+                    copy = pltpu.make_async_copy(out_ring.at[at], result.at[2], s_result.at[0])
+                    copy.start()
+                    copy.wait()
+                    total_into(held, [held, result.at[2]])
+
+            pl.when(inside(sign, k))(toward(sign, k).start)
+
+    hop(3)
     fetch(qkv_width, wide).wait()
     for_out = weights[:, :, :wide].reshape(q_width, wide)
     d_attn[...] = dot_nt(branch[...], for_out).astype(BF16)
@@ -1871,10 +1912,13 @@
             return carry
 
         lax.fori_loop(0, group, head, 0)
+        if kv_head == 0:
+            hop(2)
 
     other_rows = pl.ds(pl.multiple_of((1 - y) * rows, rows), rows)
     own_rows = pl.ds(pl.multiple_of(y * rows, rows), rows)
     kv_send[...] = d_kv[other_rows].astype(BF16)
+    hop(1)
     gate_plane.relay()
     wires.send(kv_send, kv_recv, s_kv, {"y": 1 - y})
     up_plane.relay()
@@ -1892,6 +1936,14 @@
         if kv_head < kv_heads:
             total = turn_back(total)
         d_qkv[:, pl.ds(q_width + kv_head * HD, HD)] = total.astype(BF16)
+    gate_plane.finish(gu.at[0])
+    up_plane.finish(gu.at[1])
+    keep_block = pltpu.make_async_copy(gu.at[:, z, c], blocks.at[z, c], s_block.at[z, c])
+    keep_block.start()
+    for k in range(NZ * NC - 1):
+        step = k + 1
+        zp, cp = (z + step // NC) % NZ, (c + step) % NC
+        wires.send(gu.at[:, zp, cp], blocks.at[z, c], s_block.at[z, c], {"z": zp, "c": cp})
     fetch(0, qkv_width).wait()
     for_in = weights[...].reshape(wide, qkv_width)
     d_first = dot_nt(d_qkv[...], for_in)
@@ -1931,14 +1983,6 @@
     q_planes = planes(term_q, 24)
     for plane in q_planes:
         plane.begin()
-    gate_plane.finish(gu.at[0])
-    up_plane.finish(gu.at[1])
-    keep_block = pltpu.make_async_copy(gu.at[:, z, c], blocks.at[z, c], s_block.at[z, c])
-    keep_block.start()
-    for k in range(NZ * NC - 1):
-        step = k + 1
-        zp, cp = (z + step // NC) % NZ, (c + step) % NC
-        wires.send(gu.at[:, zp, cp], blocks.at[z, c], s_block.at[z, c], {"z": zp, "c": cp})
     for plane in o_planes:
         plane.relay()
     for plane in q_planes:
@@ -1983,8 +2027,9 @@
     last(None, out_k, q_width, key_width)
     last(None, out_v, q_width + key_width, key_width)
     last(None, out_tail, qkv_width, HD)
-    for j in range(NZ - 1):
-        wires.arrived(out_ring.at[j], s_ring.at[j], sib)
+    for sign in (1, -1):
+        pl.when(z > 0 if sign > 0 else z < NZ - 1)(lambda: landed(landing(sign, 0)))
+        pl.when(inside(sign, 1))(toward(sign, 1).wait_send)
     wires.finish()
 
 
@@ -2016,7 +2061,7 @@
         out_shape=tuple(jax.ShapeDtypeStruct(shape, F32) for shape in shapes)
         + (jax.ShapeDtypeStruct((shard, spread), BF16),) * 2
         + (jax.ShapeDtypeStruct((rows, wide), BF16),)
-        + (jax.ShapeDtypeStruct((NZ - 1, rows, wide), BF16),),
+        + (jax.ShapeDtypeStruct((NZ + 1, rows, wide), BF16),),
         in_specs=[hbm] * 5 + [vmem] * len(args),
         out_specs=(vmem,) * 8 + (hbm,),
         scratch_shapes=[
@@ -2043,7 +2088,8 @@
             dma,
             pltpu.VMEM((NZ - 1, rows, wide), BF16),
             dma((2,)),
-            dma((NZ - 1,)),
+            dma((NZ + 1,)),
+            dma((2 * (NZ - 1),)),
         ]
         + plane_scratch(gate_slot, nx, ny)
         + plane_scratch(gate_slot, ny, nx)
@@ -2109,8 +2155,10 @@
             1,
         )
         grad_q, grad_k, grad_v, grad_o, tail_sum, grad_gate_w, grad_up_w, grad_in, ring = outs
-        first_row = lax.axis_index("z") * tok_rows
-        out_sum = jnp.sum(ring.astype(F32), axis=0)
+        z_place = lax.axis_index("z")
+        first_row = z_place * tok_rows
+        out_sum = jnp.where(z_place > 0, ring[0].astype(F32), 0.0)
+        out_sum += jnp.where(z_place < NZ - 1, ring[2].astype(F32), 0.0)
         for half in (made.out_own, made.out_sib):
             out_sum += lax.dynamic_slice_in_dim(half, first_row, tok_rows).astype(F32)
         return (

time: 455 us -> 449 us (0.987); the launches traced: 452 us -> 441 us
  Pallas kernels: 420 us -> 413 us
    pallas_call x1, Pallas kernels: 149 us -> 142 us  [back(): pl.pallas_call(lambda *refs: back_kernel(nx, key_width, b_rows, *refs), n...]
where the time goes in v7:
time: 449 us; the launch traced here: 441 us
  Pallas kernels  413 us (92%)
  other arithmetic  16.6 us (4%)
  local copies, waits for them, and re-layouts  10.8 us (2%)
    pallas_call x1, Pallas kernels, forward(): pl.pallas_call(lambda *refs: forward_kernel(nx, b_rows, names, *refs), na...  271 us
    pallas_call x1, Pallas kernels, back(): pl.pallas_call(lambda *refs: back_kernel(nx, key_width, b_rows, *refs), n...  142 us

profile of v7, /device:TPU:0, one launch (start us, length us, event | category | flops | bytes accessed | tf_op | source)
XLA Modules:
  0.0 441.3 jit_solution(10031606071604478536)
XLA Ops:
  0.7 0.8 constant_dynamic-slice_fusion
  1.5 1.6 fusion.5.refs_6_.refs_12_
  3.7 0.8 pad_maximum_fusion.1.refs_8_.refs_14_
  4.4 0.8 pad_maximum_fusion.refs_7_.refs_13_
  5.5 0.8 concatenate.9.refs_0_
  6.3 270.9 %forward.1 = (bf16[2,4,2,2,48,3712]{5,4,3,2,1,0:T(8,128)(2,1)}, bf16[2,2,4,2,2,48,1120]{6,5,4,3,2,1,0:T(8,128)(2,1)}, bf16[1120,1536]{1,0:T(8,128)(2,1)}, bf16[4...) custom-call(bf16[48,3712]{1,0:T(8,128)(2,1)} %concatenate.9.refs_0_,, ...), custom_call_target="tpu_custom_call" | custom-call | tf_op jit(solution)/shard_map/forward/pallas_call | solution.py:1521
  277.2 1.7 multiply_reduce_fusion.1
  278.9 1.1 slice.24
  281.0 0.8 copy-done.3
  281.8 2.2 fusion.8
  284.0 0.9 copy.32
  284.9 142.2 %back.1 = (f32[48,1536]{1,0:T(8,128)}, f32[48,256]{1,0:T(8,128)}, f32[48,256]{1,0:T(8,128)}, f32[48,1536]{1,0:T(8,128)}, f32[48,128]{1,0:T(8,128)}, /*index=5*/b...) custom-call(bf16[2,4,2,2,48,1120]{5,4,3,2,1,0:T(8,128)(2,1)} %get-tuple-elem, ...), custom_call_target="tpu_custom_call" | custom-call | flops 99999997952 | bytes 100000000 | tf_op jit(solution)/shard_map/back/pallas_call | solution.py:2055
  427.1 2.5 convert_element_type.64
  429.7 1.3 convert_element_type.65
  431.0 0.7 copy-done.1
  431.7 3.4 fusion.3
  435.1 0.7 slice_reduce_fusion.1
  435.8 0.6 slice_bitcast_fusion
  436.3 1.4 convert_element_type.66
  437.7 0.9 copy.39
  438.6 0.7 copy.40
  439.4 0.6 copy.41
  440.0 0.6 copy.42
  440.6 0.7 copy.43
  (49 shorter events, 1.8 us)
Async XLA Ops:
  0.6 4.6 %copy-start.16 = (bf16[64]{0:T(256)(128)(2,1)S(1)}, bf16[64]{0:T(256)(128)(2,1)}, u32[]{:S(2)}) copy-start(bf16[64]{0:T(256)(128)(2,1)} %param.19) | copy-start | bytes 388
  0.7 4.6 %copy-start.17 = (bf16[48]{0:T(256)(128)(2,1)S(1)}, bf16[48]{0:T(256)(128)(2,1)}, u32[]{:S(2)}) copy-start(bf16[48]{0:T(256)(128)(2,1)} %param.15) | copy-start | bytes 292
  0.7 4.7 %copy-start.18 = (bf16[48]{0:T(256)(128)(2,1)S(1)}, bf16[48]{0:T(256)(128)(2,1)}, u32[]{:S(2)}) copy-start(bf16[48]{0:T(256)(128)(2,1)} %param.21) | copy-start | bytes 292
  0.7 4.8 %copy-start.9 = (bf16[48,1536]{1,0:T(8,128)(2,1)S(1)}, bf16[48,1536]{1,0:T(8,128)(2,1)}, u32[]{:S(2)}) copy-start(bf16[48,1536]{1,0:T(8,128)(2,1)} %param.16) | copy-start | bytes 442372
  0.7 4.8 %copy-start.14 = (bf16[48,256]{1,0:T(8,128)(2,1)S(1)}, bf16[48,256]{1,0:T(8,128)(2,1)}, u32[]{:S(2)}) copy-start(bf16[48,256]{1,0:T(8,128)(2,1)} %param.17) | copy-start | bytes 73732
  0.7 4.8 %copy-start.15 = (bf16[48,256]{1,0:T(8,128)(2,1)S(1)}, bf16[48,256]{1,0:T(8,128)(2,1)}, u32[]{:S(2)}) copy-start(bf16[48,256]{1,0:T(8,128)(2,1)} %param.18) | copy-start | bytes 73732
  0.7 4.8 %copy-start.10 = (bf16[48,1536]{1,0:T(8,128)(2,1)S(1)}, bf16[48,1536]{1,0:T(8,128)(2,1)}, u32[]{:S(2)}) copy-start(bf16[48,1536]{1,0:T(8,128)(2,1)} %param.20) | copy-start | bytes 442372
  277.2 3.4 copy-start.2
  278.9 1.7 copy-start
  280.6 1.1 copy-start.3
  427.1 2.6 copy-start.5
  429.7 2.0 copy-start.1
  431.7 3.4 copy-start.11
  431.7 4.6 %copy-start.4 = (bf16[280,1536]{1,0:T(8,128)(2,1)S(1)}, bf16[280,1536]{1,0:T(8,128)(2,1)}, u32[]{:S(2)}) copy-start(bf16[280,1536]{1,0:T(8,128)(2,1)} %get-tuple-element.51) | copy-start | bytes 2580484
  435.0 2.7 copy-start.6
  436.3 2.3 copy-start.8
  437.7 1.6 copy-start.13
  437.7 2.2 copy-start.12
  437.7 2.9 copy-start.7

commit v8 on v7

--- a/solution.py
+++ b/solution.py
@@ -161,14 +161,19 @@
         w.send(self.own, dst, sem, {"z": jnp.maximum(z - 1, 0)}, lambda: z > 0)
         w.send(self.own, dst, sem, {"c": 1 - c})
 
-    def event(self, k):
+    def event(self, k, cond=None):
         w, z, c = self.wires, self.z, self.c
         zq = line_order(z, k)
         slot, sem = self.out.at[zq, c], self.recv.at[zq, c]
-        w.arrived(slot, sem, {"c": 1 - c})
+        if cond is None:
+            w.arrived(slot, sem, {"c": 1 - c})
+        else:
+            pl.when(cond())(lambda: w.arrived(slot, sem, {"c": 1 - c}))
         onward = jnp.where(zq < z, jnp.minimum(z + 1, NZ - 1), jnp.maximum(z - 1, 0))
-        w.send(slot, slot, sem, {"z": onward}, lambda: (z > 0) & (z < NZ - 1))
-        w.send(slot, slot, sem, {"c": 1 - c})
+        inner = lambda: (z > 0) & (z < NZ - 1)
+        both = inner if cond is None else lambda: inner() & cond()
+        w.send(slot, slot, sem, {"z": onward}, both)
+        w.send(slot, slot, sem, {"c": 1 - c}, cond)
 
     def sibling(self, zq):
         w, c = self.wires, self.c
@@ -1198,7 +1203,7 @@
         relay(guo.at[1, 1 - y, :, x], r.rw.at[1, 1 - y, x], planes[:-1])
         for copy in locals_[1:]:
             copy.wait()
-        take(0)
+        pl.when(inner)(lambda: take(0))
         pl.when(inner)(lambda: take(1))
 
         def load_cot(zq, cq):
@@ -1221,7 +1226,7 @@
         ]
         for copy in loads:
             copy.start()
-        line.event(2)
+        line.event(2, lambda: inner)
 
         def output(zq):
             here = pl.ds(pl.multiple_of(zq * rows, rows), rows)
@@ -1257,7 +1262,7 @@
             lax.fori_loop(0, 8, step, 0)
 
         def place_of(k):
-            late = jnp.where(k == 2, line_order(z, 2), line_order(z, 0))
+            late = jnp.where(k == 2, line_order(z, 0), line_order(z, 2))
             return jnp.where(k == 0, z, jnp.where(k == 1, line_order(z, 1), late))
 
         def flat(ref, low, high):
@@ -1266,13 +1271,15 @@
         def pair(k, carry):
             zq = place_of(k)
 
-            @pl.when(k == 0)
+            @pl.when(k == 2)
             def _():
-                for i in range(NZ - 1):
-                    near = line_order(z, i)
-                    load_cot(near, c).start()
-                    line.sibling(near)
-                    load_cot(near, other).start()
+                line.event(2, lambda: jnp.logical_not(inner))
+
+            @pl.when(k > 0)
+            def _():
+                line.sibling(zq)
+                load_cot(zq, other).start()
+                load_cot(zq, c).start()
 
             def one(j, carry):
                 cq = (other + j) % NC
@@ -1289,6 +1296,7 @@
 
                 @pl.when((k == 0) & (j == 1))
                 def _():
+                    pl.when(jnp.logical_not(inner))(lambda: take(0))
                     pl.when(jnp.logical_not(inner))(lambda: take(1))
                     pl.when(inner)(lambda: take(2))
 

time: 449 us -> 443 us (0.987)
  no operation moved by 1% of the time
where the time goes in v8:
time: 443 us; the launch traced here: 438 us
  Pallas kernels  410 us (93%)
  other arithmetic  16.6 us (4%)
  local copies, waits for them, and re-layouts  10.8 us (2%)
    pallas_call x1, Pallas kernels, forward(): pl.pallas_call(lambda *refs: forward_kernel(nx, b_rows, names, *refs), na...  269 us
    pallas_call x1, Pallas kernels, back(): pl.pallas_call(lambda *refs: back_kernel(nx, key_width, b_rows, *refs), n...  141 us

profile of v8, /device:TPU:0, one launch (start us, length us, event | category | flops | bytes accessed | tf_op | source)
XLA Modules:
  0.0 438.3 jit_solution(9126263649517961745)
XLA Ops:
  0.7 0.8 constant_dynamic-slice_fusion
  1.5 1.6 fusion.5.refs_6_.refs_12_
  3.7 0.8 pad_maximum_fusion.1.refs_8_.refs_14_
  4.4 0.8 pad_maximum_fusion.refs_7_.refs_13_
  5.5 0.8 concatenate.9.refs_0_
  6.3 268.8 %forward.1 = (bf16[2,4,2,2,48,3712]{5,4,3,2,1,0:T(8,128)(2,1)}, bf16[2,2,4,2,2,48,1120]{6,5,4,3,2,1,0:T(8,128)(2,1)}, bf16[1120,1536]{1,0:T(8,128)(2,1)}, bf16[4...) custom-call(bf16[48,3712]{1,0:T(8,128)(2,1)} %concatenate.9.refs_0_,, ...), custom_call_target="tpu_custom_call" | custom-call | tf_op jit(solution)/shard_map/forward/pallas_call | solution.py:1529
  275.1 1.7 multiply_reduce_fusion.1
  276.8 1.1 slice.24
  278.9 0.8 copy-done.3
  279.7 2.2 fusion.8
  282.0 0.9 copy.32
  282.8 141.2 %back.1 = (f32[48,1536]{1,0:T(8,128)}, f32[48,256]{1,0:T(8,128)}, f32[48,256]{1,0:T(8,128)}, f32[48,1536]{1,0:T(8,128)}, f32[48,128]{1,0:T(8,128)}, /*index=5*/b...) custom-call(bf16[2,4,2,2,48,1120]{5,4,3,2,1,0:T(8,128)(2,1)} %get-tuple-elem, ...), custom_call_target="tpu_custom_call" | custom-call | flops 99999997952 | bytes 100000000 | tf_op jit(solution)/shard_map/back/pallas_call | solution.py:2063
  424.1 2.5 convert_element_type.64
  426.6 1.3 convert_element_type.65
  427.9 0.7 copy-done.1
  428.7 3.4 fusion.3
  432.0 0.7 slice_reduce_fusion.1
  432.7 0.6 slice_bitcast_fusion
  433.3 1.4 convert_element_type.66
  434.7 0.9 copy.39
  435.6 0.7 copy.40
  436.3 0.6 copy.41
  436.9 0.6 copy.42
  437.5 0.7 copy.43
  (49 shorter events, 1.8 us)
Async XLA Ops:
  0.6 4.6 %copy-start.16 = (bf16[64]{0:T(256)(128)(2,1)S(1)}, bf16[64]{0:T(256)(128)(2,1)}, u32[]{:S(2)}) copy-start(bf16[64]{0:T(256)(128)(2,1)} %param.19) | copy-start | bytes 388
  0.7 4.6 %copy-start.17 = (bf16[48]{0:T(256)(128)(2,1)S(1)}, bf16[48]{0:T(256)(128)(2,1)}, u32[]{:S(2)}) copy-start(bf16[48]{0:T(256)(128)(2,1)} %param.15) | copy-start | bytes 292
  0.7 4.7 %copy-start.18 = (bf16[48]{0:T(256)(128)(2,1)S(1)}, bf16[48]{0:T(256)(128)(2,1)}, u32[]{:S(2)}) copy-start(bf16[48]{0:T(256)(128)(2,1)} %param.21) | copy-start | bytes 292
  0.7 4.8 %copy-start.9 = (bf16[48,1536]{1,0:T(8,128)(2,1)S(1)}, bf16[48,1536]{1,0:T(8,128)(2,1)}, u32[]{:S(2)}) copy-start(bf16[48,1536]{1,0:T(8,128)(2,1)} %param.16) | copy-start | bytes 442372
  0.7 4.8 %copy-start.14 = (bf16[48,256]{1,0:T(8,128)(2,1)S(1)}, bf16[48,256]{1,0:T(8,128)(2,1)}, u32[]{:S(2)}) copy-start(bf16[48,256]{1,0:T(8,128)(2,1)} %param.17) | copy-start | bytes 73732
  0.7 4.8 %copy-start.15 = (bf16[48,256]{1,0:T(8,128)(2,1)S(1)}, bf16[48,256]{1,0:T(8,128)(2,1)}, u32[]{:S(2)}) copy-start(bf16[48,256]{1,0:T(8,128)(2,1)} %param.18) | copy-start | bytes 73732
  0.7 4.8 %copy-start.10 = (bf16[48,1536]{1,0:T(8,128)(2,1)S(1)}, bf16[48,1536]{1,0:T(8,128)(2,1)}, u32[]{:S(2)}) copy-start(bf16[48,1536]{1,0:T(8,128)(2,1)} %param.20) | copy-start | bytes 442372
  275.1 3.4 copy-start.2
  276.8 1.7 copy-start
  278.6 1.1 copy-start.3
  424.1 2.6 copy-start.5
  426.6 2.0 copy-start.1
  428.6 3.4 copy-start.11
  428.6 4.6 %copy-start.4 = (bf16[280,1536]{1,0:T(8,128)(2,1)S(1)}, bf16[280,1536]{1,0:T(8,128)(2,1)}, u32[]{:S(2)}) copy-start(bf16[280,1536]{1,0:T(8,128)(2,1)} %get-tuple-element.51) | copy-start | bytes 2580484
  432.0 2.7 copy-start.6
  433.3 2.3 copy-start.8
  434.7 1.6 copy-start.13
  434.7 2.2 copy-start.12
  434.7 2.9 copy-start.7

commit v9 on v8

--- a/solution.py
+++ b/solution.py
@@ -1067,6 +1067,7 @@
         flat_tail = tail[...].reshape(-1, HD)
         gains = dot_nt(pick, flat_tail)
         gain_one, gain_two = gains[0:1], gains[1:2]
+        r.gains_out[...] = gains[0:8]
         low = lax.broadcasted_iota(jnp.int32, (8, HD), 1) < HD // 2
         pieces = []
         tops = [
@@ -1096,6 +1097,13 @@
                 value = turn(value)
             r.kvs[kv_own, i * HD : (i + 1) * HD] = value.astype(BF16)
         wires.send(r.kvs.at[kv_own], r.kvs.at[kv_own], r.s_kv, ypeer)
+        for k in range(NZ * NC - 1):
+            zp, cp = remote_order(k)
+            wires.arrived(guo.at[:, y, zp, x, cp], r.rt.at[zp, cp], sib)
+        keep.wait()
+        for m in range(2):
+            plane = guo.at[m, y, :, x]
+            both_ways(plane, plane, r.rw.at[m, y, x])
         pre = dot(first_in[...], weights[:, :, :, :, :, :q_width].reshape(wide, q_width))
         pre = pre + bias[:, :q_width]
         heads = q_width // HD
@@ -1103,13 +1111,6 @@
             cols = slice(i * HD, (i + 1) * HD)
             qs[:, cols] = turn(pre[:, cols]).astype(BF16)
         fetch(qkv_width, wide).start()
-        for k in range(NZ * NC - 1):
-            zp, cp = remote_order(k)
-            wires.arrived(guo.at[:, y, zp, x, cp], r.rt.at[zp, cp], sib)
-        keep.wait()
-        for m in range(2):
-            plane = guo.at[m, y, :, x]
-            both_ways(plane, plane, r.rw.at[m, y, x])
         kv_other = r.kvs.at[pl.ds(pl.multiple_of((1 - y) * rows, rows), rows)]
         wires.arrived(kv_other, r.s_kv, ypeer)
         saves = [
@@ -1482,6 +1483,7 @@
         grad_d=((units, wide), BF16),
         dh=((rows, wide), F32),
         down_out=(d.shape, BF16),
+        gains_out=((8, wide), F32),
     )
     plane_x = plane_scratch(half_slot, nx, ny)
     plane_y = plane_scratch(half_slot, ny, nx)
@@ -1531,7 +1533,7 @@
         name="forward",
         out_shape=tuple(jax.ShapeDtypeStruct(*shape) for shape in outs.values()),
         in_specs=[hbm] * 5 + [vmem] * 4,
-        out_specs=(hbm,) * 13 + (vmem,) * 2,
+        out_specs=(hbm,) * 13 + (vmem,) * 3,
         scratch_shapes=list(scratch.values()),
         compiler_params=pltpu.CompilerParams(
             collective_id=collective_id, has_side_effects=True, vmem_limit_bytes=67_043_328
@@ -2127,9 +2129,7 @@
         made = forward(
             ny, nx, b_rows, packed, gate, up, down, grad_out, x, mask, turn_c, turn_s, widths, 0
         )
-        lanes = sum(widths) + widths[1] + x.shape[1]
-        tail = made.ao[..., lanes : lanes + 2].astype(F32).reshape(-1, 2)
-        gain_one, gain_two = tail[:, 0], tail[:, 1]
+        gain_one, gain_two = made.gains_out[0:1], made.gains_out[1:2]
         middle = made.mid_out
         rescale_two = lax.rsqrt(jnp.mean(middle * middle, axis=-1, keepdims=True) + EPS)
         normed_two = middle * rescale_two
@@ -2141,7 +2141,7 @@
             grad_mid,
             grad_mid.astype(BF16),
             x,
-            gain_one[None],
+            gain_one,
             made.o_out,
             made.q_out,
             made.kv_out,

time: 443 us -> 443 us (level)
  no operation moved by 1% of the time
where the time goes in v9:
time: 443 us; the launch traced here: 438 us
  Pallas kernels  410 us (93%)
  other arithmetic  18.2 us (4%)
  local copies, waits for them, and re-layouts  9.04 us (2%)
    pallas_call x1, Pallas kernels, forward(): pl.pallas_call(lambda *refs: forward_kernel(nx, b_rows, names, *refs), na...  269 us
    pallas_call x1, Pallas kernels, back(): pl.pallas_call(lambda *refs: back_kernel(nx, key_width, b_rows, *refs), n...  141 us

profile of v9, /device:TPU:0, one launch (start us, length us, event | category | flops | bytes accessed | tf_op | source)
XLA Modules:
  0.0 437.8 jit_solution(4789368117901945225)
XLA Ops:
  0.7 0.8 constant_dynamic-slice_fusion
  1.5 1.6 fusion.5.refs_6_.refs_12_
  3.1 0.5 multiply_sine_fusion
  3.7 0.8 pad_maximum_fusion.1.refs_8_.refs_14_
  4.4 0.8 pad_maximum_fusion.refs_7_.refs_13_
  5.5 0.8 concatenate.9.refs_0_
  6.3 268.8 %forward.1 = (bf16[2,4,2,2,48,3712]{5,4,3,2,1,0:T(8,128)(2,1)}, bf16[2,2,4,2,2,48,1120]{6,5,4,3,2,1,0:T(8,128)(2,1)}, bf16[1120,1536]{1,0:T(8,128)(2,1)}, bf16[4...) custom-call(bf16[48,3712]{1,0:T(8,128)(2,1)} %concatenate.9.refs_0_,, ...), custom_call_target="tpu_custom_call" | custom-call | tf_op jit(solution)/shard_map/forward/pallas_call | solution.py:1531
  275.1 1.7 multiply_reduce_fusion.1
  276.9 1.5 fusion.9
  278.4 1.9 multiply_reduce_fusion
  280.4 2.2 fusion.8
  282.6 140.9 %back.1 = (f32[48,1536]{1,0:T(8,128)}, f32[48,256]{1,0:T(8,128)}, f32[48,256]{1,0:T(8,128)}, f32[48,1536]{1,0:T(8,128)}, f32[48,128]{1,0:T(8,128)}, /*index=5*/b...) custom-call(bf16[2,4,2,2,48,1120]{5,4,3,2,1,0:T(8,128)(2,1)} %get-tuple-elem, ...), custom_call_target="tpu_custom_call" | custom-call | flops 99999997952 | bytes 100000000 | tf_op jit(solution)/shard_map/back/pallas_call | solution.py:2065
  423.6 2.5 convert_element_type.63
  426.1 1.3 convert_element_type.64
  427.4 0.7 copy-done.1
  428.1 3.4 fusion.3
  431.5 0.7 slice_reduce_fusion
  432.2 0.6 slice_bitcast_fusion
  432.8 1.4 convert_element_type.65
  434.2 0.9 copy.34
  435.1 0.7 copy.35
  435.8 0.6 copy.36
  436.4 0.6 copy.37
  437.0 0.7 copy.38
  (45 shorter events, 0.4 us)
Async XLA Ops:
  0.6 4.6 %copy-start.16 = (bf16[64]{0:T(256)(128)(2,1)S(1)}, bf16[64]{0:T(256)(128)(2,1)}, u32[]{:S(2)}) copy-start(bf16[64]{0:T(256)(128)(2,1)} %param.19) | copy-start | bytes 388
  0.7 4.6 %copy-start.17 = (bf16[48]{0:T(256)(128)(2,1)S(1)}, bf16[48]{0:T(256)(128)(2,1)}, u32[]{:S(2)}) copy-start(bf16[48]{0:T(256)(128)(2,1)} %param.15) | copy-start | bytes 292
  0.7 4.7 %copy-start.18 = (bf16[48]{0:T(256)(128)(2,1)S(1)}, bf16[48]{0:T(256)(128)(2,1)}, u32[]{:S(2)}) copy-start(bf16[48]{0:T(256)(128)(2,1)} %param.21) | copy-start | bytes 292
  0.7 4.8 %copy-start.9 = (bf16[48,1536]{1,0:T(8,128)(2,1)S(1)}, bf16[48,1536]{1,0:T(8,128)(2,1)}, u32[]{:S(2)}) copy-start(bf16[48,1536]{1,0:T(8,128)(2,1)} %param.16) | copy-start | bytes 442372
  0.7 4.8 %copy-start.14 = (bf16[48,256]{1,0:T(8,128)(2,1)S(1)}, bf16[48,256]{1,0:T(8,128)(2,1)}, u32[]{:S(2)}) copy-start(bf16[48,256]{1,0:T(8,128)(2,1)} %param.17) | copy-start | bytes 73732
  0.7 4.8 %copy-start.15 = (bf16[48,256]{1,0:T(8,128)(2,1)S(1)}, bf16[48,256]{1,0:T(8,128)(2,1)}, u32[]{:S(2)}) copy-start(bf16[48,256]{1,0:T(8,128)(2,1)} %param.18) | copy-start | bytes 73732
  0.7 4.8 %copy-start.10 = (bf16[48,1536]{1,0:T(8,128)(2,1)S(1)}, bf16[48,1536]{1,0:T(8,128)(2,1)}, u32[]{:S(2)}) copy-start(bf16[48,1536]{1,0:T(8,128)(2,1)} %param.20) | copy-start | bytes 442372
  275.1 3.2 copy-start
  278.3 2.0 copy-start.2
  278.3 2.1 copy-start.3
  423.6 2.6 copy-start.5
  426.1 2.0 copy-start.1
  428.1 3.4 copy-start.11
  428.1 4.6 %copy-start.4 = (bf16[280,1536]{1,0:T(8,128)(2,1)S(1)}, bf16[280,1536]{1,0:T(8,128)(2,1)}, u32[]{:S(2)}) copy-start(bf16[280,1536]{1,0:T(8,128)(2,1)} %get-tuple-element.53) | copy-start | bytes 2580484
  431.5 2.7 copy-start.6
  432.8 2.3 copy-start.8
  434.2 1.6 copy-start.13
  434.2 2.2 copy-start.12
  434.2 2.9 copy-start.7
